TPU v7x, 32 devices: a whole 2x2x4 slice. The times are simulated.
32 devices in a mesh: rep: 4 (over y, x), shard: 8 (over z, core).
Axes of the slice: x: 2, y: 2, z: 4, core: 2. Of those that a mesh axis runs over, the one named last changes fastest.
Arguments:
- tokens: bfloat16 [12288, 768], P(('rep', 'shard')), may hold values from -6 to 6
- routes: int32 [12288], P(('rep', 'shard')), may hold values from 0 to 7, as said below
- slot_ids: int32 [12288], P(('rep', 'shard')), may hold values from 0 to 95, as said below
- w_query: bfloat16 [768, 768], P('shard'), may hold values from -0.21875 to 0.21875
- w_key: bfloat16 [768, 768], P('shard'), may hold values from -0.21875 to 0.21875
- w_value: bfloat16 [768, 768], P('shard'), may hold values from -0.21875 to 0.21875
- w_output: bfloat16 [768, 768], P('shard'), may hold values from -3 to 3
- w_router: bfloat16 [768, 8], P('shard'), may hold values from -0.15625 to 0.15625
- norm_attn: bfloat16 [768], P('shard'), may hold values from 0.5 to 1.5
- norm_moe: bfloat16 [768], P('shard'), may hold values from 0.5 to 1.5
- rel_table: bfloat16 [32, 12], P('shard'), may hold values from -4 to 4
- w_in: bfloat16 [8, 768, 3072], P('shard'), may hold values from -0.21875 to 0.21875
- w_out: bfloat16 [8, 3072, 768], P('shard'), may hold values from -2.390625 to 2.390625
- cotangent: bfloat16 [12288, 768], P(('rep', 'shard')), may hold values from -6 to 6
Outputs:
- mixed: bfloat16 [12288, 768], P(('rep', 'shard'))
- grad_tokens: float32 [12288, 768], P(('rep', 'shard'))
- grad_w_query: float32 [768, 768], P('shard')
- grad_w_key: float32 [768, 768], P('shard')
- grad_w_value: float32 [768, 768], P('shard')
- grad_w_output: float32 [768, 768], P('shard')
- grad_w_router: float32 [768, 8], P('shard')
- grad_norm_attn: float32 [768], P('shard')
- grad_norm_moe: float32 [768], P('shard')
- grad_rel_table: float32 [32, 12], P('shard')
- grad_w_in: float32 [8, 768, 3072], P('shard', 'rep')
- grad_w_out: float32 [8, 3072, 768], P('shard', 'rep')
Inputs may be any that keep to these rules, and one draw needn't show every extreme that they name: `routes`: in each device's block of 384 tokens no expert is named more than 96 times; in every group one expert, drawn from the seed, is named exactly 96 times in each of the group's blocks. `slot_ids`: within a block, tokens with the same route have different slots.
All inputs are finite; a program needn't handle non-finite values.
Results may differ from a plain program's by a relative error of at most 0.024.
Values may be sent and summed in bfloat16 or wider, within the bound.
A program may use at most 256 MiB of HBM per device.

v0:
```python
import jax
import jax.numpy as jnp
from jax import lax
from jax.sharding import PartitionSpec as P

PR_DEV = 128


bucket_edges = (12, 16, 23, 32, 46, 64, 91)
norm_epsilon = 1e-06
masked_score = -1e30


def passed_along(value, axis, steps):
    count = lax.axis_size(axis)
    first, last = (max(0, -steps), min(count, count - steps))
    return lax.ppermute(value, axis, [(source, source + steps) for source in range(first, last)])


def bucket_of(distance, bucket_count):
    magnitude = jnp.abs(distance)
    far_steps = jnp.zeros_like(magnitude)
    for edge_value in bucket_edges:
        far_steps = far_steps + (magnitude >= edge_value).astype(jnp.int32)
    exact_span = bucket_count // 4
    within = jnp.where(magnitude < exact_span, magnitude, exact_span + far_steps)
    return jnp.where(distance > 0, bucket_count // 2, 0) + within


def bucket_bias(buckets, table_heads):
    bias = jnp.zeros((table_heads.shape[0],) + buckets.shape, jnp.float32)
    for bucket_id in range(table_heads.shape[1]):
        bias = bias + jnp.where(
            (buckets == bucket_id)[None], table_heads[:, bucket_id][:, None, None], 0.0
        )
    return bias


def bucket_sums(grad_scores, buckets, bucket_count):
    totals = []
    for bucket_id in range(bucket_count):
        totals.append(
            jnp.sum(jnp.where((buckets == bucket_id)[None], grad_scores, 0.0), axis=(1, 2))
        )
    return jnp.stack(totals)


def norm_apply(values, gain_row):
    return (
        values
        * lax.rsqrt(jnp.mean(values * values, axis=-1, keepdims=True) + norm_epsilon)
        * gain_row
    )


def gelu_tanh(values):
    return jax.nn.gelu(values, approximate=True)


def token_layout(shard_id, row_ids, prompt_rows, cont_rows, prompt_len):
    in_prompt = row_ids < prompt_rows
    positions = jnp.where(
        in_prompt,
        shard_id * prompt_rows + row_ids,
        prompt_len + shard_id % 2 * cont_rows + row_ids - prompt_rows,
    )
    cont_ids = jnp.where(in_prompt, -1, shard_id // 2)
    return (positions, cont_ids)


def block_scores(query_heads, key_heads, key_pos, key_cont, query_pos, query_cont, table_heads):
    raw_scores = jnp.einsum(
        "qhd,khd->hqk", query_heads, key_heads, preferred_element_type=jnp.float32
    )
    buckets = bucket_of(key_pos[None, :] - query_pos[:, None], table_heads.shape[1])
    scores = raw_scores * query_heads.shape[2] ** (-0.5) + bucket_bias(buckets, table_heads)
    visible = (key_cont[None, :] == -2) | (key_cont[None, :] == query_cont[:, None]) & (
        key_pos[None, :] <= query_pos[:, None]
    )
    return (jnp.where(visible[None], scores, masked_score), visible, buckets)


def sweep_keys(
    step_fn,
    state,
    prompt_keys,
    prompt_values,
    local_keys,
    local_values,
    local_pos,
    local_cont,
    span_rows,
    head_count,
):
    head_size = prompt_keys.shape[1] // head_count
    block_count = prompt_keys.shape[0] // span_rows
    stacked = (
        prompt_keys.reshape(block_count, span_rows, head_count, head_size),
        prompt_values.reshape(block_count, span_rows, head_count, head_size),
        jnp.arange(block_count, dtype=jnp.int32) * span_rows,
    )

    def scan_step(current, item_set):
        key_heads, value_heads, first_row = item_set
        key_pos = first_row + jnp.arange(span_rows, dtype=jnp.int32)
        key_cont = jnp.full((span_rows,), -2, jnp.int32)
        return step_fn(current, key_heads, value_heads, key_pos, key_cont)

    state, prompt_out = lax.scan(scan_step, state, stacked)
    local_heads = local_keys.reshape(-1, head_count, head_size)
    local_vheads = local_values.reshape(-1, head_count, head_size)
    state, local_out = step_fn(state, local_heads, local_vheads, local_pos, local_cont)
    return (state, prompt_out, local_out)


def local(
    tokens,
    routes,
    slot_ids,
    w_query,
    w_key,
    w_value,
    w_output,
    w_router,
    norm_attn,
    norm_moe,
    rel_table,
    w_in,
    w_out,
    cotangent,
):
    shard_count = lax.axis_size("shard")
    shard_id = lax.axis_index("shard")
    token_rows = tokens.shape[0]
    model_width = tokens.shape[1]
    prompt_rows = PR_DEV
    cont_rows = token_rows - prompt_rows
    prompt_len = prompt_rows * shard_count
    gathered = (
        lax.all_gather(w_query, "shard", axis=0, tiled=True),
        lax.all_gather(w_key, "shard", axis=0, tiled=True),
        lax.all_gather(w_value, "shard", axis=0, tiled=True),
        lax.all_gather(w_output, "shard", axis=0, tiled=True),
        lax.all_gather(w_router, "shard", axis=0, tiled=True),
        lax.all_gather(norm_attn, "shard", axis=0, tiled=True),
        lax.all_gather(norm_moe, "shard", axis=0, tiled=True),
        lax.all_gather(rel_table, "shard", axis=0, tiled=True),
    )
    query_full, key_full, value_full, output_full, router_full, gain_attn, gain_moe, table_full = (
        gathered
    )
    expert_count = router_full.shape[1]
    capacity = 2 * token_rows // expert_count
    bucket_count = table_full.shape[0]
    head_count = table_full.shape[1]
    head_size = model_width // head_count
    table_heads = table_full.astype(jnp.float32).T
    factor = 1
    while shard_count % (2 * factor) == 0 and 2 * factor * prompt_rows <= 512:
        factor = factor * 2
    span_rows = factor * prompt_rows
    resid_in = tokens.astype(jnp.float32)
    normed_in, norm_pull_in = jax.vjp(norm_apply, resid_in, gain_attn.astype(jnp.float32))
    normed_low = normed_in.astype(jnp.bfloat16)
    queries = jnp.dot(normed_low, query_full, preferred_element_type=jnp.float32).astype(
        jnp.bfloat16
    )
    keys_tok = jnp.dot(normed_low, key_full, preferred_element_type=jnp.float32).astype(
        jnp.bfloat16
    )
    values_tok = jnp.dot(normed_low, value_full, preferred_element_type=jnp.float32).astype(
        jnp.bfloat16
    )
    query_heads = queries.reshape(token_rows, head_count, head_size)
    row_ids = jnp.arange(token_rows, dtype=jnp.int32)
    query_pos, query_cont = token_layout(shard_id, row_ids, prompt_rows, cont_rows, prompt_len)
    cont_index = jnp.arange(cont_rows, dtype=jnp.int32)
    before_id = shard_id - 1
    local_pos = jnp.concatenate(
        [
            prompt_len + before_id % 2 * cont_rows + cont_index,
            prompt_len + shard_id % 2 * cont_rows + cont_index,
        ]
    )
    partner_cont = jnp.where(shard_id > 0, before_id // 2, -3)
    local_cont = jnp.concatenate(
        [
            jnp.full((cont_rows,), partner_cont, jnp.int32),
            jnp.full((cont_rows,), shard_id // 2, jnp.int32),
        ]
    )
    prompt_keys_all, prompt_values_all = (
        lax.all_gather(keys_tok[:prompt_rows], "shard", axis=0, tiled=True),
        lax.all_gather(values_tok[:prompt_rows], "shard", axis=0, tiled=True),
    )
    partner_keys, partner_values = passed_along(
        (keys_tok[prompt_rows:], values_tok[prompt_rows:]), "shard", 1
    )
    local_keys = jnp.concatenate([partner_keys, keys_tok[prompt_rows:]])
    local_values = jnp.concatenate([partner_values, values_tok[prompt_rows:]])

    def stats_step(current, key_heads, value_heads, key_pos, key_cont):
        row_max, row_total = current
        scores, visible, buckets = block_scores(
            query_heads, key_heads, key_pos, key_cont, query_pos, query_cont, table_heads
        )
        new_max = jnp.maximum(row_max, jnp.max(scores, axis=-1))
        shifted = jnp.where(visible[None], jnp.exp(scores - new_max[..., None]), 0.0)
        return ((new_max, row_total * jnp.exp(row_max - new_max) + jnp.sum(shifted, axis=-1)), None)

    start_stats = (
        jnp.full((head_count, token_rows), masked_score, jnp.float32),
        jnp.zeros((head_count, token_rows), jnp.float32),
    )
    stats_out, unused_one, unused_two = sweep_keys(
        stats_step,
        start_stats,
        prompt_keys_all,
        prompt_values_all,
        local_keys,
        local_values,
        local_pos,
        local_cont,
        span_rows,
        head_count,
    )
    log_total = stats_out[0] + jnp.log(stats_out[1])

    def output_step(summed, key_heads, value_heads, key_pos, key_cont):
        scores, visible, buckets = block_scores(
            query_heads, key_heads, key_pos, key_cont, query_pos, query_cont, table_heads
        )
        weights = jnp.where(visible[None], jnp.exp(scores - log_total[..., None]), 0.0).astype(
            jnp.bfloat16
        )
        return (
            summed
            + jnp.einsum("hqk,khd->qhd", weights, value_heads, preferred_element_type=jnp.float32),
            None,
        )

    start_output = jnp.zeros((token_rows, head_count, head_size), jnp.float32)
    attended, unused_three, unused_four = sweep_keys(
        output_step,
        start_output,
        prompt_keys_all,
        prompt_values_all,
        local_keys,
        local_values,
        local_pos,
        local_cont,
        span_rows,
        head_count,
    )
    attn_low = attended.reshape(token_rows, model_width).astype(jnp.bfloat16)
    resid_mid = resid_in + jnp.dot(attn_low, output_full, preferred_element_type=jnp.float32)
    normed_mid, norm_pull_mid = jax.vjp(norm_apply, resid_mid, gain_moe.astype(jnp.float32))
    mid_low = normed_mid.astype(jnp.bfloat16)
    router_probs = jax.nn.softmax(
        jnp.dot(mid_low, router_full, preferred_element_type=jnp.float32), axis=-1
    )
    route_match = routes[:, None] == jnp.arange(expert_count, dtype=jnp.int32)[None, :]
    gate_value = jnp.sum(jnp.where(route_match, router_probs, 0.0), axis=-1)
    dispatch = routes * capacity + slot_ids
    buffer = (
        jnp.zeros((expert_count * capacity, model_width), jnp.bfloat16).at[dispatch].set(mid_low)
    )
    buffer = buffer.reshape(expert_count, capacity, model_width)
    arrived = lax.all_to_all(buffer, "shard", split_axis=0, concat_axis=0, tiled=True)
    source_count = arrived.shape[0]
    item_count = arrived.shape[1]
    rows_in = arrived.reshape(source_count * item_count, model_width)
    pre_act = jnp.dot(rows_in, w_in[0], preferred_element_type=jnp.float32)
    hidden = gelu_tanh(pre_act).astype(jnp.bfloat16)
    result = jnp.dot(hidden, w_out[0], preferred_element_type=jnp.float32).astype(jnp.bfloat16)
    returned = lax.all_to_all(
        result.reshape(source_count, item_count, model_width),
        "shard",
        split_axis=0,
        concat_axis=0,
        tiled=True,
    )
    returned, arrived, pre_kept = (returned, arrived, pre_act.reshape(source_count, item_count, -1))
    expert_tok = returned.reshape(-1, model_width)[dispatch]
    expert_single = expert_tok.astype(jnp.float32)
    mixed = (resid_mid + gate_value[:, None] * expert_single).astype(jnp.bfloat16)
    grad_final = cotangent.astype(jnp.float32)
    grad_gate = jnp.sum(grad_final * expert_single, axis=-1)
    grad_expert_tok = (gate_value[:, None] * grad_final).astype(jnp.bfloat16)
    grad_buffer = (
        jnp.zeros((expert_count * capacity, model_width), jnp.bfloat16)
        .at[dispatch]
        .set(grad_expert_tok)
    )
    grad_arrived = lax.all_to_all(
        grad_buffer.reshape(expert_count, capacity, model_width),
        "shard",
        split_axis=0,
        concat_axis=0,
        tiled=True,
    )
    rows_in = arrived.reshape(-1, model_width)
    grad_rows = grad_arrived.reshape(-1, model_width)
    pre_act = pre_kept.reshape(rows_in.shape[0], -1)
    hidden_single, gelu_pull = jax.vjp(gelu_tanh, pre_act)
    hidden = hidden_single.astype(jnp.bfloat16)
    grad_hidden = jnp.einsum("sd,fd->sf", grad_rows, w_out[0], preferred_element_type=jnp.float32)
    grad_pre = gelu_pull(grad_hidden)[0].astype(jnp.bfloat16)
    grad_rows_in = jnp.einsum(
        "sf,df->sd", grad_pre, w_in[0], preferred_element_type=jnp.float32
    ).astype(jnp.bfloat16)
    grad_back = lax.all_to_all(
        grad_rows_in.reshape(shard_count, capacity, model_width),
        "shard",
        split_axis=0,
        concat_axis=0,
        tiled=True,
    )
    grad_slot = grad_back.reshape(-1, model_width)[dispatch].astype(jnp.float32)
    grad_logits = (gate_value * grad_gate)[:, None] * (
        route_match.astype(jnp.float32) - router_probs
    )
    mid_single = mid_low.astype(jnp.float32)
    router_single = router_full.astype(jnp.float32)
    grad_router = jnp.dot(mid_single.T, grad_logits, precision=lax.Precision.HIGHEST)
    grad_mid = grad_slot + jnp.dot(grad_logits, router_single.T, precision=lax.Precision.HIGHEST)
    grad_resid_part, grad_gain_moe = norm_pull_mid(grad_mid)
    grad_resid = grad_final + grad_resid_part
    grad_attn = grad_resid.astype(jnp.bfloat16)
    grad_wo = jnp.einsum("td,te->de", attn_low, grad_attn, preferred_element_type=jnp.float32)
    grad_heads = jnp.einsum(
        "te,de->td", grad_attn, output_full, preferred_element_type=jnp.float32
    ).astype(jnp.bfloat16)
    grad_heads = grad_heads.reshape(token_rows, head_count, head_size)
    prompt_keys_back, prompt_values_back = (
        lax.all_gather(keys_tok[:prompt_rows], "shard", axis=0, tiled=True),
        lax.all_gather(values_tok[:prompt_rows], "shard", axis=0, tiled=True),
    )
    row_delta = jnp.einsum("thd,thd->ht", grad_heads.astype(jnp.float32), attended)

    def grad_step(current, key_heads, value_heads, key_pos, key_cont):
        grad_query, grad_table = current
        scores, visible, buckets = block_scores(
            query_heads, key_heads, key_pos, key_cont, query_pos, query_cont, table_heads
        )
        weights = jnp.where(visible[None], jnp.exp(scores - log_total[..., None]), 0.0)
        grad_weights = jnp.einsum(
            "qhd,khd->hqk", grad_heads, value_heads, preferred_element_type=jnp.float32
        )
        grad_scores = weights * (grad_weights - row_delta[..., None])
        grad_table = grad_table + bucket_sums(grad_scores, buckets, bucket_count)
        grad_raw = (grad_scores * query_heads.shape[2] ** (-0.5)).astype(jnp.bfloat16)
        grad_query = grad_query + jnp.einsum(
            "hqk,khd->qhd", grad_raw, key_heads, preferred_element_type=jnp.float32
        )
        grad_key_rows = jnp.einsum(
            "hqk,qhd->khd", grad_raw, query_heads, preferred_element_type=jnp.float32
        )
        grad_value_rows = jnp.einsum(
            "hqk,qhd->khd",
            weights.astype(jnp.bfloat16),
            grad_heads,
            preferred_element_type=jnp.float32,
        )
        return ((grad_query, grad_table), (grad_key_rows, grad_value_rows))

    start_grads = (
        jnp.zeros((token_rows, head_count, head_size), jnp.float32),
        jnp.zeros((bucket_count, head_count), jnp.float32),
    )
    grad_state, prompt_out, local_out = sweep_keys(
        grad_step,
        start_grads,
        prompt_keys_back,
        prompt_values_back,
        local_keys,
        local_values,
        local_pos,
        local_cont,
        span_rows,
        head_count,
    )
    grad_query_rows, grad_table = grad_state
    prompt_grad_keys = prompt_out[0].reshape(prompt_len, model_width)
    prompt_grad_values = prompt_out[1].reshape(prompt_len, model_width)
    own_grad_keys, own_grad_values = (
        lax.psum_scatter(
            prompt_grad_keys.astype(jnp.bfloat16), "shard", scatter_dimension=0, tiled=True
        ).astype(jnp.float32),
        lax.psum_scatter(
            prompt_grad_values.astype(jnp.bfloat16), "shard", scatter_dimension=0, tiled=True
        ).astype(jnp.float32),
    )
    local_grad_keys = local_out[0].reshape(2 * cont_rows, model_width)
    local_grad_values = local_out[1].reshape(2 * cont_rows, model_width)
    next_keys, next_values = (
        passed_along(local_grad_keys[:cont_rows].astype(jnp.bfloat16), "shard", -1).astype(
            jnp.float32
        ),
        passed_along(local_grad_values[:cont_rows].astype(jnp.bfloat16), "shard", -1).astype(
            jnp.float32
        ),
    )
    grad_keys_tok = jnp.concatenate(
        [own_grad_keys, local_grad_keys[cont_rows:] + next_keys]
    ).astype(jnp.bfloat16)
    grad_values_tok = jnp.concatenate(
        [own_grad_values, local_grad_values[cont_rows:] + next_values]
    ).astype(jnp.bfloat16)
    grad_queries_tok = grad_query_rows.reshape(token_rows, model_width).astype(jnp.bfloat16)
    grad_wq = jnp.einsum(
        "td,te->de", normed_low, grad_queries_tok, preferred_element_type=jnp.float32
    )
    grad_wk = jnp.einsum("td,te->de", normed_low, grad_keys_tok, preferred_element_type=jnp.float32)
    grad_wv = jnp.einsum(
        "td,te->de", normed_low, grad_values_tok, preferred_element_type=jnp.float32
    )
    grad_normed = jnp.einsum(
        "te,de->td", grad_queries_tok, query_full, preferred_element_type=jnp.float32
    )
    grad_normed = grad_normed + jnp.einsum(
        "te,de->td", grad_keys_tok, key_full, preferred_element_type=jnp.float32
    )
    grad_normed = grad_normed + jnp.einsum(
        "te,de->td", grad_values_tok, value_full, preferred_element_type=jnp.float32
    )
    grad_resid_in, grad_gain_attn = norm_pull_in(grad_normed)
    grad_tokens = grad_resid + grad_resid_in
    dense_local = (
        grad_wq,
        grad_wk,
        grad_wv,
        grad_wo,
        grad_router,
        grad_gain_attn,
        grad_gain_moe,
        grad_table,
    )
    dense_shards = (
        lax.psum_scatter(
            dense_local[0].astype(jnp.bfloat16), "shard", scatter_dimension=0, tiled=True
        ).astype(jnp.float32),
        lax.psum_scatter(
            dense_local[1].astype(jnp.bfloat16), "shard", scatter_dimension=0, tiled=True
        ).astype(jnp.float32),
        lax.psum_scatter(
            dense_local[2].astype(jnp.bfloat16), "shard", scatter_dimension=0, tiled=True
        ).astype(jnp.float32),
        lax.psum_scatter(
            dense_local[3].astype(jnp.bfloat16), "shard", scatter_dimension=0, tiled=True
        ).astype(jnp.float32),
        lax.psum_scatter(
            dense_local[4].astype(jnp.bfloat16), "shard", scatter_dimension=0, tiled=True
        ).astype(jnp.float32),
        lax.psum_scatter(
            dense_local[5].astype(jnp.bfloat16), "shard", scatter_dimension=0, tiled=True
        ).astype(jnp.float32),
        lax.psum_scatter(
            dense_local[6].astype(jnp.bfloat16), "shard", scatter_dimension=0, tiled=True
        ).astype(jnp.float32),
        lax.psum_scatter(
            dense_local[7].astype(jnp.bfloat16), "shard", scatter_dimension=0, tiled=True
        ).astype(jnp.float32),
    )
    dense_sums = (
        lax.psum(dense_shards[0].astype(jnp.bfloat16), "rep").astype(jnp.float32),
        lax.psum(dense_shards[1].astype(jnp.bfloat16), "rep").astype(jnp.float32),
        lax.psum(dense_shards[2].astype(jnp.bfloat16), "rep").astype(jnp.float32),
        lax.psum(dense_shards[3].astype(jnp.bfloat16), "rep").astype(jnp.float32),
        lax.psum(dense_shards[4].astype(jnp.bfloat16), "rep").astype(jnp.float32),
        lax.psum(dense_shards[5].astype(jnp.bfloat16), "rep").astype(jnp.float32),
        lax.psum(dense_shards[6].astype(jnp.bfloat16), "rep").astype(jnp.float32),
        lax.psum(dense_shards[7].astype(jnp.bfloat16), "rep").astype(jnp.float32),
    )
    grad_w_out = jnp.einsum("sf,sd->fd", hidden, grad_rows, preferred_element_type=jnp.float32)
    grad_w_in = jnp.einsum("sd,sf->df", rows_in, grad_pre, preferred_element_type=jnp.float32)
    expert_in_grad, expert_out_grad = (
        lax.psum_scatter(
            grad_w_in[None].astype(jnp.bfloat16), "rep", scatter_dimension=1, tiled=True
        ).astype(jnp.float32),
        lax.psum_scatter(
            grad_w_out[None].astype(jnp.bfloat16), "rep", scatter_dimension=1, tiled=True
        ).astype(jnp.float32),
    )
    return (
        mixed,
        grad_tokens,
        dense_sums[0],
        dense_sums[1],
        dense_sums[2],
        dense_sums[3],
        dense_sums[4],
        dense_sums[5],
        dense_sums[6],
        dense_sums[7],
        expert_in_grad,
        expert_out_grad,
    )


def solution(mesh):
    return jax.shard_map(
        local,
        mesh=mesh,
        in_specs=(
            P(("rep", "shard"), None),
            P(("rep", "shard")),
            P(("rep", "shard")),
            P("shard", None),
            P("shard", None),
            P("shard", None),
            P("shard", None),
            P("shard", None),
            P("shard"),
            P("shard"),
            P("shard", None),
            P("shard", None, None),
            P("shard", None, None),
            P(("rep", "shard"), None),
        ),
        out_specs=(
            P(("rep", "shard"), None),
            P(("rep", "shard"), None),
            P("shard", None),
            P("shard", None),
            P("shard", None),
            P("shard", None),
            P("shard", None),
            P("shard"),
            P("shard"),
            P("shard", None),
            P("shard", "rep", None),
            P("shard", "rep", None),
        ),
        check_vma=False,
    )
```

profile of v0, /device:TPU:0, one launch (start us, length us, event | category | flops | bytes accessed | tf_op | source)
XLA Modules:
  0.0 1171.0 jit_solution(7529008617130550368)
XLA Ops:
  38.1 21.0 %all-gather.9.cloned.1.call-done = bf16[768,768]{1,0:T(8,128)(2,1)} async-done(((bf16[96,768]{1,0:T(8,128)(2,1)}), bf16[768,768]{1,0:T(8,128)(2,1)}) %all-gather.9.cloned.1.call-update) | async-done | bytes 1179664 | tf_op jit(solution)/shard_map/all_gather | solution.py:142
  96.7 41.2 %fusion.170 = (f32[12,384]{1,0:T(8,128)}, f32[12,384,512]{2,1,0:T(8,128)}) fusion(f32[12]{0:T(128)S(1)} %get-tuple-element.756, pred[384,512]{1,0:T(8,128)(4,1)} %get-tuple-element.818, f32[12]{0:T(128)S(1)} %get-tuple-element.757, pred[384,512]{1,0:T(8,128)(4,1)} %get-tuple-element.817, f32[12]{0:T(128)S(1)} %get-tuple-element.758, ...), kind=kOutput, calls=%fused_computation.565 | convolution fusion | flops 460058112 | bytes 17321472 | tf_op jit(solution)/shard_map/qhd,khd->hqk/dot_general | solution.py:72
  146.7 110.8 %while.41 = (s32[]{:T(128)}, f32[12,384]{1,0:T(8,128)S(1)}, f32[12,384]{1,0:T(8,128)}, bf16[2,512,12,64]{1,3,2,0:T(8,128)(2,1)}, bf16[384,12,64]{0,2,1:T(8,128)(...) while((s32[]{:T(128)}, f32[12,384]{1,0:T(8,128)S(1)}, ...), condition=%wide.region_4.5_spmd.clone, body=%wide.region_1.4_spmd.clone.sunk | while | flops 474243968 | bytes 33246976 | solution.py:109
  156.3 36.4 %fusion.228 = (f32[12,384]{1,0:T(8,128)S(1)}, f32[12,384,512]{1,2,0:T(8,128)S(1)}) fusion(f32[12]{0:T(128)} %get-tuple-element.1246, pred[384,512]{0,1:T(8,128)(4,1)} %get-tuple-element.1247, f32[12]{0:T(128)} %get-tuple-element.1248, pred[384,512]{0,1:T(8,128)(4,1)} %get-tuple-element.1249, f32[12]{0:T(128)} %get-tuple-element.1250, ...), kind=kOutput, calls=%fused_computation.563.clone.1 | convolution fusion | flops 457698816 | bytes 17139252 | tf_op jit(solution)/shard_map/while/body/eval_jaxpr/qhd,khd->hqk/dot_general | solution.py:72
  204.5 36.3 %fusion.228 = (f32[12,384]{1,0:T(8,128)S(1)}, f32[12,384,512]{1,2,0:T(8,128)S(1)}) fusion(f32[12]{0:T(128)} %get-tuple-element.1246, pred[384,512]{0,1:T(8,128)(4,1)} %get-tuple-element.1247, f32[12]{0:T(128)} %get-tuple-element.1248, pred[384,512]{0,1:T(8,128)(4,1)} %get-tuple-element.1249, f32[12]{0:T(128)} %get-tuple-element.1250, ...), kind=kOutput, calls=%fused_computation.563.clone.1 | convolution fusion | flops 457698816 | bytes 17139252 | tf_op jit(solution)/shard_map/while/body/eval_jaxpr/qhd,khd->hqk/dot_general | solution.py:72
  264.6 96.1 %while.42 = (s32[]{:T(128)}, f32[384,12,64]{0,2,1:T(8,128)}, bf16[2,512,12,64]{1,3,2,0:T(8,128)(2,1)}, bf16[2,512,12,64]{1,3,2,0:T(8,128)(2,1)S(1)}, bf16[384,12...) while((s32[]{:T(128)}, f32[384,12,64]{0,2,1:T(8,128)}, ...), condition=%wide.region_8.9_spmd.clone, body=%wide.region_7.8_spmd.clone.sunk | while | flops 774441344 | bytes 17157788 | solution.py:109
  274.0 38.4 %fusion.234 = f32[384,12,64]{0,2,1:T(8,128)} fusion(f32[12,384]{1,0:T(8,128)} %get-tuple-element.1562, f32[12]{0:T(128)} %get-tuple-element.1322, f32[12]{0:T(128)} %get-tuple-element.1323, f32[12]{0:T(128)} %get-tuple-element.1324, f32[12]{0:T(128)} %get-tuple-element.1325, f32[12]{0:T(128)} %get-tuple-element.1326, f32[12]{0:T(128)} %get-tuple-element.1327, ...), kind=kOutput, calls=%fused_computation.101.clone.1 | convolution fusion | flops 762642432 | bytes 10855936 | tf_op jit(solution)/shard_map/while/body/eval_jaxpr/hqk,khd->qhd/dot_general | solution.py:238
  321.7 38.8 %fusion.234 = f32[384,12,64]{0,2,1:T(8,128)} fusion(f32[12,384]{1,0:T(8,128)} %get-tuple-element.1562, f32[12]{0:T(128)} %get-tuple-element.1322, f32[12]{0:T(128)} %get-tuple-element.1323, f32[12]{0:T(128)} %get-tuple-element.1324, f32[12]{0:T(128)} %get-tuple-element.1325, f32[12]{0:T(128)} %get-tuple-element.1326, f32[12]{0:T(128)} %get-tuple-element.1327, ...), kind=kOutput, calls=%fused_computation.101.clone.1 | convolution fusion | flops 762642432 | bytes 10855936 | tf_op jit(solution)/shard_map/while/body/eval_jaxpr/hqk,khd->qhd/dot_general | solution.py:238
  377.8 35.4 %all-gather.1 = bf16[8,96,8]{1,2,0:T(8,128)(2,1)S(1)} all-gather(bf16[1,96,8]{1,2,0:T(8,128)(2,1)} %bitcast.702), channel_id=1, replica_groups=mesh['rep'=4,'shard'=8] {'shard'}, dimensions={0}, use_global_device_ids=true | all-gather | bytes 13824 | tf_op jit(solution)/shard_map/all_gather | solution.py:144
  500.6 22.3 %all-to-all-done.3 = bf16[8,96,768]{2,1,0:T(8,128)(2,1)S(1)} async-done(((bf16[8,96,768]{2,1,0:T(8,128)(2,1)}), bf16[8,96,768]{2,1,0:T(8,128)(2,1)S(1)}, u32[]{:S(2)}, u32[]{:S(2)}) %all-to-all-start.3) | async-done | bytes 1179680 | tf_op jit(solution)/shard_map/all_to_all | solution.py:312
  537.2 213.5 %while.43 = (s32[]{:T(128)}, f32[384,12,64]{0,2,1:T(8,128)}, f32[32,12]{1,0:T(8,128)}, bf16[2,512,12,64]{1,3,2,0:T(8,128)(2,1)}, bf16[2,512,12,64]{1,3,2,0:T(8,1...) while((s32[]{:T(128)}, f32[384,12,64]{0,2,1:T(8,128)}, ...), condition=%wide.region_50.51_spmd.clone, body=%wide.region_17.50_spmd.clone.sunk | while | flops 1845562240 | bytes 228942320 | solution.py:109
  546.7 34.4 %fusion.242 = f32[12,384,512]{1,2,0:T(8,128)S(1)} fusion(f32[12,384]{1,0:T(8,128)} %get-tuple-element.1610, f32[12]{0:T(128)S(1)} %get-tuple-element.1415, f32[12]{0:T(128)S(1)} %get-tuple-element.1416, f32[12]{0:T(128)S(1)} %get-tuple-element.1417, f32[12]{0:T(128)S(1)} %get-tuple-element.1418, f32[12]{0:T(128)S(1)} %get-tuple-element.1419, ...), kind=kOutput, calls=%fused_computation.189.clone.1 | convolution fusion | flops 457703424 | bytes 17140756 | tf_op jit(solution)/shard_map/while/body/eval_jaxpr/qhd,khd->hqk/dot_general | solution.py:72
  608.4 22.0 %select_reduce_fusion.69 = (f32[12]{0:T(128)S(1)}, f32[12]{0:T(128)S(1)}, f32[12]{0:T(128)S(1)}, f32[12]{0:T(128)S(1)}, f32[12]{0:T(128)S(1)}, /*index=5*/f32[12...) fusion(f32[12,384,512]{1,2,0:T(8,128)S(1)} %get-tuple-element.1, ...), kind=kLoop, calls=%fused_computation.190.clone.1 | loop fusion | flops 84934432 | bytes 12976992 | tf_op jit(solution)/shard_map/while/body/eval_jaxpr/reduce_sum | solution.py:43
  651.2 34.4 %fusion.242 = f32[12,384,512]{1,2,0:T(8,128)S(1)} fusion(f32[12,384]{1,0:T(8,128)} %get-tuple-element.1610, f32[12]{0:T(128)S(1)} %get-tuple-element.1415, f32[12]{0:T(128)S(1)} %get-tuple-element.1416, f32[12]{0:T(128)S(1)} %get-tuple-element.1417, f32[12]{0:T(128)S(1)} %get-tuple-element.1418, f32[12]{0:T(128)S(1)} %get-tuple-element.1419, ...), kind=kOutput, calls=%fused_computation.189.clone.1 | convolution fusion | flops 457703424 | bytes 17140756 | tf_op jit(solution)/shard_map/while/body/eval_jaxpr/qhd,khd->hqk/dot_general | solution.py:72
  712.9 22.0 %select_reduce_fusion.69 = (f32[12]{0:T(128)S(1)}, f32[12]{0:T(128)S(1)}, f32[12]{0:T(128)S(1)}, f32[12]{0:T(128)S(1)}, f32[12]{0:T(128)S(1)}, /*index=5*/f32[12...) fusion(f32[12,384,512]{1,2,0:T(8,128)S(1)} %get-tuple-element.1, ...), kind=kLoop, calls=%fused_computation.190.clone.1 | loop fusion | flops 84934432 | bytes 12976992 | tf_op jit(solution)/shard_map/while/body/eval_jaxpr/reduce_sum | solution.py:43
  767.3 25.4 %select_reduce_fusion.50 = (f32[12]{0:T(128)}, f32[12]{0:T(128)}, f32[12]{0:T(128)}, f32[12]{0:T(128)}, f32[12]{0:T(128)}, /*index=5*/f32[12]{0:T(128)}, f32[12]...) fusion(pred[384,512]{1,0:T(8,128)(4,1)} %get-tuple-element.800,, ...), kind=kOutput, calls=%fused_computation.348 | convolution fusion | flops 377487360 | bytes 23237280 | tf_op jit(solution)/shard_map/qhd,khd->hqk/dot_general | solution.py:347
  836.4 24.7 %reduce-scatter.22.cloned.1.call-done = bf16[96,768]{1,0:T(8,128)(2,1)} async-done(((bf16[768,768]{1,0:T(8,128)(2,1)}), bf16[96,768]{1,0:T(8,128)(2,1)}) %reduce-scatter.22.cloned.1.call-update) | async-done | bytes 147472 | tf_op jit(solution)/shard_map/reduce_scatter | solution.py:449
  861.1 33.6 %reduce-scatter.16.cloned.1.call-done = bf16[96,768]{1,0:T(8,128)(2,1)} async-done(((bf16[768,768]{1,0:T(8,128)(2,1)}), bf16[96,768]{1,0:T(8,128)(2,1)}) %reduce-scatter.16.cloned.1.call-update) | async-done | bytes 147472 | tf_op jit(solution)/shard_map/reduce_scatter | solution.py:440
  894.7 33.2 %reduce-scatter.20.cloned.1.call-done = bf16[96,768]{1,0:T(8,128)(2,1)} async-done(((bf16[768,768]{1,0:T(8,128)(2,1)}), bf16[96,768]{1,0:T(8,128)(2,1)}) %reduce-scatter.20.cloned.1.call-update) | async-done | bytes 147472 | tf_op jit(solution)/shard_map/reduce_scatter | solution.py:446
  927.9 33.9 %reduce-scatter.18.cloned.1.call-done = bf16[96,768]{1,0:T(8,128)(2,1)} async-done(((bf16[768,768]{1,0:T(8,128)(2,1)}), bf16[96,768]{1,0:T(8,128)(2,1)}) %reduce-scatter.18.cloned.1.call-update) | async-done | bytes 147472 | tf_op jit(solution)/shard_map/reduce_scatter | solution.py:443
  981.1 22.9 %select_reduce_fusion.32 = (f32[12]{0:T(128)S(1)}, f32[12]{0:T(128)S(1)}, f32[12]{0:T(128)S(1)}, f32[12]{0:T(128)S(1)}, f32[12]{0:T(128)S(1)}, /*index=5*/f32[12...) fusion(f32[12,384,512]{2,1,0:T(8,128)} %copy-done.2, ...), kind=kLoop, calls=%fused_computation.330 | loop fusion | flops 84934432 | bytes 12976992 | tf_op jit(solution)/shard_map/reduce_sum | solution.py:43
  1011.8 26.3 %all-reduce.6 = (bf16[768]{0:T(1024)(128)(2,1)S(1)}, bf16[768]{0:T(1024)(128)(2,1)S(1)}, bf16[32,12]{1,0:T(8,128)(2,1)S(1)}) all-reduce(bf16[768]{0:T(1024)(128)(2,1)S(1)} %get-tuple-element.475, bf16[768]{0:T(1024)(128)(2,1)} %get-tuple-element.473, ...), channel_id=9, replica_groups=mesh['rep'=4,'shard'=8] {'shard'}, use_global_device_ids=true, to_apply=%region_65.66.clone | all-reduce | flops 1920 | bytes 7680
  1059.1 42.3 %reduce-scatter.26.cloned.1.call-done = bf16[1,768,768]{2,1,0:T(8,128)(2,1)} async-done(((bf16[1,3072,768]{2,1,0:T(8,128)(2,1)}), bf16[1,768,768]{2,1,0:T(8,128)(2,1)}) %reduce-scatter.26.cloned.1.call-update) | async-done | bytes 1179664 | tf_op jit(solution)/shard_map/reduce_scatter | solution.py:481
  1104.2 57.1 %reduce-scatter.24.cloned.1.call-done = bf16[1,192,3072]{2,1,0:T(8,128)(2,1)} async-done(((bf16[1,768,3072]{2,1,0:T(8,128)(2,1)}), bf16[1,192,3072]{2,1,0:T(8,128)(2,1)}) %reduce-scatter.24.cloned.1.call-update) | async-done | bytes 1179664 | tf_op jit(solution)/shard_map/reduce_scatter | solution.py:478
  (607 shorter events, 449.3 us)
Async XLA Ops:
  7.2 28.0 %all-gather.13.cloned.1.call-start = ((), (), s32[]{:S(2)}) async-start(), calls=%async_computation.15 | async-start | bytes 1327104 | tf_op jit(solution)/shard_map/all_gather | solution.py:141
  7.9 51.2 %all-gather.9.cloned.1.call-start = ((), (), s32[]{:S(2)}) async-start(), calls=%async_computation.13 | async-start | bytes 1327104 | tf_op jit(solution)/shard_map/all_gather | solution.py:142
  8.7 81.1 %all-gather.17.cloned.1.call-start = ((), (), s32[]{:S(2)}) async-start(), calls=%async_computation.17 | async-start | bytes 1327104 | tf_op jit(solution)/shard_map/all_gather | solution.py:140
  9.4 128.6 %all-gather.15.cloned.1.call-start = ((), (), s32[]{:S(2)}) async-start(), calls=%async_computation.16 | async-start | bytes 1769472 | tf_op jit(solution)/shard_map/all_gather | solution.py:193
  38.1 104.3 %all-gather.11.cloned.1.call-start = ((), (), s32[]{:S(2)}) async-start(), calls=%async_computation.14 | async-start | bytes 1769472 | tf_op jit(solution)/shard_map/all_gather | solution.py:194
  62.8 305.1 %all-gather.19.cloned.1.call-start = ((), (), s32[]{:S(2)}) async-start(), calls=%async_computation.18 | async-start | bytes 1327104 | tf_op jit(solution)/shard_map/all_gather | solution.py:143
  82.7 10.1 collective-permute-start
  87.3 6.9 collective-permute-start.1
  373.5 49.5 %all-to-all-start = ((bf16[8,96,768]{2,1,0:T(8,128)(2,1)}), bf16[8,96,768]{2,1,0:T(8,128)(2,1)S(1)}, u32[]{:S(2)}, u32[]{:S(2)}) async-start(bf16[8,96,768]{2,1,0:T(8,128)(2,1)} %bitcast.45), calls=%async_computation | async-start | bytes 2359296 | tf_op jit(solution)/shard_map/all_to_all | solution.py:269
  423.0 33.8 %all-to-all-start.2 = ((bf16[8,96,768]{2,1,0:T(8,128)(2,1)}), bf16[8,96,768]{2,1,0:T(8,128)(2,1)}, u32[]{:S(2)}, u32[]{:S(2)}) async-start(bf16[8,96,768]{2,1,0:T(8,128)(2,1)} %bitcast.51), calls=%async_computation.2 | async-start | bytes 2359296 | tf_op jit(solution)/shard_map/all_to_all | solution.py:295
  456.8 33.3 %all-to-all-start.1 = ((bf16[8,96,768]{2,1,0:T(8,128)(2,1)}), bf16[8,96,768]{2,1,0:T(8,128)(2,1)S(1)}, u32[]{:S(2)}, u32[]{:S(2)}) async-start(bf16[8,96,768]{2,1,0:T(8,128)(2,1)} %bitcast.648), calls=%async_computation.1 | async-start | bytes 2359296 | tf_op jit(solution)/shard_map/all_to_all | solution.py:276
  490.1 32.9 %all-to-all-start.3 = ((bf16[8,96,768]{2,1,0:T(8,128)(2,1)}), bf16[8,96,768]{2,1,0:T(8,128)(2,1)S(1)}, u32[]{:S(2)}, u32[]{:S(2)}) async-start(bf16[8,96,768]{2,1,0:T(8,128)(2,1)} %bitcast.647), calls=%async_computation.3 | async-start | bytes 2359296 | tf_op jit(solution)/shard_map/all_to_all | solution.py:312
  493.6 316.7 %reduce-scatter.30.cloned.1.call-start = ((), (), s32[]{:S(2)}) async-start(), calls=%async_computation.26 | async-start | bytes 1769472
  758.0 73.9 %reduce-scatter.28.cloned.1.call-start = ((), (), s32[]{:S(2)}) async-start(), calls=%async_computation.25 | async-start | bytes 1769472
  765.3 95.8 %reduce-scatter.22.cloned.1.call-start = ((), (), s32[]{:S(2)}) async-start(), calls=%async_computation.22 | async-start | bytes 1327104 | tf_op jit(solution)/shard_map/reduce_scatter | solution.py:449
  767.2 127.5 %reduce-scatter.16.cloned.1.call-start = ((), (), s32[]{:S(2)}) async-start(), calls=%async_computation.19 | async-start | bytes 1327104 | tf_op jit(solution)/shard_map/reduce_scatter | solution.py:440
  800.8 127.1 %reduce-scatter.20.cloned.1.call-start = ((), (), s32[]{:S(2)}) async-start(), calls=%async_computation.21 | async-start | bytes 1327104 | tf_op jit(solution)/shard_map/reduce_scatter | solution.py:446
  806.6 3.6 collective-permute-start.3
  813.7 148.1 %reduce-scatter.18.cloned.1.call-start = ((), (), s32[]{:S(2)}) async-start(), calls=%async_computation.20 | async-start | bytes 1327104 | tf_op jit(solution)/shard_map/reduce_scatter | solution.py:443
  818.7 13.1 %collective-permute-start.2 = (bf16[256,768]{0,1:T(8,128)(2,1)S(1)}, bf16[256,768]{0,1:T(8,128)(2,1)S(1)}, u32[]{:S(2)}, u32[]{:S(2)}) collective-permute-start(bf16[256,768]{0,1:T(8,128)(2,1)S(1)} %bitcast.650), channel_id=1, source_target_pairs={{1,0},{2,1},{3,2},{4,3},{5,4},{6,5},{7,6},{9,8},{10,9},{11,10},{12... | collective-permute-start | bytes 1179656 | tf_op jit(solution)/shard_map/ppermute | solution.py:17
  835.0 171.2 %reduce-scatter.32.cloned.1.call-start = ((), (), s32[]{:S(2)}) async-start(), calls=%async_computation.27 | async-start | bytes 221184
  836.4 216.1 %all-reduce.12.cloned.1.call-start = ((), (), s32[]{:S(2)}) async-start(), calls=%async_computation.28 | async-start | bytes 1179648 | tf_op jit(solution)/shard_map/psum | solution.py:466
  961.8 139.6 %reduce-scatter.26.cloned.1.call-start = ((), (), s32[]{:S(2)}) async-start(), calls=%async_computation.24 | async-start | bytes 5898240 | tf_op jit(solution)/shard_map/reduce_scatter | solution.py:481
  971.6 189.7 %reduce-scatter.24.cloned.1.call-start = ((), (), s32[]{:S(2)}) async-start(), calls=%async_computation.23 | async-start | bytes 5898240 | tf_op jit(solution)/shard_map/reduce_scatter | solution.py:478
  (185 other events, 3576.5 us)
Sparse Core Ops, SparseCore 0:
  9.7 25.4 all-gather.12
  36.8 22.2 all-gather.8
  60.8 22.4 all-gather.16
  85.3 24.8 all-gather.14
  112.3 24.5 all-gather.10
  138.4 22.1 all-gather.18
  758.1 32.4 reduce-scatter.29
  793.5 32.7 reduce-scatter.27
  828.5 32.4 reduce-scatter.21
  863.8 30.8 reduce-scatter.15
  897.0 30.8 reduce-scatter.19
  930.6 31.1 reduce-scatter.17
  964.6 28.6 reduce-scatter.31
  996.6 44.7 all-reduce.11
  1044.2 57.1 reduce-scatter.25
  1104.2 57.0 reduce-scatter.23
where the time goes:
time: 1180 us; the launch traced here: 1170 us
  matrix products  443 us (38%)
  waiting for transfers between devices  308 us (26%)
  other arithmetic  165 us (14%)
  blocking collectives  101 us (9%)
  local copies, waits for them, and re-layouts  89.5 us (8%)
  starting transfers between devices  25.1 us (2%)
  loops' own time  22.2 us (2%)
  between operations  17.5 us (1%)
    dot_general x5, matrix products, block_scores(): jnp.einsum('qhd,khd->hqk', query_heads, key_heads, preferred_element_type...  183 us
    dot_general x3, matrix products, output_step(): jnp.einsum('hqk,khd->qhd', weights, value_heads, preferred_element_type=j...  84.3 us
    reduce_sum x3, other arithmetic, bucket_sums(): jnp.sum(jnp.where((buckets == bucket_id)[None], grad_scores, 0.0), axis=(...  66.9 us
    dot_general x3, matrix products, grad_step(): jnp.einsum('qhd,khd->hqk', grad_heads, value_heads, preferred_element_typ...  62.5 us
    reduce_scatter x1, waiting for transfers between devices, local(): lax.psum_scatter(grad_w_in[None].astype(jnp.bfloat16), 'rep', scatter_dim...  57.1 us
    unnamed x2, blocking collectives  44.5 us
    reduce_scatter x1, waiting for transfers between devices, local(): lax.psum_scatter(grad_w_out[None].astype(jnp.bfloat16), 'rep', scatter_di...  42.3 us
    eq x6, other arithmetic, bucket_bias(): buckets == bucket_id  37.4 us
  transfers between devices with their start and end apart: 24, of which 13 were waited for; matrix products, arithmetic and copies ran while one was open for 38% of the time, Pallas kernels for 0%

commit v1 on v0

v1 whole, which is shorter than its diff:
```python
import jax
import jax.numpy as jnp
import numpy as np
from jax import lax
from jax.experimental import pallas as pl
from jax.experimental.pallas import tpu as pltpu
from jax.sharding import PartitionSpec as P

PR_DEV = 128


bucket_edges = (12, 16, 23, 32, 46, 64, 91)
norm_epsilon = 1e-06
masked_score = -1e30


def norm_apply(values, gain_row):
    return (
        values
        * lax.rsqrt(jnp.mean(values * values, axis=-1, keepdims=True) + norm_epsilon)
        * gain_row
    )


def gelu_tanh(values):
    return jax.nn.gelu(values, approximate=True)


TILE = 128
SPAN = 2 * TILE
far_before, far_after, causal_tile, hidden_tile, tile_kinds = 3, 4, 5, 6, 7
vmem_cap = 60 * 1024 * 1024


def nt(left, right):
    return lax.dot_general(
        left, right, (((1,), (1,)), ((), ())), preferred_element_type=jnp.float32
    )


def nn(left, right):
    return jnp.dot(left, right, preferred_element_type=jnp.float32)


def fill_tiles(tiles_ref, rev_row, low, high):
    spread = jnp.broadcast_to(rev_row, (TILE, 4 * TILE))
    rolled = pltpu.roll(spread, 0, 1, stride=1, stride_axis=0)
    keys = lax.broadcasted_iota(jnp.int32, (TILE, TILE), 0)
    rows = lax.broadcasted_iota(jnp.int32, (TILE, TILE), 1)
    tiles_ref[0] = rolled[:, TILE : 2 * TILE]
    tiles_ref[1] = rolled[:, :TILE]
    tiles_ref[2] = rolled[:, 3 * TILE :]
    tiles_ref[far_before] = jnp.broadcast_to(low, (TILE, TILE))
    tiles_ref[far_after] = jnp.broadcast_to(high, (TILE, TILE))
    tiles_ref[causal_tile] = jnp.where(keys <= rows, rolled[:, :TILE], masked_score)
    tiles_ref[hidden_tile] = jnp.full((TILE, TILE), masked_score, jnp.float32)


def prompt_tile(block, chunk, shard_id, block_count):
    if chunk == 0:
        gap = block - shard_id
        far = jnp.where(gap < 0, far_before, far_after)
        return jnp.where(jnp.abs(gap) <= 1, gap + 1, far)
    if chunk == 1 and block == block_count - 1:
        return jnp.where(shard_id % 2 == 0, 0, far_before)
    return far_before


def local_tile(block, chunk, shard_id):
    if block >= 2:
        return ((causal_tile, 0), (hidden_tile, causal_tile))[block - 2][chunk]
    kind = 0 if (block, chunk) == (1, 0) else far_before
    return jnp.where(shard_id % 2 == 1, kind, hidden_tile)


def prompt_grid(part, shard_id, block_count):
    return [
        [prompt_tile(2 * part + half, chunk, shard_id, block_count) for chunk in range(3)]
        for half in range(2)
    ]


def local_grid(part, shard_id):
    return [[local_tile(2 * part + half, chunk, shard_id) for chunk in range(2)] for half in range(2)]


def with_bias(scores, tiles_ref, grid):
    return jnp.concatenate(
        [
            jnp.concatenate(
                [
                    scores[i * TILE : (i + 1) * TILE, j * TILE : (j + 1) * TILE] + tiles_ref[kind]
                    for j, kind in enumerate(row)
                ],
                axis=1,
            )
            for i, row in enumerate(grid)
        ],
        axis=0,
    )


def fold8(values):
    return values.reshape(values.shape[0] // 8, 8, values.shape[1])


def head_mask(rows, side):
    lanes = lax.broadcasted_iota(jnp.int32, (rows, TILE), 1)
    return (lanes < TILE // 2) if side == 0 else (lanes >= TILE // 2)


def attn_forward_kernel(
    rev_ref, q_ref, k_ref, v_ref, out_ref, lse_ref,
    tiles, vt, sp, sl, ot,
):
    shard_id = lax.axis_index("shard")
    rows = q_ref.shape[0]
    prompt_rows = TILE
    blocks = k_ref.shape[0] // TILE - 4
    half = TILE // 2

    @pl.loop(0, q_ref.shape[1] // TILE)
    def pair_loop(pair):
        cols = pl.ds(pl.multiple_of(pair * TILE, TILE), TILE)
        vt[...] = v_ref[:, cols].T
        q_pair = q_ref[:, cols] * jnp.asarray(0.125, q_ref.dtype)
        for side in range(2):
            head = pair * 2 + side
            rev_row = rev_ref[pl.ds(head, 1), :]
            fill_tiles(tiles, rev_row, rev_row[:, 4 * TILE // 2 - 1 : 4 * TILE // 2], rev_row[:, 4 * TILE // 2 : 4 * TILE // 2 + 1])
            q_head = jnp.where(head_mask(rows, side), q_pair, jnp.zeros_like(q_pair))
            top = jnp.full((8, rows), masked_score, jnp.float32)
            for part in range(blocks // 2):
                keys = slice(part * SPAN, (part + 1) * SPAN)
                scores = with_bias(nt(k_ref[keys, cols], q_head), tiles, prompt_grid(part, shard_id, blocks))
                sp[keys, :] = scores
                top = jnp.maximum(top, jnp.max(fold8(scores), axis=0))
            top_local = top[:, prompt_rows:]
            for part in range(2):
                keys = slice(part * SPAN, (part + 1) * SPAN)
                held = slice((blocks // 2 + part) * SPAN, (blocks // 2 + part + 1) * SPAN)
                scores = with_bias(nt(k_ref[held, cols], q_head[prompt_rows:]), tiles, local_grid(part, shard_id))
                sl[keys, :] = scores
                top_local = jnp.maximum(top_local, jnp.max(fold8(scores), axis=0))
            top = jnp.max(jnp.concatenate([top[:, :prompt_rows], top_local], axis=1), axis=0, keepdims=True)
            total = jnp.zeros((8, rows), jnp.float32)
            summed = jnp.zeros((half, rows), jnp.float32)
            heads = slice(side * half, (side + 1) * half)
            for part in range(blocks // 2):
                keys = slice(part * SPAN, (part + 1) * SPAN)
                weights = jnp.exp(sp[keys, :] - top)
                total = total + jnp.sum(fold8(weights), axis=0)
                summed = summed + nn(vt[heads, keys], weights.astype(jnp.bfloat16))
            top_c = top[:, prompt_rows:]
            total_c = total[:, prompt_rows:]
            summed_c = summed[:, prompt_rows:]
            for part in range(2):
                keys = slice(part * SPAN, (part + 1) * SPAN)
                held = slice((blocks // 2 + part) * SPAN, (blocks // 2 + part + 1) * SPAN)
                weights = jnp.exp(sl[keys, :] - top_c)
                total_c = total_c + jnp.sum(fold8(weights), axis=0)
                summed_c = summed_c + nn(vt[heads, held], weights.astype(jnp.bfloat16))
            total = jnp.sum(jnp.concatenate([total[:, :prompt_rows], total_c], axis=1), axis=0, keepdims=True)
            summed = jnp.concatenate([summed[:, :prompt_rows], summed_c], axis=1)
            ot[heads, :] = summed / total
            lse_ref[pl.ds(head, 1), :] = top + jnp.log(total)
        out_ref[:, cols] = ot[...].T


def attn_forward(rev, queries, keys, values):
    rows, width = queries.shape
    head_rows = rev.shape[0]
    spec = pl.BlockSpec(memory_space=pltpu.VMEM)
    return pl.pallas_call(
        attn_forward_kernel,
        out_shape=(
            jax.ShapeDtypeStruct((rows, width), jnp.float32),
            jax.ShapeDtypeStruct((head_rows, rows), jnp.float32),
        ),
        in_specs=[spec] * 4,
        out_specs=(spec, spec),
        scratch_shapes=[
            pltpu.VMEM((tile_kinds, TILE, TILE), jnp.float32),
            pltpu.VMEM((TILE, keys.shape[0]), jnp.bfloat16),
            pltpu.VMEM((keys.shape[0] - 2 * SPAN, rows), jnp.float32),
            pltpu.VMEM((2 * SPAN, rows - TILE), jnp.float32),
            pltpu.VMEM((TILE, rows), jnp.float32),
        ],
        compiler_params=pltpu.CompilerParams(vmem_limit_bytes=vmem_cap),
        cost_estimate=pl.CostEstimate(flops=20_000_000_000, bytes_accessed=12_000_000, transcendentals=8_000_000),
        name="attn_forward",
    )(rev, queries, keys, values)


def attn_backward_kernel(
    rev_ref, hot_ref, q_ref, k_ref, v_ref, g_ref, o_ref, lse_ref,
    dq_ref, dk_ref, dv_ref, table_ref,
    tiles, sums, diag, kt, dqt, far_sums, dk_sum, dv_sum,
):
    shard_id = lax.axis_index("shard")
    rows = q_ref.shape[0]
    prompt_rows = TILE
    blocks = k_ref.shape[0] // TILE - 4
    half = TILE // 2
    diag[...] = jnp.zeros_like(diag)
    far_sums[...] = jnp.zeros_like(far_sums)
    tile_rows = lax.broadcasted_iota(jnp.int32, (TILE, TILE), 0)
    tile_cols = lax.broadcasted_iota(jnp.int32, (TILE, TILE), 1)
    flip = (tile_rows + tile_cols == TILE - 1).astype(jnp.float32)

    @pl.loop(0, q_ref.shape[1] // TILE)
    def pair_loop(pair):
        cols = pl.ds(pl.multiple_of(pair * TILE, TILE), TILE)
        kt[...] = k_ref[:, cols].T
        q_pair = q_ref[:, cols] * jnp.asarray(0.125, q_ref.dtype)
        g_pair = g_ref[:, cols]
        delta_t = (g_pair.astype(jnp.float32) * o_ref[:, cols]).T
        for side in range(2):
            head = pair * 2 + side
            heads = slice(side * half, (side + 1) * half)
            rev_row = rev_ref[pl.ds(head, 1), :]
            fill_tiles(tiles, rev_row, rev_row[:, 4 * TILE // 2 - 1 : 4 * TILE // 2], rev_row[:, 4 * TILE // 2 : 4 * TILE // 2 + 1])
            sums[...] = jnp.zeros_like(sums)
            mask = head_mask(rows, side)
            q_head = jnp.where(mask, q_pair, jnp.zeros_like(q_pair))
            g_head = jnp.where(mask, g_pair, jnp.zeros_like(g_pair))
            delta = jnp.sum(delta_t[heads, :], axis=0, keepdims=True)
            log_total = lse_ref[pl.ds(head, 1), :]

            def block_grads(part, first, grid):
                keys = slice(part * SPAN, (part + 1) * SPAN)
                q_rows, g_rows = q_head[first:], g_head[first:]
                scores = with_bias(nt(k_ref[keys, cols], q_rows), tiles, grid)
                weights = jnp.exp(scores - log_total[:, first:])
                grad_weights = nt(v_ref[keys, cols], g_rows)
                grad_scores = weights * (grad_weights - delta[:, first:])
                for i, row in enumerate(grid):
                    for j, kind in enumerate(row):
                        sums[kind] += grad_scores[i * TILE : (i + 1) * TILE, j * TILE : (j + 1) * TILE]
                raw = grad_scores.astype(jnp.bfloat16)
                dk = nn(raw, q_rows)
                dv = nn(weights.astype(jnp.bfloat16), g_rows)
                if side == 0:
                    dk_sum[keys, :] = dk
                    dv_sum[keys, :] = dv
                else:
                    dk_ref[keys, cols] = (dk_sum[keys, :] + dk).astype(dk_ref.dtype)
                    dv_ref[keys, cols] = (dv_sum[keys, :] + dv).astype(dv_ref.dtype)
                return nn(kt[heads, keys], raw)

            dq = jnp.zeros((half, rows), jnp.float32)
            for part in range(blocks // 2):
                dq = dq + block_grads(part, 0, prompt_grid(part, shard_id, blocks))
            dq_c = dq[:, prompt_rows:]
            for part in range(2):
                dq_c = dq_c + block_grads(blocks // 2 + part, prompt_rows, local_grid(part, shard_id))
            dqt[heads, :] = jnp.concatenate([dq[:, :prompt_rows], dq_c], axis=1)
            near = jnp.concatenate(
                [sums[1] + sums[causal_tile], sums[0], jnp.zeros((TILE, TILE), jnp.float32), sums[2]], axis=1
            )
            flipped = jnp.dot(flip, near, precision=lax.Precision.HIGHEST, preferred_element_type=jnp.float32)
            rolled = pltpu.roll(flipped, 3 * TILE + 1, 1, stride=1, stride_axis=0)
            diag[pl.ds(head, 1), :] = jnp.sum(rolled, axis=0, keepdims=True)
            far_sums[pl.ds(head, 1), :] = jnp.concatenate(
                [jnp.sum(sums[far_before], axis=0, keepdims=True), jnp.sum(sums[far_after], axis=0, keepdims=True)], axis=1
            )
        dq_ref[:, cols] = (dqt[...].T * 0.125).astype(dq_ref.dtype)

    by_bucket = jnp.dot(diag[...], hot_ref[...], precision=lax.Precision.HIGHEST, preferred_element_type=jnp.float32)
    lanes = lax.broadcasted_iota(jnp.int32, by_bucket.shape, 1)
    before = jnp.sum(far_sums[:, :TILE], axis=1, keepdims=True)
    after = jnp.sum(far_sums[:, TILE:], axis=1, keepdims=True)
    table_ref[...] = by_bucket + jnp.where(lanes == 15, before, 0.0) + jnp.where(lanes == 31, after, 0.0)


def attn_backward(rev, hot, queries, keys, values, grad_heads, attended, lse):
    rows, width = queries.shape
    head_rows = rev.shape[0]
    spec = pl.BlockSpec(memory_space=pltpu.VMEM)
    return pl.pallas_call(
        attn_backward_kernel,
        out_shape=(
            jax.ShapeDtypeStruct((rows, width), jnp.bfloat16),
            jax.ShapeDtypeStruct(keys.shape, jnp.bfloat16),
            jax.ShapeDtypeStruct(values.shape, jnp.bfloat16),
            jax.ShapeDtypeStruct((head_rows, hot.shape[1]), jnp.float32),
        ),
        in_specs=[spec] * 8,
        out_specs=(spec,) * 4,
        scratch_shapes=[
            pltpu.VMEM((tile_kinds, TILE, TILE), jnp.float32),
            pltpu.VMEM((tile_kinds, TILE, TILE), jnp.float32),
            pltpu.VMEM((head_rows, 4 * TILE), jnp.float32),
            pltpu.VMEM((TILE, keys.shape[0]), jnp.bfloat16),
            pltpu.VMEM((TILE, rows), jnp.float32),
            pltpu.VMEM((head_rows, 2 * TILE), jnp.float32),
            pltpu.VMEM((keys.shape[0], TILE), jnp.float32),
            pltpu.VMEM((keys.shape[0], TILE), jnp.float32),
        ],
        compiler_params=pltpu.CompilerParams(vmem_limit_bytes=vmem_cap),
        cost_estimate=pl.CostEstimate(flops=40_000_000_000, bytes_accessed=24_000_000, transcendentals=8_000_000),
        name="attn_backward",
    )(rev, hot, queries, keys, values, grad_heads, attended, lse)


def distance_buckets(bucket_count):
    steps = np.arange(4 * TILE)
    gap = -np.where(steps < 2 * TILE, steps, steps - 4 * TILE)
    size = np.abs(gap)
    far = sum((size >= edge).astype(np.int64) for edge in bucket_edges)
    exact = bucket_count // 4
    return np.where(gap > 0, bucket_count // 2, 0) + np.where(size < exact, size, exact + far)


QUARTERS = 4
mesh_ids = pl.DeviceIdType.MESH


def places():
    rep, shard = lax.axis_index("rep"), lax.axis_index("shard")
    return rep, shard // 2, shard % 2, lax.axis_size("shard") // 2, rep % QUARTERS


def peer_lists():
    rep, chip, core, chips, quarter = places()
    along = [(rep, (chip + k) % chips * 2 + core) for k in range(1, chips)]
    across = [(rep - quarter + (quarter + j) % QUARTERS, chip * 2 + core) for j in range(1, QUARTERS)]
    twin = (rep, chip * 2 + 1 - core)
    return along, across, twin


def greet(devices):
    barrier = pltpu.get_barrier_semaphore()
    for device in devices:
        pl.semaphore_signal(barrier, inc=1, device_id=device, device_id_type=mesh_ids)
    pl.semaphore_wait(barrier, len(devices))


def send(source, target, sems, device):
    return pltpu.make_async_remote_copy(
        src_ref=source, dst_ref=target, send_sem=sems[0], recv_sem=sems[1],
        device_id=device, device_id_type=mesh_ids,
    )


def gather_kernel(
    w_ref, tok_ref, small_ref, wg_ref, tg_ref, near_ref, sg_ref,
    wz_s, wz_r, tz_s, tz_r, sz_s, sz_r, wr_s, wr_r, wt_s, wt_r, et_s, et_r, loc,
):
    rep, chip, core, chips, quarter = places()
    along, across, twin = peer_lists()
    prompt = tok_ref.at[pl.ds(0, PR_DEV)]
    rest = tok_ref.at[pl.ds(PR_DEV, tok_ref.shape[0] - PR_DEV)]
    own = [
        pltpu.make_async_copy(w_ref, wg_ref.at[:, chip, core], loc.at[0]),
        pltpu.make_async_copy(prompt, tg_ref.at[chip, core], loc.at[1]),
        pltpu.make_async_copy(small_ref, sg_ref.at[chip, core], loc.at[2]),
    ]
    for copy in own:
        copy.start()
    greet(along + across + [twin])
    w_out, t_out, s_out = [], [], []
    for k, device in enumerate(along):
        w_out.append(send(w_ref.at[:, quarter], wg_ref.at[:, chip, core, quarter], (wz_s.at[k], wz_r.at[k]), device))
        s_out.append(send(small_ref, sg_ref.at[chip, core], (sz_s.at[k], sz_r.at[k]), device))
        t_out.append(send(prompt, tg_ref.at[chip, core], (tz_s.at[k], tz_r.at[k]), device))
    for copy in w_out + s_out + t_out:
        copy.start()
    near = send(rest, near_ref, (et_s.at[0], et_r.at[0]), twin)
    near.start()
    for copy in own:
        copy.wait()
    row_out = [send(wg_ref.at[:, chip, core], wg_ref.at[:, chip, core], (wt_s.at[0], wt_r.at[0]), twin)]
    row_out[0].start()
    r_out = []
    for k in range(1, chips):
        source = (chip + chips - k) % chips
        piece = wg_ref.at[:, source, core, quarter]
        send(piece, piece, (wz_s.at[k - 1], wz_r.at[k - 1]), twin).wait_recv()
        for j, device in enumerate(across):
            r_out.append(send(piece, piece, (wr_s.at[k - 1, j], wr_r.at[k - 1, j]), device))
            r_out[-1].start()
    for k in range(1, chips):
        source = (chip + chips - k) % chips
        for j in range(1, QUARTERS):
            piece = wg_ref.at[:, source, core, (quarter + QUARTERS - j) % QUARTERS]
            send(piece, piece, (wr_s.at[k - 1, j - 1], wr_r.at[k - 1, j - 1]), twin).wait_recv()
        row = wg_ref.at[:, source, core]
        row_out.append(send(row, row, (wt_s.at[k], wt_r.at[k]), twin))
        row_out[-1].start()
    for k in range(1, chips):
        source = (chip + chips - k) % chips
        send(prompt, tg_ref.at[source, core], (tz_s.at[k - 1], tz_r.at[k - 1]), twin).wait_recv()
        send(small_ref, sg_ref.at[source, core], (sz_s.at[k - 1], sz_r.at[k - 1]), twin).wait_recv()
    ends = [
        send(tg_ref.at[:, core], tg_ref.at[:, core], (et_s.at[1], et_r.at[1]), twin),
        send(sg_ref.at[:, core], sg_ref.at[:, core], (et_s.at[2], et_r.at[2]), twin),
    ]
    for copy in ends:
        copy.start()
    near.wait_recv()
    for k in range(chips):
        source = (chip + chips - k) % chips
        row = wg_ref.at[:, source, 1 - core]
        send(row, row, (wt_s.at[k], wt_r.at[k]), twin).wait_recv()
    send(tg_ref.at[:, core], tg_ref.at[:, 1 - core], (et_s.at[1], et_r.at[1]), twin).wait_recv()
    send(sg_ref.at[:, core], sg_ref.at[:, 1 - core], (et_s.at[2], et_r.at[2]), twin).wait_recv()
    for copy in w_out + s_out + t_out + r_out + row_out + ends + [near]:
        copy.wait_send()


def gather_all(weights, tokens, small):
    chips = lax.axis_size("shard") // 2
    width = tokens.shape[1]
    pairs = pltpu.SemaphoreType.DMA
    anywhere = pl.BlockSpec(memory_space=pl.ANY)
    count = chips - 1
    return pl.pallas_call(
        gather_kernel,
        out_shape=(
            jax.ShapeDtypeStruct((weights.shape[0], chips, 2) + weights.shape[1:], weights.dtype),
            jax.ShapeDtypeStruct((chips, 2, PR_DEV, width), tokens.dtype),
            jax.ShapeDtypeStruct((tokens.shape[0] - PR_DEV, width), tokens.dtype),
            jax.ShapeDtypeStruct((chips, 2) + small.shape, small.dtype),
        ),
        in_specs=[anywhere] * 3,
        out_specs=(anywhere,) * 4,
        scratch_shapes=[
            pairs((count,)), pairs((count,)), pairs((count,)), pairs((count,)), pairs((count,)), pairs((count,)),
            pairs((count, 3)), pairs((count, 3)), pairs((chips,)), pairs((chips,)), pairs((3,)), pairs((3,)),
            pairs((3,)),
        ],
        compiler_params=pltpu.CompilerParams(collective_id=0, has_side_effects=True),
        cost_estimate=pl.CostEstimate(flops=0, bytes_accessed=100_000_000, transcendentals=0),
        name="gather_all",
    )(weights, tokens, small)


def reduce_kernel(
    d_ref, p_ref, e_ref, out_ref, po_ref, eo_ref,
    half, summed, third, thirds, fourth, fourths, last, gathered, p_half, p_sum, p_in,
    ds_s, ds_r, ps_s, ps_r, dr_s, dr_r, dh_s, dh_r, dz_s, dz_r, pz_s, pz_r, da_s, da_r,
):
    rep, chip, core, chips, quarter = places()
    along, across, twin = peer_lists()
    classes = lax.axis_size("rep") // QUARTERS
    above = [
        ((rep // QUARTERS + k) % classes * QUARTERS + quarter, chip * 2 + core) for k in range(1, classes)
    ]
    greet(along + across + above + [twin])
    single = jnp.float32
    first = [
        send(p_ref.at[:, 1 - core], p_half, (ps_s.at[0], ps_r.at[0]), twin),
        send(e_ref, eo_ref, (ps_s.at[1], ps_r.at[1]), twin),
    ] + [
        send(d_ref.at[k, 1 - core], half.at[k], (ds_s.at[k], ds_r.at[k]), twin) for k in range(chips)
    ]
    for copy in first:
        copy.start()
    pending = list(first)
    first[0].wait_recv()
    for k in range(chips):
        p_sum[k] = (p_ref[k, core].astype(single) + p_half[k].astype(single)).astype(p_sum.dtype)
    for k, device in enumerate(along):
        copy = send(p_sum.at[(chip + k + 1) % chips], p_in.at[k], (pz_s.at[k], pz_r.at[k]), device)
        copy.start()
        pending.append(copy)
    for k in range(chips):
        first[2 + k].wait_recv()
        for t in range(QUARTERS):
            summed[t, k] = (d_ref[k, core, t].astype(single) + half[k, t].astype(single)).astype(summed.dtype)
    for j, device in enumerate(across):
        copy = send(summed.at[(quarter + j + 1) % QUARTERS], third.at[j], (dr_s.at[j], dr_r.at[j]), device)
        copy.start()
        pending.append(copy)
    for j in range(QUARTERS - 1):
        send(third.at[j], third.at[j], (dr_s.at[j], dr_r.at[j]), twin).wait_recv()
    for k in range(chips):
        total = summed[quarter, k].astype(single)
        for j in range(QUARTERS - 1):
            total = total + third[j, k].astype(single)
        thirds[k] = total.astype(thirds.dtype)
    if classes > 1:
        for j, device in enumerate(above):
            copy = send(thirds, fourth.at[j], (dh_s.at[j], dh_r.at[j]), device)
            copy.start()
            pending.append(copy)
        for j in range(classes - 1):
            send(thirds, fourth.at[j], (dh_s.at[j], dh_r.at[j]), twin).wait_recv()
        for k in range(chips):
            total = thirds[k].astype(single)
            for j in range(classes - 1):
                total = total + fourth[j, k].astype(single)
            fourths[k] = total.astype(fourths.dtype)
    else:
        fourths = thirds
    for k, device in enumerate(along):
        copy = send(fourths.at[(chip + k + 1) % chips], last.at[k], (dz_s.at[k], dz_r.at[k]), device)
        copy.start()
        pending.append(copy)
    for k in range(chips - 1):
        send(p_in.at[k], p_in.at[k], (pz_s.at[k], pz_r.at[k]), twin).wait_recv()
    total = p_sum[chip].astype(single)
    for k in range(chips - 1):
        total = total + p_in[k].astype(single)
    po_ref[...] = total
    for k in range(chips - 1):
        send(last.at[k], last.at[k], (dz_s.at[k], dz_r.at[k]), twin).wait_recv()
    total = fourths[chip].astype(single)
    for k in range(chips - 1):
        total = total + last[k].astype(single)
    gathered[quarter] = total.astype(gathered.dtype)
    for j, device in enumerate(across):
        copy = send(gathered.at[quarter], gathered.at[quarter], (da_s.at[j], da_r.at[j]), device)
        copy.start()
        pending.append(copy)
    for j in range(QUARTERS - 1):
        piece = gathered.at[(quarter + QUARTERS - j - 1) % QUARTERS]
        send(piece, piece, (da_s.at[j], da_r.at[j]), twin).wait_recv()
    out_ref[...] = gathered[...].astype(single)
    first[1].wait_recv()
    for copy in pending:
        copy.wait_send()


def reduce_all(dense, prompt_part, near_part):
    chips = lax.axis_size("shard") // 2
    classes = lax.axis_size("rep") // QUARTERS
    piece = dense.shape[3:]
    low = jnp.bfloat16
    pairs = pltpu.SemaphoreType.DMA
    spec = pl.BlockSpec(memory_space=pltpu.VMEM)
    count = chips - 1
    return pl.pallas_call(
        reduce_kernel,
        out_shape=(
            jax.ShapeDtypeStruct((QUARTERS,) + piece, jnp.float32),
            jax.ShapeDtypeStruct(prompt_part.shape[2:], jnp.float32),
            jax.ShapeDtypeStruct(near_part.shape, low),
        ),
        in_specs=[spec] * 3,
        out_specs=(spec,) * 3,
        scratch_shapes=[
            pltpu.VMEM((chips, QUARTERS) + piece, low),
            pltpu.VMEM((QUARTERS, chips) + piece, low),
            pltpu.VMEM((QUARTERS - 1, chips) + piece, low),
            pltpu.VMEM((chips,) + piece, low),
            pltpu.VMEM((max(classes - 1, 1), chips if classes > 1 else 1) + piece, low),
            pltpu.VMEM((chips if classes > 1 else 1,) + piece, low),
            pltpu.VMEM((count,) + piece, low),
            pltpu.VMEM((QUARTERS,) + piece, low),
            pltpu.VMEM((chips,) + prompt_part.shape[2:], low),
            pltpu.VMEM((chips,) + prompt_part.shape[2:], low),
            pltpu.VMEM((count,) + prompt_part.shape[2:], low),
            pairs((chips,)), pairs((chips,)), pairs((2,)), pairs((2,)), pairs((3,)), pairs((3,)),
            pairs((max(classes - 1, 1),)), pairs((max(classes - 1, 1),)),
            pairs((count,)), pairs((count,)), pairs((count,)), pairs((count,)), pairs((3,)), pairs((3,)),
        ],
        compiler_params=pltpu.CompilerParams(collective_id=1, has_side_effects=True, vmem_limit_bytes=vmem_cap),
        cost_estimate=pl.CostEstimate(flops=0, bytes_accessed=200_000_000, transcendentals=0),
        name="reduce_all",
    )(dense, prompt_part, near_part)


def local(
    tokens,
    routes,
    slot_ids,
    w_query,
    w_key,
    w_value,
    w_output,
    w_router,
    norm_attn,
    norm_moe,
    rel_table,
    w_in,
    w_out,
    cotangent,
):
    shard_count = lax.axis_size("shard")
    token_rows, model_width = tokens.shape
    cont_rows = token_rows - PR_DEV
    prompt_len = PR_DEV * shard_count
    low, single = jnp.bfloat16, jnp.float32
    weight_rows, expert_count = w_router.shape
    table_rows, head_count = rel_table.shape
    bucket_count = table_rows * shard_count
    capacity = 2 * token_rows // expert_count

    weights = jnp.stack([w_query, w_key, w_value, w_output]).reshape(4, QUARTERS, -1, model_width)
    small = jnp.concatenate(
        [w_router, norm_attn[:, None], norm_moe[:, None],
         jnp.pad(rel_table, ((0, weight_rows - table_rows), (0, 0)))], axis=1
    )
    small = jnp.pad(small, ((0, 0), (0, TILE - small.shape[1])))
    weights, prompt_tok, near_tok, small = gather_all(weights, tokens, small)
    query_full, key_full, value_full, output_full = (
        weights[i].reshape(model_width, model_width) for i in range(4)
    )
    small = small.reshape(model_width, TILE)
    router_full = small[:, :expert_count]
    gain_attn = small[:, expert_count].astype(single)
    gain_moe = small[:, expert_count + 1].astype(single)
    table_full = small.reshape(shard_count, weight_rows, TILE)[
        :, :table_rows, expert_count + 2 : expert_count + 2 + head_count
    ].reshape(bucket_count, head_count)

    buckets = distance_buckets(bucket_count)
    hot = (buckets[:, None] == np.arange(TILE)[None]).astype(np.float32)
    rev = jnp.dot(
        jnp.pad(table_full.T, ((0, 16 - head_count), (0, 0))),
        jnp.asarray(hot[:, :bucket_count].T, low),
        preferred_element_type=single,
    )
    resid_in = tokens.astype(single)

    def scaled(values):
        return values * lax.rsqrt(jnp.mean(values * values, axis=-1, keepdims=True) + norm_epsilon)

    every_tok = jnp.concatenate(
        [prompt_tok.reshape(prompt_len, model_width), near_tok, tokens[PR_DEV:]]
    ).astype(single)
    normed_all = (scaled(every_tok) * gain_attn).astype(low)
    normed_own, norm_pull_in = jax.vjp(norm_apply, resid_in, gain_attn)
    normed_own = normed_own.astype(low)
    queries = jnp.dot(normed_own, query_full, preferred_element_type=single).astype(low)
    keys = jnp.dot(normed_all, key_full, preferred_element_type=single).astype(low)
    values = jnp.dot(normed_all, value_full, preferred_element_type=single).astype(low)
    attended, lse = attn_forward(rev, queries, keys, values)
    attn_low = attended.astype(low)
    resid_mid = resid_in + jnp.dot(attn_low, output_full, preferred_element_type=single)
    normed_mid, norm_pull_mid = jax.vjp(norm_apply, resid_mid, gain_moe)
    mid_low = normed_mid.astype(low)
    router_probs = jax.nn.softmax(
        jnp.dot(mid_low, router_full, preferred_element_type=single), axis=-1
    )
    route_match = routes[:, None] == jnp.arange(expert_count, dtype=jnp.int32)[None, :]
    gate_value = jnp.sum(jnp.where(route_match, router_probs, 0.0), axis=-1)
    dispatch = routes * capacity + slot_ids
    slots = jnp.arange(expert_count * capacity, dtype=jnp.int32)
    place = (slots[:, None] == dispatch[None, :]).astype(low)

    def to_experts(rows):
        buffer = jnp.dot(place, rows, preferred_element_type=single).astype(low)
        return lax.all_to_all(
            buffer.reshape(expert_count, capacity, model_width),
            "shard", split_axis=0, concat_axis=0, tiled=True,
        ).reshape(-1, model_width)

    def from_experts(rows):
        back = lax.all_to_all(
            rows.reshape(expert_count, capacity, model_width),
            "shard", split_axis=0, concat_axis=0, tiled=True,
        ).reshape(-1, model_width)
        return lax.dot_general(place, back, (((0,), (0,)), ((), ())), preferred_element_type=single)

    grad_final = cotangent.astype(single)
    rows_in = to_experts(mid_low)
    grad_rows = to_experts((gate_value[:, None] * grad_final).astype(low))
    pre_act = jnp.dot(rows_in, w_in[0], preferred_element_type=single)
    hidden_single, gelu_pull = jax.vjp(gelu_tanh, pre_act)
    hidden = hidden_single.astype(low)
    expert_single = from_experts(
        jnp.dot(hidden, w_out[0], preferred_element_type=single).astype(low)
    )
    mixed = (resid_mid + gate_value[:, None] * expert_single).astype(low)
    grad_gate = jnp.sum(grad_final * expert_single, axis=-1)
    grad_hidden = jnp.einsum("sd,fd->sf", grad_rows, w_out[0], preferred_element_type=single)
    grad_pre = gelu_pull(grad_hidden)[0].astype(low)
    grad_slot = from_experts(
        jnp.einsum("sf,df->sd", grad_pre, w_in[0], preferred_element_type=single).astype(low)
    )
    grad_w_out = jnp.einsum("sf,sd->fd", hidden, grad_rows, preferred_element_type=single)
    grad_w_in = jnp.einsum("sd,sf->df", rows_in, grad_pre, preferred_element_type=single)
    grad_w_in, grad_w_out = grad_w_in[None].astype(low), grad_w_out[None].astype(low)

    grad_logits = (gate_value * grad_gate)[:, None] * (route_match.astype(single) - router_probs)
    grad_router = jnp.dot(
        mid_low.astype(single).T, grad_logits, precision=lax.Precision.HIGHEST
    )
    grad_mid = grad_slot + jnp.dot(
        grad_logits, router_full.astype(single).T, precision=lax.Precision.HIGHEST
    )
    grad_resid_part, grad_gain_moe = norm_pull_mid(grad_mid)
    grad_resid = grad_final + grad_resid_part
    grad_attn = grad_resid.astype(low)
    grad_heads = jnp.einsum(
        "te,de->td", grad_attn, output_full, preferred_element_type=single
    ).astype(low)
    grad_heads, grad_w_in, grad_w_out = lax.optimization_barrier((grad_heads, grad_w_in, grad_w_out))
    expert_in_grad = lax.psum_scatter(grad_w_in, "rep", scatter_dimension=1, tiled=True).astype(single)
    expert_out_grad = lax.psum_scatter(grad_w_out, "rep", scatter_dimension=1, tiled=True).astype(single)
    grad_queries, grad_keys, grad_values, grad_table = attn_backward(
        rev, jnp.asarray(hot), queries, keys, values, grad_heads, attended, lse
    )
    outer = lambda left, right: jnp.einsum("td,te->de", left, right, preferred_element_type=single)
    back = lambda left, right: jnp.einsum("te,de->td", left, right, preferred_element_type=single)
    grad_all = back(grad_keys, key_full) + back(grad_values, value_full)
    grad_own = back(grad_queries, query_full)
    grad_gain_attn = jnp.sum(grad_all * scaled(every_tok), axis=0) + jnp.sum(
        grad_own * scaled(resid_in), axis=0
    )
    table_small = jnp.pad(
        grad_table[:head_count, :bucket_count].T.reshape(shard_count, table_rows, head_count),
        ((0, 0), (0, weight_rows - table_rows), (0, 0)),
    ).reshape(model_width, head_count)
    small_grads = jnp.concatenate(
        [grad_router, grad_gain_attn[:, None], grad_gain_moe[:, None], table_small], axis=1
    )
    small_grads = jnp.pad(small_grads, ((0, 0), (0, TILE - small_grads.shape[1])))
    dense = jnp.concatenate(
        [
            outer(normed_own, grad_queries), outer(normed_all, grad_keys),
            outer(normed_all, grad_values), outer(attn_low, grad_attn), small_grads,
        ],
        axis=1,
    ).astype(low)
    chips = shard_count // 2
    dense, prompt_sum, near_grad = reduce_all(
        dense.reshape(chips, 2, QUARTERS, weight_rows // QUARTERS, -1),
        grad_all[:prompt_len].astype(low).reshape(chips, 2, PR_DEV, model_width),
        grad_all[prompt_len : prompt_len + cont_rows].astype(low),
    )
    grad_normed = grad_own + jnp.concatenate(
        [prompt_sum, grad_all[prompt_len + cont_rows :] + near_grad.astype(single)]
    )
    grad_tokens = grad_resid + norm_pull_in(grad_normed)[0]
    dense = dense.reshape(weight_rows, -1)
    parts = [dense[:, i * model_width : (i + 1) * model_width] for i in range(4)]
    tail = dense[:, 4 * model_width :]
    return (
        mixed,
        grad_tokens,
        *parts,
        tail[:, :expert_count],
        tail[:, expert_count],
        tail[:, expert_count + 1],
        tail[:table_rows, expert_count + 2 : expert_count + 2 + head_count],
        expert_in_grad,
        expert_out_grad,
    )


def solution(mesh):
    return jax.shard_map(
        local,
        mesh=mesh,
        in_specs=(
            P(("rep", "shard"), None),
            P(("rep", "shard")),
            P(("rep", "shard")),
            P("shard", None),
            P("shard", None),
            P("shard", None),
            P("shard", None),
            P("shard", None),
            P("shard"),
            P("shard"),
            P("shard", None),
            P("shard", None, None),
            P("shard", None, None),
            P(("rep", "shard"), None),
        ),
        out_specs=(
            P(("rep", "shard"), None),
            P(("rep", "shard"), None),
            P("shard", None),
            P("shard", None),
            P("shard", None),
            P("shard", None),
            P("shard", None),
            P("shard"),
            P("shard"),
            P("shard", None),
            P("shard", "rep", None),
            P("shard", "rep", None),
        ),
        check_vma=False,
    )
```

time: 1180 us -> 455 us (0.39)
  matrix products: 443 us -> 110 us
  waiting for transfers between devices: 308 us -> 71.8 us
  Pallas kernels: 0 us -> 183 us
  other arithmetic: 165 us -> 18.1 us
  blocking collectives: 101 us -> 0 us
  local copies, waits for them, and re-layouts: 89.5 us -> 24.5 us
  loops' own time: 22.2 us -> 0 us
    dot_general x41 -> x26, matrix products: 443 us -> 110 us  [the longest x3 13.1 us: local(): jnp.einsum('te,de->td', left, right, preferred_element_type=single)]
    reduce_scatter x6 -> x2, waiting for transfers between devices: 225 us -> 0.01 us  [the longest x1 0.01 us: local(): lax.psum_scatter(grad_w_in, 'rep', scatter_dimension=1, tiled=True)]
    pallas_call x0 -> x4, Pallas kernels: none -> 183 us  [the longest x1 80.8 us: reduce_all(): pl.pallas_call(reduce_kernel, out_shape=(jax.ShapeDtypeStruct((QUARTERS,)...]
    reduce_sum x8 -> x3, other arithmetic: 76.6 us -> 2.5 us  [the longest x1 2.17 us: scaled(): jnp.mean(values * values, axis=-1, keepdims=True) + norm_epsilon]
    all_gather x2 -> x0, blocking collectives: 46.2 us -> none  [the longest x1 35.4 us: local(): lax.all_gather(w_router, 'shard', axis=0, tiled=True)]
    unnamed x2 -> x0, blocking collectives: 44.5 us -> none
    eq x7 -> x0, other arithmetic: 37.4 us -> none  [the longest x6 37.4 us: bucket_bias(): buckets == bucket_id]
    all_to_all x4, waiting for transfers between devices: 43.6 us -> 71.5 us  [the longest x2 46.1 us: to_experts(): lax.all_to_all(buffer.reshape(expert_count, capacity, model_width), 'shar...]
  transfers between devices with their start and end apart: 24 -> 6, of which waited for: 13 -> 4; matrix products, arithmetic and copies ran while one was open for 38% -> 20% of each run, Pallas kernels for 0% -> 25%
where the time goes in v1:
time: 455 us; the launch traced here: 451 us
  Pallas kernels  183 us (40%)
  matrix products  110 us (24%)
  waiting for transfers between devices  71.8 us (16%)
  starting transfers between devices  28.7 us (6%)
  local copies, waits for them, and re-layouts  24.5 us (5%)
  other arithmetic  18.1 us (4%)
  between operations  15 us (3%)
    pallas_call x1, Pallas kernels, reduce_all(): pl.pallas_call(reduce_kernel, out_shape=(jax.ShapeDtypeStruct((QUARTERS,)...  80.8 us
    pallas_call x1, Pallas kernels, gather_all(): pl.pallas_call(gather_kernel, out_shape=(jax.ShapeDtypeStruct((weights.sh...  52.4 us
    all_to_all x2, waiting for transfers between devices, to_experts(): lax.all_to_all(buffer.reshape(expert_count, capacity, model_width), 'shar...  46.1 us
    pallas_call x1, Pallas kernels, attn_backward(): pl.pallas_call(attn_backward_kernel, out_shape=(jax.ShapeDtypeStruct((row...  32.9 us
    all_to_all x2, waiting for transfers between devices, from_experts(): lax.all_to_all(rows.reshape(expert_count, capacity, model_width), 'shard'...  25.4 us
    all_to_all x2, starting transfers between devices, to_experts(): lax.all_to_all(buffer.reshape(expert_count, capacity, model_width), 'shar...  19.5 us
    pallas_call x1, Pallas kernels, attn_forward(): pl.pallas_call(attn_forward_kernel, out_shape=(jax.ShapeDtypeStruct((rows...  16.6 us
    dot_general x3, matrix products, local(): jnp.einsum('te,de->td', left, right, preferred_element_type=single)  13.1 us
  transfers between devices with their start and end apart: 6, of which 4 were waited for; matrix products, arithmetic and copies ran while one was open for 20% of the time, Pallas kernels for 25%

profile of v1, /device:TPU:0, one launch (start us, length us, event | category | flops | bytes accessed | tf_op | source)
XLA Modules:
  0.0 451.0 jit_solution(15813460880930874068)
XLA Ops:
  13.8 52.4 %gather_all.1 = (bf16[4,4,2,4,24,768]{5,4,3,2,1,0:T(8,128)(2,1)}, bf16[4,2,128,768]{3,2,1,0:T(8,128)(2,1)}, bf16[256,768]{1,0:T(8,128)(2,1)}, bf16[4,2,96,128]{3,2,1,0:T(8,128)(2,1)}) custom-call(bf16[4,4,24,768]{3,2,1,0:T(8,128)(2,1)} %pad_maximum_fusion.1.w_ref, bf16[384,768]{1,0:T(8,128)(2,1)} %tok_ref.1, bf16[96,128]{1,0:T(8,128)(2,1)} %pad.23.small_ref), custom_call_target="tpu_custom_call" | custom-call | bytes 100000000 | tf_op jit(solution)/shard_map/gather_all/pallas_call | solution.py:418
  66.2 4.2 fusion.78
  74.1 5.0 %convolution_convert_fusion.3.k_ref = bf16[1536,768]{1,0:T(8,128)(2,1)} fusion(bf16[768,768]{1,0:T(8,128)(2,1)} %bitcast.103, f32[768]{0:T(1024)S(1)} %convert_reduce_fusion.1, f32[1536]{0:T(1024)S(1)} %add_rsqrt_fusion, bf16[256,768]{1,0:T(8,128)(2,1)S(1)} %slice.74, bf16[256,768]{1,0:T(8,128)(2,1)} %get-tuple-element.31, bf16[1024,768]{1,0:T(8,128)(2,1)S(1)} %bitcast.92), kind=kOutput, calls=%fused_computation.31 | convolution fusion | flops 1823735808 | bytes 5907456 | tf_op jit(solution)/shard_map/dot_general | solution.py:628
  79.1 5.4 %convolution_convert_fusion.2.v_ref = bf16[1536,768]{1,0:T(8,128)(2,1)} fusion(bf16[768,768]{1,0:T(8,128)(2,1)S(1)} %bitcast.101, f32[768]{0:T(1024)S(1)} %convert_reduce_fusion.1, f32[1536]{0:T(1024)S(1)} %add_rsqrt_fusion, bf16[256,768]{1,0:T(8,128)(2,1)S(1)} %slice.74, bf16[256,768]{1,0:T(8,128)(2,1)S(1)} %copy-done.22, bf16[1024,768]{1,0:T(8,128)(2,1)S(1)} %bitcast.93), kind=kOutput, calls=%fused_computation.30 | convolution fusion | flops 1823735808 | bytes 5907456 | tf_op jit(solution)/shard_map/dot_general | solution.py:629
  86.8 16.6 %attn_forward.1 = (f32[384,768]{1,0:T(8,128)}, f32[16,384]{1,0:T(8,128)}) custom-call(f32[16,512]{1,0:T(8,128)} %fusion.60.rev_ref, bf16[384,768]{1,0:T(8,128)(2,1)} %convolution_convert_fusion.11.q_ref, bf16[1536,768]{1,0:T(8,128)(2,1)} %convolution_convert_fusion.3.k_ref, bf16[1536,768]{1,0:T(8,128)(2,1)} %convolution_convert_fusion.2.v_ref), custom_call_target="tpu_custom_call" | custom-call | flops 20000000000 | bytes 12000000 | tf_op jit(solution)/shard_map/attn_forward/pallas_call | solution.py:174
  108.2 4.9 %all-to-all-start = ((bf16[8,96,768]{2,1,0:T(8,128)(2,1)}), bf16[8,96,768]{2,1,0:T(8,128)(2,1)}, u32[]{:S(2)}, u32[]{:S(2)}) async-start(bf16[8,96,768]{2,1,0:T(8,128)(2,1)} %bitcast.106), calls=%async_computation | async-start | bytes 2359296 | tf_op jit(solution)/shard_map/all_to_all | solution.py:646
  115.5 27.2 %all-to-all-done = bf16[8,96,768]{2,1,0:T(8,128)(2,1)} async-done(((bf16[8,96,768]{2,1,0:T(8,128)(2,1)}), bf16[8,96,768]{2,1,0:T(8,128)(2,1)}, u32[]{:S(2)}, u32[]{:S(2)}) %all-to-all-start) | async-done | bytes 1179680 | tf_op jit(solution)/shard_map/all_to_all | solution.py:646
  142.6 14.6 %all-to-all-start.2 = ((bf16[8,96,768]{2,1,0:T(8,128)(2,1)}), bf16[8,96,768]{2,1,0:T(8,128)(2,1)}, u32[]{:S(2)}, u32[]{:S(2)}) async-start(bf16[8,96,768]{2,1,0:T(8,128)(2,1)} %bitcast.107), calls=%async_computation.2 | async-start | bytes 2359296 | tf_op jit(solution)/shard_map/all_to_all | solution.py:646
  157.3 10.2 %fusion.18 = f32[768,3072]{1,0:T(8,128)} fusion(bf16[768,768]{1,0:T(8,128)(2,1)} %bitcast.16, bf16[1,768,3072]{2,1,0:T(8,128)(2,1)} %param.27), kind=kOutput, calls=%fused_computation.25 | convolution fusion | flops 3623878656 | bytes 15335424 | tf_op jit(solution)/shard_map/dot_general | solution.py:661
  167.4 18.9 %all-to-all-done.2 = bf16[8,96,768]{2,1,0:T(8,128)(2,1)} async-done(((bf16[8,96,768]{2,1,0:T(8,128)(2,1)}), bf16[8,96,768]{2,1,0:T(8,128)(2,1)}, u32[]{:S(2)}, u32[]{:S(2)}) %all-to-all-start.2) | async-done | bytes 1179680 | tf_op jit(solution)/shard_map/all_to_all | solution.py:646
  186.4 12.0 %fusion.6 = bf16[768,3072]{1,0:T(8,128)(2,1)S(1)} fusion(f32[768,3072]{1,0:T(8,128)} %fusion.18, bf16[768,768]{1,0:T(8,128)(2,1)} %bitcast.22, bf16[1,3072,768]{2,1,0:T(8,128)(2,1)} %param.28), kind=kOutput, calls=%fused_computation.8 | convolution fusion | flops 3671064576 | bytes 20054016 | tf_op jit(solution)/shard_map/sd,fd->sf/dot_general | solution.py:669
  198.4 8.9 %fusion.24 = bf16[768,768]{1,0:T(8,128)(2,1)} fusion(bf16[768,3072]{1,0:T(8,128)(2,1)S(1)} %fusion.6, bf16[1,768,3072]{2,1,0:T(8,128)(2,1)} %param.27), kind=kOutput, calls=%fused_computation.45 | convolution fusion | flops 3624468480 | bytes 10616832 | tf_op jit(solution)/shard_map/sf,df->sd/dot_general | solution.py:672
  207.3 4.3 all-to-all-start.3
  211.6 11.6 %fusion.27 = bf16[768,768]{1,0:T(8,128)(2,1)} fusion(bf16[1,3072,768]{2,1,0:T(8,128)(2,1)} %param.28, f32[768,3072]{1,0:T(8,128)} %fusion.18), kind=kOutput, calls=%fused_computation.46 | convolution fusion | flops 3645702144 | bytes 15335424 | tf_op jit(solution)/shard_map/dot_general | solution.py:665
  223.2 17.8 %all-to-all-done.3 = bf16[8,96,768]{2,1,0:T(8,128)(2,1)} async-done(((bf16[8,96,768]{2,1,0:T(8,128)(2,1)}), bf16[8,96,768]{2,1,0:T(8,128)(2,1)}, u32[]{:S(2)}, u32[]{:S(2)}) %all-to-all-start.3) | async-done | bytes 1179680 | tf_op jit(solution)/shard_map/all_to_all | solution.py:652
  241.0 4.3 all-to-all-start.1
  245.5 8.8 %fusion.20 = bf16[1,768,3072]{2,1,0:T(8,128)(2,1)} fusion(bf16[768,768]{1,0:T(8,128)(2,1)} %bitcast.16, bf16[768,3072]{1,0:T(8,128)(2,1)} %copy-done.52), kind=kOutput, calls=%fused_computation.27 | convolution fusion | flops 3626237952 | bytes 10616832 | tf_op jit(solution)/shard_map/sd,sf->df/dot_general | solution.py:675
  254.3 9.7 %fusion.21 = bf16[1,3072,768]{2,1,0:T(8,128)(2,1)} fusion(bf16[768,768]{1,0:T(8,128)(2,1)} %bitcast.22, f32[768,3072]{1,0:T(8,128)} %fusion.18), kind=kOutput, calls=%fused_computation.28 | convolution fusion | flops 3647471616 | bytes 15335424 | tf_op jit(solution)/shard_map/sf,sd->fd/dot_general | solution.py:674
  264.0 3.1 fusion.40
  267.1 7.6 %all-to-all-done.1 = bf16[8,96,768]{2,1,0:T(8,128)(2,1)} async-done(((bf16[8,96,768]{2,1,0:T(8,128)(2,1)}), bf16[8,96,768]{2,1,0:T(8,128)(2,1)}, u32[]{:S(2)}, u32[]{:S(2)}) %all-to-all-start.1) | async-done | bytes 1179680 | tf_op jit(solution)/shard_map/all_to_all | solution.py:652
  282.9 32.9 %attn_backward.1 = (bf16[384,768]{1,0:T(8,128)(2,1)}, bf16[1536,768]{1,0:T(8,128)(2,1)}, bf16[1536,768]{1,0:T(8,128)(2,1)}, f32[16,128]{1,0:T(8,128)}) custom-call(f32[16,512]{1,0:T(8,128)} %fusion.60.rev_ref, f32[512,128]{1,0:T(8,128)} %constant.42.clone.hot_ref, bf16[384,768]{1,0:T(8,128)(2,1)} %convolution_convert_fusion.11.q_ref, ...), custom_call_target="tpu_custom_call" | custom-call | flops 40000000000 | bytes 24000000 | tf_op jit(solution)/shard_map/attn_backward/pallas_call | solution.py:280
  315.9 3.9 fusion.82
  319.8 7.1 %fusion.77 = (bf16[1536,768]{1,0:T(8,128)(2,1)S(1)}, f32[768]{0:T(1024)}, f32[1536,768]{1,0:T(8,128)}) fusion(f32[1536]{0:T(1024)S(1)} %copy-done.46, bf16[256,768]{1,0:T(8,128)(2,1)S(1)} %copy-done.11, bf16[256,768]{1,0:T(8,128)(2,1)S(1)} %copy-done.23, bf16[1024,768]{1,0:T(8,128)(2,1)S(1)} %bitcast.94, f32[1536,768]{1,0:T(8,128)S(1)} %fusion.82, ...), kind=kOutput, calls=%fused_computation.125 | convolution fusion | flops 1824914688 | bytes 17703936 | tf_op jit(solution)/shard_map/te,de->td/dot_general | solution.py:698
  348.7 80.8 %reduce_all.1 = (f32[4,24,3200]{2,1,0:T(8,128)}, f32[128,768]{1,0:T(8,128)}, bf16[256,768]{1,0:T(8,128)(2,1)}) custom-call(bf16[4,2,4,24,3200]{4,3,2,1,0:T(8,128)(2,1)} %constant_dynamic-update-slice_fusion.d_ref, bf16[4,2,128,768]{3,2,1,0:T(8,128)(2,1)} %bitcast.83, bf16[256,768]{1,0:T(8,128)(2,1)} %slice.98.e_ref), custom_call_target="tpu_custom_call" | custom-call | bytes 200000000 | tf_op jit(solution)/shard_map/reduce_all/pallas_call | solution.py:534
  (181 shorter events, 63.9 us)
Async XLA Ops:
  8.4 63.4 %copy-start.42 = (f32[384]{0:T(512)}, f32[384]{0:T(512)S(1)}, u32[]{:S(2)}) copy-start(f32[384]{0:T(512)S(1)} %fusion.37) | copy-start | bytes 4612
  9.5 69.6 %copy-start.10 = (bf16[256,768]{1,0:T(8,128)(2,1)}, bf16[256,768]{1,0:T(8,128)(2,1)S(1)}, u32[]{:S(2)}) copy-start(bf16[256,768]{1,0:T(8,128)(2,1)S(1)} %slice.74) | copy-start | bytes 1179652
  70.4 14.8 %copy-start.4 = (bf16[1,4,2,4,24,768]{5,4,3,2,1,0:T(8,128)(2,1)}, bf16[1,4,2,4,24,768]{5,4,3,2,1,0:T(8,128)(2,1)S(1)}, u32[]{:S(2)}) copy-start(bf16[1,4,2,4,24,768]{5,4,3,2,1,0:T(8,128)(2,1)S(1)} %get-tuple-element.89) | copy-start | bytes 3538948
  70.4 32.9 %copy-start.1 = (bf16[1,4,2,4,24,768]{5,4,3,2,1,0:T(8,128)(2,1)}, bf16[1,4,2,4,24,768]{5,4,3,2,1,0:T(8,128)(2,1)S(1)}, u32[]{:S(2)}) copy-start(bf16[1,4,2,4,24,768]{5,4,3,2,1,0:T(8,128)(2,1)S(1)} %get-tuple-element.87) | copy-start | bytes 3538948
  71.8 13.4 %copy-start.28 = (f32[768]{0:T(1024)}, f32[768]{0:T(1024)S(1)}, u32[]{:S(2)}) copy-start(f32[768]{0:T(1024)S(1)} %convert_reduce_fusion.1) | copy-start | bytes 9220
  71.8 13.4 %copy-start.38 = (f32[384]{0:T(512)}, f32[384]{0:T(512)S(1)}, u32[]{:S(2)}) copy-start(f32[384]{0:T(512)S(1)} %fusion.68) | copy-start | bytes 4612
  79.1 5.4 %copy-start.33 = (bf16[32,512]{1,0:T(8,128)(2,1)S(1)}, bf16[32,512]{1,0:T(8,128)(2,1)}, u32[]{:S(2)}) copy-start(bf16[32,512]{1,0:T(8,128)(2,1)} %constant.41.clone) | copy-start | bytes 98308
  79.1 6.2 %copy-start = (bf16[384,768]{1,0:T(8,128)(2,1)S(1)}, bf16[384,768]{1,0:T(8,128)(2,1)}, u32[]{:S(2)}) copy-start(bf16[384,768]{1,0:T(8,128)(2,1)} %tok_ref.1) | copy-start | bytes 1769476
  106.0 170.9 %copy-start.34 = (f32[384]{0:T(512)}, f32[384]{0:T(512)S(1)}, u32[]{:S(2)}) copy-start(f32[384]{0:T(512)S(1)} %fusion.69) | copy-start | bytes 4612
  106.3 6.8 %copy-start.6 = (bf16[4,2,96,128]{3,2,1,0:T(8,128)(2,1)S(1)}, bf16[4,2,96,128]{3,2,1,0:T(8,128)(2,1)}, u32[]{:S(2)}) copy-start(bf16[4,2,96,128]{3,2,1,0:T(8,128)(2,1)} %get-tuple-element.28) | copy-start | bytes 589828
  106.3 7.1 %copy-start.31 = (s32[384]{0:T(512)S(1)}, s32[384]{0:T(512)}, u32[]{:S(2)}) copy-start(s32[384]{0:T(512)} %param.17) | copy-start | bytes 4612
  106.4 7.1 %copy-start.20 = (bf16[384,768]{1,0:T(8,128)(2,1)S(1)}, bf16[384,768]{1,0:T(8,128)(2,1)}, u32[]{:S(2)}) copy-start(bf16[384,768]{1,0:T(8,128)(2,1)} %param.29) | copy-start | bytes 1769476
  108.2 34.4 %all-to-all-start = ((bf16[8,96,768]{2,1,0:T(8,128)(2,1)}), bf16[8,96,768]{2,1,0:T(8,128)(2,1)}, u32[]{:S(2)}, u32[]{:S(2)}) async-start(bf16[8,96,768]{2,1,0:T(8,128)(2,1)} %bitcast.106), calls=%async_computation | async-start | bytes 2359296 | tf_op jit(solution)/shard_map/all_to_all | solution.py:646
  113.4 163.5 %copy-start.26 = (f32[384]{0:T(512)}, f32[384]{0:T(512)S(1)}, u32[]{:S(2)}) copy-start(f32[384]{0:T(512)S(1)} %get-tuple-element.100) | copy-start | bytes 4612
  113.5 163.4 %copy-start.32 = (f32[384]{0:T(512)}, f32[384]{0:T(512)S(1)}, u32[]{:S(2)}) copy-start(f32[384]{0:T(512)S(1)} %fusion.59) | copy-start | bytes 4612
  113.5 163.3 %copy-start.40 = (f32[384]{0:T(512)}, f32[384]{0:T(512)S(1)}, u32[]{:S(2)}) copy-start(f32[384]{0:T(512)S(1)} %select_reduce_fusion) | copy-start | bytes 4612
  142.6 43.8 %all-to-all-start.2 = ((bf16[8,96,768]{2,1,0:T(8,128)(2,1)}), bf16[8,96,768]{2,1,0:T(8,128)(2,1)}, u32[]{:S(2)}, u32[]{:S(2)}) async-start(bf16[8,96,768]{2,1,0:T(8,128)(2,1)} %bitcast.107), calls=%async_computation.2 | async-start | bytes 2359296 | tf_op jit(solution)/shard_map/all_to_all | solution.py:646
  198.4 8.9 %copy-start.52 = (bf16[768,3072]{1,0:T(8,128)(2,1)}, bf16[768,3072]{1,0:T(8,128)(2,1)S(1)}, u32[]{:S(2)}) copy-start(bf16[768,3072]{1,0:T(8,128)(2,1)S(1)} %fusion.6) | copy-start | bytes 14155780
  207.3 33.7 %all-to-all-start.3 = ((bf16[8,96,768]{2,1,0:T(8,128)(2,1)}), bf16[8,96,768]{2,1,0:T(8,128)(2,1)}, u32[]{:S(2)}, u32[]{:S(2)}) async-start(bf16[8,96,768]{2,1,0:T(8,128)(2,1)} %bitcast.109), calls=%async_computation.3 | async-start | bytes 2359296 | tf_op jit(solution)/shard_map/all_to_all | solution.py:652
  241.0 33.7 %all-to-all-start.1 = ((bf16[8,96,768]{2,1,0:T(8,128)(2,1)}), bf16[8,96,768]{2,1,0:T(8,128)(2,1)}, u32[]{:S(2)}, u32[]{:S(2)}) async-start(bf16[8,96,768]{2,1,0:T(8,128)(2,1)} %bitcast.105), calls=%async_computation.1 | async-start | bytes 2359296 | tf_op jit(solution)/shard_map/all_to_all | solution.py:652
  245.3 192.9 %reduce-scatter.3.cloned.1.call-start = ((), (), s32[]{:S(2)}) async-start(), calls=%async_computation.6 | async-start | bytes 5898240 | tf_op jit(solution)/shard_map/reduce_scatter | solution.py:692
  282.1 159.0 %reduce-scatter.5.cloned.1.call-start = ((), (), s32[]{:S(2)}) async-start(), calls=%async_computation.7 | async-start | bytes 5898240 | tf_op jit(solution)/shard_map/reduce_scatter | solution.py:693
  282.9 32.9 %copy-start.17 = (bf16[1,4,2,4,24,768]{5,4,3,2,1,0:T(8,128)(2,1)S(1)}, bf16[1,4,2,4,24,768]{5,4,3,2,1,0:T(8,128)(2,1)}, u32[]{:S(2)}) copy-start(bf16[1,4,2,4,24,768]{5,4,3,2,1,0:T(8,128)(2,1)} %get-tuple-element.88) | copy-start | bytes 3538948
  429.5 5.9 %copy-start.13 = (f32[128,768]{1,0:T(8,128)S(1)}, f32[128,768]{1,0:T(8,128)}, u32[]{:S(2)}) copy-start(f32[128,768]{1,0:T(8,128)} %get-tuple-element.39) | copy-start | bytes 1179652
  (36 other events, 107.6 us)
Sparse Core Ops, SparseCore 0:
  282.2 55.0 reduce-scatter.2
  340.3 88.8 reduce-scatter.4

commit v2 on v1

v2 whole, which is shorter than its diff:
```python
import jax
import jax.numpy as jnp
import numpy as np
from jax import lax
from jax.experimental import pallas as pl
from jax.experimental.pallas import tpu as pltpu
from jax.sharding import PartitionSpec as P

PR_DEV = 128
TILE = 128
SPAN = 2 * TILE
QUARTERS = 4
far_before, far_after, causal_tile, hidden_tile, tile_kinds = 3, 4, 5, 6, 7
vmem_cap = 60 * 1024 * 1024
mesh_ids = pl.DeviceIdType.MESH
bucket_edges = (12, 16, 23, 32, 46, 64, 91)
norm_epsilon = 1e-06
masked_score = -1e30
low, single = jnp.bfloat16, jnp.float32
in_vmem = pl.BlockSpec(memory_space=pltpu.VMEM)
anywhere = pl.BlockSpec(memory_space=pl.ANY)


def inverse_rms(values):
    return lax.rsqrt(jnp.mean(values * values, axis=-1, keepdims=True) + norm_epsilon)


def norm_pull(grad, values, gain):
    scale = inverse_rms(values)
    pulled = grad * gain
    mean = jnp.mean(pulled * values, axis=-1, keepdims=True)
    return scale * pulled - values * (scale * scale * scale * mean)


def nt(left, right):
    return lax.dot_general(left, right, (((1,), (1,)), ((), ())), preferred_element_type=single)


def tn(left, right):
    return lax.dot_general(left, right, (((0,), (0,)), ((), ())), preferred_element_type=single)


def nn(left, right):
    return jnp.dot(left, right, preferred_element_type=single)


def thirds_of(values):
    first = values.astype(low)
    rest = values - first.astype(single)
    second = rest.astype(low)
    return first, second, (rest - second.astype(single)).astype(low)


def fill_tiles(tiles_ref, rev_row, low, high):
    spread = jnp.broadcast_to(rev_row, (TILE, 4 * TILE))
    rolled = pltpu.roll(spread, 0, 1, stride=1, stride_axis=0)
    keys = lax.broadcasted_iota(jnp.int32, (TILE, TILE), 0)
    rows = lax.broadcasted_iota(jnp.int32, (TILE, TILE), 1)
    tiles_ref[0] = rolled[:, TILE : 2 * TILE]
    tiles_ref[1] = rolled[:, :TILE]
    tiles_ref[2] = rolled[:, 3 * TILE :]
    tiles_ref[far_before] = jnp.broadcast_to(low, (TILE, TILE))
    tiles_ref[far_after] = jnp.broadcast_to(high, (TILE, TILE))
    tiles_ref[causal_tile] = jnp.where(keys <= rows, rolled[:, :TILE], masked_score)
    tiles_ref[hidden_tile] = jnp.full((TILE, TILE), masked_score, jnp.float32)


def prompt_tile(block, chunk, shard_id, block_count):
    if chunk == 0:
        gap = block - shard_id
        far = jnp.where(gap < 0, far_before, far_after)
        return jnp.where(jnp.abs(gap) <= 1, gap + 1, far)
    if chunk == 1 and block == block_count - 1:
        return jnp.where(shard_id % 2 == 0, 0, far_before)
    return far_before


def local_tile(block, chunk, shard_id):
    if block >= 2:
        return ((causal_tile, 0), (hidden_tile, causal_tile))[block - 2][chunk]
    kind = 0 if (block, chunk) == (1, 0) else far_before
    return jnp.where(shard_id % 2 == 1, kind, hidden_tile)


def prompt_grid(part, shard_id, block_count):
    return [
        [prompt_tile(2 * part + half, chunk, shard_id, block_count) for chunk in range(3)]
        for half in range(2)
    ]


def local_grid(part, shard_id):
    return [[local_tile(2 * part + half, chunk, shard_id) for chunk in range(2)] for half in range(2)]


def with_bias(scores, tiles_ref, grid):
    return jnp.concatenate(
        [
            jnp.concatenate(
                [
                    scores[i * TILE : (i + 1) * TILE, j * TILE : (j + 1) * TILE] + tiles_ref[kind]
                    for j, kind in enumerate(row)
                ],
                axis=1,
            )
            for i, row in enumerate(grid)
        ],
        axis=0,
    )


def fold8(values):
    return values.reshape(values.shape[0] // 8, 8, values.shape[1])


def head_mask(rows, side):
    lanes = lax.broadcasted_iota(jnp.int32, (rows, TILE), 1)
    return (lanes < TILE // 2) if side == 0 else (lanes >= TILE // 2)


def distance_buckets(bucket_count):
    steps = np.arange(4 * TILE)
    gap = -np.where(steps < 2 * TILE, steps, steps - 4 * TILE)
    size = np.abs(gap)
    far = sum((size >= edge).astype(np.int64) for edge in bucket_edges)
    exact = bucket_count // 4
    return np.where(gap > 0, bucket_count // 2, 0) + np.where(size < exact, size, exact + far)


def front_kernel(
    every_ref, tok_ref, w_ref, small_ref, bucket_ref, route_ref, row_ref, cot_ref,
    n_ref, q_ref, k_ref, v_ref, o_ref, lse_ref, rev_ref, mid_ref, gate_ref, gain_ref, x_ref, gin_ref,
    tiles, vt, sp, sl, ot, gbuf, gs, gr, loc,
):
    shard_id = lax.axis_index("shard")
    shards = lax.axis_size("shard")
    rows, width = tok_ref.shape
    experts = shards
    blocks = every_ref.shape[0] // TILE - 4
    half = TILE // 2
    heads_held = rev_ref.shape[0]

    rep = lax.axis_index("rep")
    others = [(rep, (shard_id + k) % shards) for k in range(1, shards)]
    slots = lax.broadcasted_iota(jnp.int32, (x_ref.shape[0], rows), 0)
    place = (slots == row_ref[0:1, :]).astype(low)
    gbuf[...] = nn(place, cot_ref[...]).astype(low).reshape(gbuf.shape)
    greet(others)
    mine = pltpu.make_async_copy(gbuf.at[shard_id], gin_ref.at[shard_id], loc)
    mine.start()
    sent = [
        send(gbuf.at[device[1]], gin_ref.at[shard_id], (gs.at[k], gr.at[k]), device)
        for k, device in enumerate(others)
    ]
    for copy in sent:
        copy.start()

    small_t = small_ref[...].astype(single).T
    gain_attn = small_t[experts : experts + 1]
    gain_moe = small_t[experts + 1 : experts + 2]
    gain_ref[...] = jnp.concatenate([gain_attn, gain_moe, jnp.zeros((6, width), single)], axis=0)
    shard_rows = width // shards
    table_rows = 2 * TILE // 8 // shards
    owner = lax.broadcasted_iota(jnp.int32, (shards, shard_rows, 4 * TILE), 0)
    offset = lax.broadcasted_iota(jnp.int32, (shards, shard_rows, 4 * TILE), 1)
    held = jnp.where(offset < table_rows, owner * table_rows + offset, -1).reshape(width, 4 * TILE)
    hot = (held == bucket_ref[0:1, :]).astype(low)
    table_t = small_t[experts + 2 : experts + 2 + heads_held].astype(low)
    rev_ref[...] = nn(table_t, hot)

    @pl.loop(0, every_ref.shape[0] // SPAN)
    def project(part):
        span = pl.ds(pl.multiple_of(part * SPAN, SPAN), SPAN)
        values = every_ref[span, :].astype(single)
        normed = (values * inverse_rms(values) * gain_attn).astype(low)
        n_ref[span, :] = normed
        k_ref[span, :] = nn(normed, w_ref[1]).astype(low)
        v_ref[span, :] = nn(normed, w_ref[2]).astype(low)

    own = pl.ds(pl.multiple_of(shard_id * TILE, TILE), TILE)
    normed = jnp.concatenate([n_ref[own, :], n_ref[(blocks + 2) * TILE :, :]], axis=0)
    q_ref[...] = (nn(normed, w_ref[0]).astype(low) * jnp.asarray(0.125, low)).astype(low)

    @pl.loop(0, width // TILE)
    def pair_loop(pair):
        cols = pl.ds(pl.multiple_of(pair * TILE, TILE), TILE)
        vt[...] = v_ref[:, cols].T
        q_pair = q_ref[:, cols]
        for side in range(2):
            head = pair * 2 + side
            rev_row = rev_ref[pl.ds(head, 1), :]
            fill_tiles(tiles, rev_row, rev_row[:, SPAN - 1 : SPAN], rev_row[:, SPAN : SPAN + 1])
            q_head = jnp.where(head_mask(rows, side), q_pair, jnp.zeros_like(q_pair))
            top = jnp.full((8, rows), masked_score, single)
            for part in range(blocks // 2):
                keys = slice(part * SPAN, (part + 1) * SPAN)
                scores = with_bias(nt(k_ref[keys, cols], q_head), tiles, prompt_grid(part, shard_id, blocks))
                sp[keys, :] = scores
                top = jnp.maximum(top, jnp.max(fold8(scores), axis=0))
            top_local = top[:, PR_DEV:]
            for part in range(2):
                keys = slice(part * SPAN, (part + 1) * SPAN)
                held = slice((blocks // 2 + part) * SPAN, (blocks // 2 + part + 1) * SPAN)
                scores = with_bias(nt(k_ref[held, cols], q_head[PR_DEV:]), tiles, local_grid(part, shard_id))
                sl[keys, :] = scores
                top_local = jnp.maximum(top_local, jnp.max(fold8(scores), axis=0))
            top = jnp.max(jnp.concatenate([top[:, :PR_DEV], top_local], axis=1), axis=0, keepdims=True)
            total = jnp.zeros((8, rows), single)
            summed = jnp.zeros((half, rows), single)
            heads = slice(side * half, (side + 1) * half)
            for part in range(blocks // 2):
                keys = slice(part * SPAN, (part + 1) * SPAN)
                weights = jnp.exp(sp[keys, :] - top)
                total = total + jnp.sum(fold8(weights), axis=0)
                summed = summed + nn(vt[heads, keys], weights.astype(low))
            top_c = top[:, PR_DEV:]
            total_c = total[:, PR_DEV:]
            summed_c = summed[:, PR_DEV:]
            for part in range(2):
                keys = slice(part * SPAN, (part + 1) * SPAN)
                held = slice((blocks // 2 + part) * SPAN, (blocks // 2 + part + 1) * SPAN)
                weights = jnp.exp(sl[keys, :] - top_c)
                total_c = total_c + jnp.sum(fold8(weights), axis=0)
                summed_c = summed_c + nn(vt[heads, held], weights.astype(low))
            total = jnp.sum(jnp.concatenate([total[:, :PR_DEV], total_c], axis=1), axis=0, keepdims=True)
            summed = jnp.concatenate([summed[:, :PR_DEV], summed_c], axis=1)
            ot[heads, :] = summed / total
            lse_ref[pl.ds(head, 1), :] = top + jnp.log(total)
        o_ref[:, cols] = ot[...].T

    resid_mid = tok_ref[...].astype(single) + nn(o_ref[...].astype(low), w_ref[3])
    mid_ref[...] = resid_mid
    mid_low = (resid_mid * inverse_rms(resid_mid) * gain_moe).astype(low)
    probs = router_softmax(mid_low, small_ref[...], experts)
    lanes = lax.broadcasted_iota(jnp.int32, probs.shape, 1)
    gate = jnp.sum(jnp.where(lanes == route_ref[...], probs, 0.0), axis=1, keepdims=True)
    gate_ref[...] = jnp.broadcast_to(gate, gate_ref.shape)
    x_ref[...] = nn(place, mid_low).astype(low)
    mine.wait()
    for k in range(shards - 1):
        piece = gin_ref.at[(shard_id + shards - k - 1) % shards]
        send(piece, piece, (gs.at[k], gr.at[k]), others[0]).wait_recv()
    for copy in sent:
        copy.wait_send()


def router_softmax(rows_low, small, experts):
    logits = nn(rows_low, small)
    lanes = lax.broadcasted_iota(jnp.int32, logits.shape, 1)
    logits = jnp.where(lanes < experts, logits, masked_score)
    powers = jnp.exp(logits - jnp.max(logits, axis=1, keepdims=True))
    return powers / jnp.sum(powers, axis=1, keepdims=True)


def front(every_tok, tokens, weights, small, bucket_row, route_col, row_slots, cotangent, slot_count):
    rows, width = tokens.shape
    keys = every_tok.shape[0]
    shards = lax.axis_size("shard")
    shape = jax.ShapeDtypeStruct
    return pl.pallas_call(
        front_kernel,
        out_shape=(
            shape((keys, width), low), shape((rows, width), low), shape((keys, width), low),
            shape((keys, width), low), shape((rows, width), single), shape((16, rows), single),
            shape((16, 4 * TILE), single), shape((rows, width), single), shape((rows, TILE), single),
            shape((8, width), single), shape((slot_count, width), low),
            shape((shards, slot_count // shards, width), low),
        ),
        in_specs=[in_vmem] * 8,
        out_specs=(in_vmem,) * 11 + (anywhere,),
        scratch_shapes=[
            pltpu.VMEM((tile_kinds, TILE, TILE), single),
            pltpu.VMEM((TILE, keys), low),
            pltpu.VMEM((keys - 2 * SPAN, rows), single),
            pltpu.VMEM((2 * SPAN, rows - TILE), single),
            pltpu.VMEM((TILE, rows), single),
            pltpu.VMEM((shards, slot_count // shards, width), low),
            pltpu.SemaphoreType.DMA((shards - 1,)), pltpu.SemaphoreType.DMA((shards - 1,)), pltpu.SemaphoreType.DMA,
        ],
        compiler_params=pltpu.CompilerParams(collective_id=2, has_side_effects=True, vmem_limit_bytes=vmem_cap),
        cost_estimate=pl.CostEstimate(flops=30_000_000_000, bytes_accessed=20_000_000, transcendentals=8_000_000),
        name="front",
    )(every_tok, tokens, weights, small, bucket_row, route_col, row_slots, cotangent)


def moe_kernel(
    x_ref, g_ref, small_ref, w_in_ref, w_out_ref,
    back_ref, out_ref, gwin_ref, gwout_ref, rg_ref,
    w_in, w_out, xin, gm, gg, hid, gpre, acc, gacc, logit_grads, x_t, gwin, gwout,
    xs, xr, ms, mr, ws, ls, os_in, os_out,
):
    rep, chip, core, chips, quarter = places()
    experts = chips * 2
    here = chip * 2 + core
    pair_rows = acc.shape[0]
    cap = pair_rows // 2
    hidden = w_in_ref.shape[1]
    block = 512
    loads = [
        pltpu.make_async_copy(w_in_ref, w_in, ws.at[0]),
        pltpu.make_async_copy(w_out_ref, w_out, ws.at[1]),
    ]
    for copy in loads:
        copy.start()
    twin = (rep, chip * 2 + 1 - core)
    targets = [
        (k, side, (rep, (chip + k) % chips * 2 + side)) for k in range(1, chips) for side in range(2)
    ]
    greet([twin] + [device for _, _, device in targets])
    sent = [send(x_ref.at[chip, 1 - core], xin.at[chip, core], (xs.at[0, 0], xr.at[0, core]), twin)]
    for k, side, device in targets:
        sent.append(
            send(x_ref.at[(chip + k) % chips, side], xin.at[chip, core], (xs.at[k, side], xr.at[k, core]), device)
        )
    for copy in sent:
        copy.start()
    xin[chip, core] = x_ref[chip, core]
    for copy in loads:
        copy.wait()

    def arrived(k, source, side):
        piece = xin.at[source, side]
        send(piece, piece, (xs.at[0, 0], xr.at[k, side]), twin).wait_recv()

    @pl.loop(0, chips)
    def chunk(k):
        source = (chip + chips - k) % chips

        @pl.when(k == 0)
        def _():
            arrived(0, chip, 1 - core)

        @pl.when(k > 0)
        def _():
            for side in range(2):
                arrived(k, source, side)

        rows = xin[source].reshape(pair_rows, xin.shape[3])
        grads = g_ref[source].reshape(pair_rows, xin.shape[3])
        probs = router_softmax(rows, small_ref[...], experts)
        lanes = lax.broadcasted_iota(jnp.int32, probs.shape, 1)
        gate = jnp.sum(jnp.where(lanes == here, probs, 0.0), axis=1, keepdims=True)
        gated = (gate * grads.astype(single)).astype(low)
        span = pl.ds(pl.multiple_of(source * pair_rows, pair_rows), pair_rows)
        gg[span, :] = gated
        acc[...] = jnp.zeros_like(acc)
        gacc[...] = jnp.zeros_like(gacc)

        @pl.loop(0, hidden // block)
        def strip(part):
            cols = pl.ds(pl.multiple_of(part * block, block), block)
            pre = nn(rows, w_in[:, cols])
            grad_hidden = nt(gated, w_out[cols, :])
            square = pre * pre
            wave = jnp.tanh(0.7978845608028654 * pre * (1.0 + 0.044715 * square))
            left = 0.5 + 0.5 * wave
            active = (pre * left).astype(low)
            slope = left + (0.5 * pre) * (1.0 - wave * wave) * (
                0.7978845608028654 + 0.10703222440890037 * square
            )
            grad_pre = (grad_hidden * slope).astype(low)
            hid[span, cols] = active
            gpre[span, cols] = grad_pre
            acc[...] += nn(active, w_out[cols, :])
            gacc[...] += nt(grad_pre, w_in[:, cols])

        out = acc[...].astype(low)
        out_ref[source] = out.reshape(out_ref.shape[1:])
        grad_gate = jnp.sum(grads.astype(single) * out.astype(single), axis=1, keepdims=True)
        chosen = jnp.where(lanes == here, 1.0, 0.0)
        grad_logits = jnp.where(lanes < experts, gate * grad_gate * (chosen - probs), 0.0)
        logit_grads[span, :] = grad_logits
        router = small_ref[...]
        total = gacc[...] + sum(nt(part, router) for part in thirds_of(grad_logits))
        gm[source] = total.astype(low).reshape(gm.shape[1:])

        def reply(side, slot):
            return send(
                gm.at[source, side], back_ref.at[chip, core], (ms.at[k, slot], mr.at[k, core]), (rep, source * 2 + side)
            )

        @pl.when(k == 0)
        def _():
            reply(1 - core, 0).start()
            pltpu.make_async_copy(gm.at[chip, core], back_ref.at[chip, core], ls).start()

        @pl.when(k > 0)
        def _():
            for side in range(2):
                reply(side, side).start()

    every = xin[...].reshape(gg.shape)
    x_t[...] = every.T
    writes = []
    for part in range(hidden // block):
        cols = slice(part * block, (part + 1) * block)
        gwin[:, cols] = nn(x_t[...], gpre[:, cols]).astype(low)
        writes.append(pltpu.make_async_copy(gwin.at[:, cols], gwin_ref.at[:, cols], os_in.at[part]))
        writes[-1].start()
        gwout[cols, :] = tn(hid[:, cols], gg[...]).astype(low)
        writes.append(pltpu.make_async_copy(gwout.at[cols], gwout_ref.at[cols], os_out.at[part]))
        writes[-1].start()
    rg_ref[...] = sum(nn(x_t[...], part) for part in thirds_of(logit_grads[...]))
    pltpu.make_async_copy(gm.at[chip, core], back_ref.at[chip, core], ls).wait()

    def replied(k, source, side):
        piece = back_ref.at[source, side]
        send(piece, piece, (ms.at[0, 0], mr.at[k, side]), twin).wait_recv()

    replied(0, chip, 1 - core)
    for k in range(1, chips):
        for side in range(2):
            replied(k, (chip + k) % chips, side)
    for copy in sent:
        copy.wait_send()
    for copy in writes:
        copy.wait()
    send(gm.at[chip, 0], back_ref.at[chip, core], (ms.at[0, 0], mr.at[0, 0]), twin).wait_send()
    for k in range(1, chips):
        for side in range(2):
            send(gm.at[chip, 0], back_ref.at[chip, core], (ms.at[k, side], mr.at[0, 0]), twin).wait_send()


def moe(rows_out, grad_in, small, w_in, w_out):
    chips, _, cap, width = rows_out.shape
    slots = chips * 2 * cap
    hidden = w_in.shape[1]
    shape = jax.ShapeDtypeStruct
    pairs = pltpu.SemaphoreType.DMA
    strips = hidden // 512
    return pl.pallas_call(
        moe_kernel,
        out_shape=(
            shape(rows_out.shape, low), shape(rows_out.shape, low), shape((width, hidden), low),
            shape((hidden, width), low), shape((width, TILE), single),
        ),
        in_specs=[in_vmem] * 3 + [anywhere] * 2,
        out_specs=(anywhere, in_vmem, anywhere, anywhere, in_vmem),
        scratch_shapes=[
            pltpu.VMEM((width, hidden), low), pltpu.VMEM((hidden, width), low),
            pltpu.VMEM(rows_out.shape, low), pltpu.VMEM(rows_out.shape, low), pltpu.VMEM((slots, width), low),
            pltpu.VMEM((slots, hidden), low), pltpu.VMEM((slots, hidden), low),
            pltpu.VMEM((2 * cap, width), single), pltpu.VMEM((2 * cap, width), single), pltpu.VMEM((slots, TILE), single),
            pltpu.VMEM((width, slots), low), pltpu.VMEM((width, hidden), low), pltpu.VMEM((hidden, width), low),
            pairs((chips, 2)), pairs((chips, 2)), pairs((chips, 2)), pairs((chips, 2)), pairs((2,)), pairs,
            pairs((strips,)), pairs((strips,)),
        ],
        compiler_params=pltpu.CompilerParams(collective_id=3, has_side_effects=True, vmem_limit_bytes=vmem_cap),
        cost_estimate=pl.CostEstimate(flops=40_000_000_000, bytes_accessed=40_000_000, transcendentals=3_000_000),
        name="moe",
    )(rows_out, grad_in, small, w_in, w_out)


def back_kernel(
    back_ref, col_ref, mid_ref, cot_ref, gain_ref, every_ref, w_ref, n_ref, q_ref, k_ref, v_ref, o_ref,
    lse_ref, rev_ref, bucket_ref, rg_ref,
    dense_ref, p_ref, e_ref, own_ref, gres_ref,
    tiles, sums, diag, kt, dqt, far_sums, dk_sum, dv_sum, g_ref, dq_ref, dk_ref, dv_ref, attn_gain,
):
    shard_id = lax.axis_index("shard")
    shards = lax.axis_size("shard")
    rows, width = mid_ref.shape
    blocks = k_ref.shape[0] // TILE - 4
    half = TILE // 2
    experts = shards
    heads_held = rev_ref.shape[0]
    diag[...] = jnp.zeros_like(diag)
    far_sums[...] = jnp.zeros_like(far_sums)
    tile_rows = lax.broadcasted_iota(jnp.int32, (TILE, TILE), 0)
    tile_cols = lax.broadcasted_iota(jnp.int32, (TILE, TILE), 1)
    flip = (tile_rows + tile_cols == TILE - 1).astype(single)

    slots = lax.broadcasted_iota(jnp.int32, (rows, back_ref.shape[0]), 1)
    grad_mid = nn((slots == col_ref[...]).astype(low), back_ref[...])
    resid_mid = mid_ref[...]
    grad_gain_moe = jnp.sum(grad_mid * resid_mid * inverse_rms(resid_mid), axis=0, keepdims=True)
    grad_resid = cot_ref[...].astype(single) + norm_pull(grad_mid, resid_mid, gain_ref[1:2, :])
    gres_ref[...] = grad_resid
    grad_attn = grad_resid.astype(low)
    g_ref[...] = nt(grad_attn, w_ref[3]).astype(low)
    dense_ref[:, 3 * width : 4 * width] = tn(o_ref[...].astype(low), grad_attn).astype(low)

    @pl.loop(0, width // TILE)
    def pair_loop(pair):
        cols = pl.ds(pl.multiple_of(pair * TILE, TILE), TILE)
        kt[...] = k_ref[:, cols].T
        q_pair = q_ref[:, cols]
        g_pair = g_ref[:, cols]
        delta_t = (g_pair.astype(single) * o_ref[:, cols]).T
        for side in range(2):
            head = pair * 2 + side
            heads = slice(side * half, (side + 1) * half)
            rev_row = rev_ref[pl.ds(head, 1), :]
            fill_tiles(tiles, rev_row, rev_row[:, SPAN - 1 : SPAN], rev_row[:, SPAN : SPAN + 1])
            sums[...] = jnp.zeros_like(sums)
            mask = head_mask(rows, side)
            q_head = jnp.where(mask, q_pair, jnp.zeros_like(q_pair))
            g_head = jnp.where(mask, g_pair, jnp.zeros_like(g_pair))
            delta = jnp.sum(delta_t[heads, :], axis=0, keepdims=True)
            log_total = lse_ref[pl.ds(head, 1), :]

            def block_grads(part, first, grid):
                keys = slice(part * SPAN, (part + 1) * SPAN)
                q_rows, g_rows = q_head[first:], g_head[first:]
                scores = with_bias(nt(k_ref[keys, cols], q_rows), tiles, grid)
                weights = jnp.exp(scores - log_total[:, first:])
                grad_weights = nt(v_ref[keys, cols], g_rows)
                grad_scores = weights * (grad_weights - delta[:, first:])
                for i, row in enumerate(grid):
                    for j, kind in enumerate(row):
                        sums[kind] += grad_scores[i * TILE : (i + 1) * TILE, j * TILE : (j + 1) * TILE]
                raw = grad_scores.astype(low)
                dk = nn(raw, q_rows)
                dv = nn(weights.astype(low), g_rows)
                if side == 0:
                    dk_sum[keys, :] = dk
                    dv_sum[keys, :] = dv
                else:
                    dk_ref[keys, cols] = (dk_sum[keys, :] + dk).astype(low)
                    dv_ref[keys, cols] = (dv_sum[keys, :] + dv).astype(low)
                return nn(kt[heads, keys], raw)

            dq = jnp.zeros((half, rows), single)
            for part in range(blocks // 2):
                dq = dq + block_grads(part, 0, prompt_grid(part, shard_id, blocks))
            dq_c = dq[:, PR_DEV:]
            for part in range(2):
                dq_c = dq_c + block_grads(blocks // 2 + part, PR_DEV, local_grid(part, shard_id))
            dqt[heads, :] = jnp.concatenate([dq[:, :PR_DEV], dq_c], axis=1)
            near = jnp.concatenate(
                [sums[1] + sums[causal_tile], sums[0], jnp.zeros((TILE, TILE), single), sums[2]], axis=1
            )
            flipped = jnp.dot(flip, near, precision=lax.Precision.HIGHEST, preferred_element_type=single)
            rolled = pltpu.roll(flipped, 3 * TILE + 1, 1, stride=1, stride_axis=0)
            diag[pl.ds(head, 1), :] = jnp.sum(rolled, axis=0, keepdims=True)
            far_sums[pl.ds(head, 1), :] = jnp.concatenate(
                [jnp.sum(sums[far_before], axis=0, keepdims=True), jnp.sum(sums[far_after], axis=0, keepdims=True)],
                axis=1,
            )
        dq_ref[:, cols] = (dqt[...].T * 0.125).astype(low)

    lanes = lax.broadcasted_iota(jnp.int32, (heads_held, 4 * TILE), 1)
    before = jnp.sum(far_sums[:, :TILE], axis=1, keepdims=True)
    after = jnp.sum(far_sums[:, TILE:], axis=1, keepdims=True)
    by_gap = diag[...] + jnp.where(lanes == SPAN - 1, before, 0.0) + jnp.where(lanes == SPAN, after, 0.0)
    shard_rows = width // shards
    table_rows = 2 * TILE // 8 // shards
    owner = lax.broadcasted_iota(jnp.int32, (shards, shard_rows, 4 * TILE), 0)
    offset = lax.broadcasted_iota(jnp.int32, (shards, shard_rows, 4 * TILE), 1)
    held = jnp.where(offset < table_rows, owner * table_rows + offset, -1).reshape(width, 4 * TILE)
    hot = (held == bucket_ref[0:1, :]).astype(low)
    grad_table = sum(nt(part, hot) for part in thirds_of(by_gap))

    attn_gain[...] = jnp.zeros_like(attn_gain)
    own = pl.ds(pl.multiple_of(shard_id * TILE, TILE), TILE)
    tail = slice((blocks + 2) * TILE, (blocks + 4) * TILE)
    normed = jnp.concatenate([n_ref[own, :], n_ref[tail, :]], axis=0)
    dense_ref[:, :width] = tn(normed, dq_ref[...]).astype(low)
    grad_own = nt(dq_ref[...], w_ref[0])
    values = jnp.concatenate([every_ref[own, :], every_ref[tail, :]], axis=0).astype(single)
    attn_gain[...] += jnp.sum(fold8(grad_own * (values * inverse_rms(values))), axis=0)
    own_ref[...] = grad_own

    def pull_rows(part):
        span = pl.ds(pl.multiple_of(part * SPAN, SPAN), SPAN)
        values = every_ref[span, :].astype(single)
        grads = nt(dk_ref[span, :], w_ref[1]) + nt(dv_ref[span, :], w_ref[2])
        attn_gain[...] += jnp.sum(fold8(grads * (values * inverse_rms(values))), axis=0)
        return grads

    @pl.loop(0, blocks // 2)
    def pull_prompt(part):
        p_ref[pl.ds(pl.multiple_of(part * SPAN, SPAN), SPAN), :] = pull_rows(part).astype(low)

    e_ref[...] = pull_rows(blocks // 2).astype(low)
    own_ref[PR_DEV:, :] += pull_rows(blocks // 2 + 1)

    @pl.loop(0, width // SPAN)
    def outer(part):
        cols = pl.ds(pl.multiple_of(part * SPAN, SPAN), SPAN)
        k_cols = pl.ds(pl.multiple_of(width + part * SPAN, SPAN), SPAN)
        v_cols = pl.ds(pl.multiple_of(2 * width + part * SPAN, SPAN), SPAN)
        dense_ref[:, k_cols] = tn(n_ref[...], dk_ref[:, cols]).astype(low)
        dense_ref[:, v_cols] = tn(n_ref[...], dv_ref[:, cols]).astype(low)

    small_t = jnp.concatenate(
        [
            jnp.zeros((experts, width), single), jnp.sum(attn_gain[...], axis=0, keepdims=True), grad_gain_moe,
            grad_table, jnp.zeros((TILE - experts - 2 - heads_held, width), single),
        ],
        axis=0,
    )
    dense_ref[:, 4 * width :] = (small_t.T + rg_ref[...]).astype(low)


def back(returned, col_slots, mid, cotangent, gains, every_tok, weights, kept, bucket_row, router_grads):
    rows, width = mid.shape
    normed, queries, keys, values, attended, lse, rev = kept
    count = keys.shape[0]
    shape = jax.ShapeDtypeStruct
    args = (
        returned, col_slots, mid, cotangent, gains, every_tok, weights, normed, queries, keys, values, attended,
        lse, rev, bucket_row, router_grads,
    )
    return pl.pallas_call(
        back_kernel,
        out_shape=(
            shape((width, 4 * width + TILE), low), shape((count - 2 * SPAN, width), low), shape((SPAN, width), low),
            shape((rows, width), single), shape((rows, width), single),
        ),
        in_specs=[in_vmem] * len(args),
        out_specs=(in_vmem,) * 5,
        scratch_shapes=[
            pltpu.VMEM((tile_kinds, TILE, TILE), single), pltpu.VMEM((tile_kinds, TILE, TILE), single),
            pltpu.VMEM((16, 4 * TILE), single), pltpu.VMEM((TILE, count), low), pltpu.VMEM((TILE, rows), single),
            pltpu.VMEM((16, 2 * TILE), single), pltpu.VMEM((count, TILE), single), pltpu.VMEM((count, TILE), single),
            pltpu.VMEM((rows, width), low), pltpu.VMEM((rows, width), low), pltpu.VMEM((count, width), low),
            pltpu.VMEM((count, width), low), pltpu.VMEM((8, width), single),
        ],
        compiler_params=pltpu.CompilerParams(vmem_limit_bytes=vmem_cap),
        cost_estimate=pl.CostEstimate(flops=60_000_000_000, bytes_accessed=40_000_000, transcendentals=8_000_000),
        name="back",
    )(*args)


def places():
    rep, shard = lax.axis_index("rep"), lax.axis_index("shard")
    return rep, shard // 2, shard % 2, lax.axis_size("shard") // 2, rep % QUARTERS


def peer_lists():
    rep, chip, core, chips, quarter = places()
    along = [(rep, (chip + k) % chips * 2 + core) for k in range(1, chips)]
    across = [(rep - quarter + (quarter + j) % QUARTERS, chip * 2 + core) for j in range(1, QUARTERS)]
    twin = (rep, chip * 2 + 1 - core)
    return along, across, twin


def greet(devices):
    barrier = pltpu.get_barrier_semaphore()
    for device in devices:
        pl.semaphore_signal(barrier, inc=1, device_id=device, device_id_type=mesh_ids)
    pl.semaphore_wait(barrier, len(devices))


def send(source, target, sems, device):
    return pltpu.make_async_remote_copy(
        src_ref=source, dst_ref=target, send_sem=sems[0], recv_sem=sems[1],
        device_id=device, device_id_type=mesh_ids,
    )


def gather_kernel(
    w_ref, tok_ref, small_ref, wg_ref, tg_ref, sg_ref,
    wz_s, wz_r, tz_s, tz_r, sz_s, sz_r, wr_s, wr_r, wt_s, wt_r, tt_s, tt_r, et_s, et_r, loc,
):
    rep, chip, core, chips, quarter = places()
    along, across, twin = peer_lists()
    rest_rows = tok_ref.shape[0] - PR_DEV
    prompt_len = chips * 2 * PR_DEV
    prompt = tok_ref.at[pl.ds(0, PR_DEV)]
    rest = tok_ref.at[pl.ds(PR_DEV, rest_rows)]
    near_rows = tg_ref.at[pl.ds(prompt_len, rest_rows)]

    def tok_rows(source, side):
        return tg_ref.at[pl.ds(pl.multiple_of((source * 2 + side) * PR_DEV, PR_DEV), PR_DEV)]

    mine = tok_rows(chip, core)
    own = [
        pltpu.make_async_copy(w_ref, wg_ref.at[:, chip, core], loc.at[0]),
        pltpu.make_async_copy(prompt, mine, loc.at[1]),
        pltpu.make_async_copy(small_ref, sg_ref.at[chip, core], loc.at[2]),
        pltpu.make_async_copy(rest, tg_ref.at[pl.ds(prompt_len + rest_rows, rest_rows)], loc.at[3]),
    ]
    for copy in own:
        copy.start()
    greet(along + across + [twin])
    started = []

    def go(copy):
        copy.start()
        started.append(copy)

    for k, device in enumerate(along):
        go(send(w_ref.at[:, quarter], wg_ref.at[:, chip, core, quarter], (wz_s.at[k], wz_r.at[k]), device))
        go(send(small_ref, sg_ref.at[chip, core], (sz_s.at[k], sz_r.at[k]), device))
    go(send(rest, near_rows, (et_s.at[0], et_r.at[0]), twin))
    go(send(prompt, mine, (tt_s.at[0], tt_r.at[0]), twin))
    go(send(w_ref, wg_ref.at[:, chip, core], (wt_s.at[0], wt_r.at[0]), twin))
    for k in range(1, chips):
        source = (chip + chips - k) % chips
        piece = wg_ref.at[:, source, core, quarter]
        send(piece, piece, (wz_s.at[k - 1], wz_r.at[k - 1]), twin).wait_recv()
        for j, device in enumerate(across):
            go(send(piece, piece, (wr_s.at[k - 1, j], wr_r.at[k - 1, j]), device))
        go(send(prompt, mine, (tz_s.at[k - 1], tz_r.at[k - 1]), along[k - 1]))
    for k in range(1, chips):
        source = (chip + chips - k) % chips
        for j in range(1, QUARTERS):
            piece = wg_ref.at[:, source, core, (quarter + QUARTERS - j) % QUARTERS]
            send(piece, piece, (wr_s.at[k - 1, j - 1], wr_r.at[k - 1, j - 1]), twin).wait_recv()
        row = wg_ref.at[:, source, core]
        go(send(row, row, (wt_s.at[k], wt_r.at[k]), twin))
        theirs = tok_rows(source, core)
        send(theirs, theirs, (tz_s.at[k - 1], tz_r.at[k - 1]), twin).wait_recv()
        go(send(theirs, theirs, (tt_s.at[k], tt_r.at[k]), twin))
        send(small_ref, sg_ref.at[source, core], (sz_s.at[k - 1], sz_r.at[k - 1]), twin).wait_recv()
    for copy in own:
        copy.wait()
    go(send(sg_ref.at[:, core], sg_ref.at[:, core], (et_s.at[1], et_r.at[1]), twin))
    send(rest, near_rows, (et_s.at[0], et_r.at[0]), twin).wait_recv()
    for k in range(chips):
        source = (chip + chips - k) % chips
        row = wg_ref.at[:, source, 1 - core]
        send(row, row, (wt_s.at[k], wt_r.at[k]), twin).wait_recv()
        theirs = tok_rows(source, 1 - core)
        send(theirs, theirs, (tt_s.at[k], tt_r.at[k]), twin).wait_recv()
    send(sg_ref.at[:, core], sg_ref.at[:, 1 - core], (et_s.at[1], et_r.at[1]), twin).wait_recv()
    for copy in started:
        copy.wait_send()


def gather_all(weights, tokens, small):
    chips = lax.axis_size("shard") // 2
    width = tokens.shape[1]
    pairs = pltpu.SemaphoreType.DMA
    count = chips - 1
    return pl.pallas_call(
        gather_kernel,
        out_shape=(
            jax.ShapeDtypeStruct((weights.shape[0], chips, 2) + weights.shape[1:], weights.dtype),
            jax.ShapeDtypeStruct((2 * chips * PR_DEV + 2 * (tokens.shape[0] - PR_DEV), width), tokens.dtype),
            jax.ShapeDtypeStruct((chips, 2) + small.shape, small.dtype),
        ),
        in_specs=[anywhere] * 3,
        out_specs=(anywhere,) * 3,
        scratch_shapes=[
            pairs((count,)), pairs((count,)), pairs((count,)), pairs((count,)), pairs((count,)), pairs((count,)),
            pairs((count, 3)), pairs((count, 3)), pairs((chips,)), pairs((chips,)), pairs((chips,)), pairs((chips,)),
            pairs((2,)), pairs((2,)), pairs((4,)),
        ],
        compiler_params=pltpu.CompilerParams(collective_id=0, has_side_effects=True),
        cost_estimate=pl.CostEstimate(flops=0, bytes_accessed=100_000_000, transcendentals=0),
        name="gather_all",
    )(weights, tokens, small)


def reduce_kernel(
    d_ref, p_ref, e_ref, out_ref, po_ref, eo_ref,
    half, summed, third, thirds, fourth, fourths, last, gathered, p_half, p_sum, p_in,
    ds_s, ds_r, ps_s, ps_r, dr_s, dr_r, dh_s, dh_r, dz_s, dz_r, pz_s, pz_r, da_s, da_r,
):
    rep, chip, core, chips, quarter = places()
    along, across, twin = peer_lists()
    classes = lax.axis_size("rep") // QUARTERS
    above = [
        ((rep // QUARTERS + k) % classes * QUARTERS + quarter, chip * 2 + core) for k in range(1, classes)
    ]
    greet(along + across + above + [twin])
    first = [
        send(p_ref.at[:, 1 - core], p_half, (ps_s.at[0], ps_r.at[0]), twin),
        send(e_ref, eo_ref, (ps_s.at[1], ps_r.at[1]), twin),
    ] + [
        send(d_ref.at[k, 1 - core], half.at[k], (ds_s.at[k], ds_r.at[k]), twin) for k in range(chips)
    ]
    for copy in first:
        copy.start()
    pending = list(first)
    first[0].wait_recv()
    for k in range(chips):
        p_sum[k] = (p_ref[k, core].astype(single) + p_half[k].astype(single)).astype(p_sum.dtype)
    for k, device in enumerate(along):
        copy = send(p_sum.at[(chip + k + 1) % chips], p_in.at[k], (pz_s.at[k], pz_r.at[k]), device)
        copy.start()
        pending.append(copy)
    for k in range(chips):
        first[2 + k].wait_recv()
        for t in range(QUARTERS):
            summed[t, k] = (d_ref[k, core, t].astype(single) + half[k, t].astype(single)).astype(summed.dtype)
    for j, device in enumerate(across):
        copy = send(summed.at[(quarter + j + 1) % QUARTERS], third.at[j], (dr_s.at[j], dr_r.at[j]), device)
        copy.start()
        pending.append(copy)
    for j in range(QUARTERS - 1):
        send(third.at[j], third.at[j], (dr_s.at[j], dr_r.at[j]), twin).wait_recv()
    for k in range(chips):
        total = summed[quarter, k].astype(single)
        for j in range(QUARTERS - 1):
            total = total + third[j, k].astype(single)
        thirds[k] = total.astype(thirds.dtype)
    if classes > 1:
        for j, device in enumerate(above):
            copy = send(thirds, fourth.at[j], (dh_s.at[j], dh_r.at[j]), device)
            copy.start()
            pending.append(copy)
        for j in range(classes - 1):
            send(thirds, fourth.at[j], (dh_s.at[j], dh_r.at[j]), twin).wait_recv()
        for k in range(chips):
            total = thirds[k].astype(single)
            for j in range(classes - 1):
                total = total + fourth[j, k].astype(single)
            fourths[k] = total.astype(fourths.dtype)
    else:
        fourths = thirds
    for k, device in enumerate(along):
        copy = send(fourths.at[(chip + k + 1) % chips], last.at[k], (dz_s.at[k], dz_r.at[k]), device)
        copy.start()
        pending.append(copy)
    for k in range(chips - 1):
        send(p_in.at[k], p_in.at[k], (pz_s.at[k], pz_r.at[k]), twin).wait_recv()
    total = p_sum[chip].astype(single)
    for k in range(chips - 1):
        total = total + p_in[k].astype(single)
    po_ref[...] = total
    for k in range(chips - 1):
        send(last.at[k], last.at[k], (dz_s.at[k], dz_r.at[k]), twin).wait_recv()
    total = fourths[chip].astype(single)
    for k in range(chips - 1):
        total = total + last[k].astype(single)
    gathered[quarter] = total.astype(gathered.dtype)
    for j, device in enumerate(across):
        copy = send(gathered.at[quarter], gathered.at[quarter], (da_s.at[j], da_r.at[j]), device)
        copy.start()
        pending.append(copy)
    for j in range(QUARTERS - 1):
        piece = gathered.at[(quarter + QUARTERS - j - 1) % QUARTERS]
        send(piece, piece, (da_s.at[j], da_r.at[j]), twin).wait_recv()
    out_ref[...] = gathered[...].astype(single)
    first[1].wait_recv()
    for copy in pending:
        copy.wait_send()


def reduce_all(dense, prompt_part, near_part):
    chips = lax.axis_size("shard") // 2
    classes = lax.axis_size("rep") // QUARTERS
    piece = dense.shape[3:]
    pairs = pltpu.SemaphoreType.DMA
    count = chips - 1
    return pl.pallas_call(
        reduce_kernel,
        out_shape=(
            jax.ShapeDtypeStruct((QUARTERS,) + piece, single),
            jax.ShapeDtypeStruct(prompt_part.shape[2:], single),
            jax.ShapeDtypeStruct(near_part.shape, low),
        ),
        in_specs=[in_vmem] * 3,
        out_specs=(in_vmem,) * 3,
        scratch_shapes=[
            pltpu.VMEM((chips, QUARTERS) + piece, low),
            pltpu.VMEM((QUARTERS, chips) + piece, low),
            pltpu.VMEM((QUARTERS - 1, chips) + piece, low),
            pltpu.VMEM((chips,) + piece, low),
            pltpu.VMEM((max(classes - 1, 1), chips if classes > 1 else 1) + piece, low),
            pltpu.VMEM((chips if classes > 1 else 1,) + piece, low),
            pltpu.VMEM((count,) + piece, low),
            pltpu.VMEM((QUARTERS,) + piece, low),
            pltpu.VMEM((chips,) + prompt_part.shape[2:], low),
            pltpu.VMEM((chips,) + prompt_part.shape[2:], low),
            pltpu.VMEM((count,) + prompt_part.shape[2:], low),
            pairs((chips,)), pairs((chips,)), pairs((2,)), pairs((2,)), pairs((3,)), pairs((3,)),
            pairs((max(classes - 1, 1),)), pairs((max(classes - 1, 1),)),
            pairs((count,)), pairs((count,)), pairs((count,)), pairs((count,)), pairs((3,)), pairs((3,)),
        ],
        compiler_params=pltpu.CompilerParams(collective_id=1, has_side_effects=True, vmem_limit_bytes=vmem_cap),
        cost_estimate=pl.CostEstimate(flops=0, bytes_accessed=200_000_000, transcendentals=0),
        name="reduce_all",
    )(dense, prompt_part, near_part)


def local(
    tokens,
    routes,
    slot_ids,
    w_query,
    w_key,
    w_value,
    w_output,
    w_router,
    norm_attn,
    norm_moe,
    rel_table,
    w_in,
    w_out,
    cotangent,
):
    shard_count = lax.axis_size("shard")
    token_rows, model_width = tokens.shape
    prompt_len = PR_DEV * shard_count
    weight_rows, expert_count = w_router.shape
    table_rows, head_count = rel_table.shape
    capacity = 2 * token_rows // expert_count
    slot_count = expert_count * capacity

    weights = jnp.stack([w_query, w_key, w_value, w_output]).reshape(4, QUARTERS, -1, model_width)
    small = jnp.concatenate(
        [w_router, norm_attn[:, None], norm_moe[:, None],
         jnp.pad(rel_table, ((0, weight_rows - table_rows), (0, 0)))], axis=1
    )
    small = jnp.pad(small, ((0, 0), (0, TILE - small.shape[1])))
    dispatch = routes * capacity + slot_ids

    weights, every_tok, small = gather_all(weights, tokens, small)
    weights = weights.reshape(4, model_width, model_width)
    small = small.reshape(model_width, TILE)
    bucket_row = jnp.asarray(np.tile(distance_buckets(table_rows * shard_count), (8, 1)), jnp.int32)
    normed, queries, keys, values, attended, lse, rev, mid, gate, gains, slots_out, grad_in = front(
        every_tok, tokens, weights, small, bucket_row, routes[:, None],
        jnp.broadcast_to(dispatch[None, :], (8, token_rows)), cotangent, slot_count,
    )
    by_chip = (shard_count // 2, 2, capacity, model_width)
    grad_back, result, grad_w_in, grad_w_out, router_grads = moe(
        slots_out.reshape(by_chip), grad_in.reshape(by_chip), small, w_in[0], w_out[0]
    )
    grad_w_in, grad_w_out = grad_w_in[None], grad_w_out[None]
    grad_back = grad_back.reshape(slot_count, model_width)
    returned = lax.all_to_all(
        result.reshape(expert_count, capacity, model_width), "shard", split_axis=0, concat_axis=0, tiled=True
    ).reshape(slot_count, model_width)
    expert_in_grad = lax.psum_scatter(grad_w_in, "rep", scatter_dimension=1, tiled=True).astype(single)
    expert_out_grad = lax.psum_scatter(grad_w_out, "rep", scatter_dimension=1, tiled=True).astype(single)
    dense, prompt_part, near_part, grad_own, grad_resid = back(
        grad_back, dispatch[:, None], mid, cotangent, gains, every_tok, weights,
        (normed, queries, keys, values, attended, lse, rev), bucket_row, router_grads,
    )
    place = (jnp.arange(slot_count, dtype=jnp.int32)[:, None] == dispatch[None, :]).astype(low)
    expert_single = lax.dot_general(
        place, returned, (((0,), (0,)), ((), ())), preferred_element_type=single
    )
    mixed = (mid + gate[:, :1] * expert_single).astype(low)
    chips = shard_count // 2
    dense, prompt_sum, near_grad = reduce_all(
        dense.reshape(chips, 2, QUARTERS, weight_rows // QUARTERS, -1),
        prompt_part.reshape(chips, 2, PR_DEV, model_width), near_part,
    )
    grad_normed = grad_own + jnp.concatenate([prompt_sum, near_grad.astype(single)])
    grad_tokens = grad_resid + norm_pull(grad_normed, tokens.astype(single), gains[0:1])
    dense = dense.reshape(weight_rows, -1)
    parts = [dense[:, i * model_width : (i + 1) * model_width] for i in range(4)]
    tail = dense[:, 4 * model_width :]
    return (
        mixed,
        grad_tokens,
        *parts,
        tail[:, :expert_count],
        tail[:, expert_count],
        tail[:, expert_count + 1],
        tail[:table_rows, expert_count + 2 : expert_count + 2 + head_count],
        expert_in_grad,
        expert_out_grad,
    )


def solution(mesh):
    return jax.shard_map(
        local,
        mesh=mesh,
        in_specs=(
            P(("rep", "shard"), None),
            P(("rep", "shard")),
            P(("rep", "shard")),
            P("shard", None),
            P("shard", None),
            P("shard", None),
            P("shard", None),
            P("shard", None),
            P("shard"),
            P("shard"),
            P("shard", None),
            P("shard", None, None),
            P("shard", None, None),
            P(("rep", "shard"), None),
        ),
        out_specs=(
            P(("rep", "shard"), None),
            P(("rep", "shard"), None),
            P("shard", None),
            P("shard", None),
            P("shard", None),
            P("shard", None),
            P("shard", None),
            P("shard"),
            P("shard"),
            P("shard", None),
            P("shard", "rep", None),
            P("shard", "rep", None),
        ),
        check_vma=False,
    )
```

time: 455 us -> 342 us (0.75)
  Pallas kernels: 183 us -> 290 us
  matrix products: 110 us -> 3.16 us
  waiting for transfers between devices: 71.8 us -> 0.72 us
  starting transfers between devices: 28.7 us -> 8.05 us
  local copies, waits for them, and re-layouts: 24.5 us -> 12.3 us
  other arithmetic: 18.1 us -> 12.1 us
    pallas_call x2 -> x3, Pallas kernels: 49.5 us -> 157 us  [the longest x1 71.9 us: moe(): pl.pallas_call(moe_kernel, out_shape=(shape(rows_out.shape, low), shape(r...]
    dot_general x26 -> x1, matrix products: 110 us -> 3.16 us  [local(): lax.dot_general(place, returned, (((0,), (0,)), ((), ())), preferred_elem...]
    all_to_all x4 -> x1, waiting for transfers between devices: 71.5 us -> 0.01 us  [local(): lax.all_to_all(result.reshape(expert_count, capacity, model_width), 'shar...]
    all_to_all x4 -> x1, starting transfers between devices: 28 us -> 7.98 us  [local(): lax.all_to_all(result.reshape(expert_count, capacity, model_width), 'shar...]
    pallas_call x1, Pallas kernels: 80.8 us -> 93.7 us  [reduce_all(): pl.pallas_call(reduce_kernel, out_shape=(jax.ShapeDtypeStruct((QUARTERS,)...]
    pallas_call x1, Pallas kernels: 52.4 us -> 39.7 us  [gather_all(): pl.pallas_call(gather_kernel, out_shape=(jax.ShapeDtypeStruct((weights.sh...]
    slice x6 -> x2, local copies, waits for them, and re-layouts: 8.47 us -> 0.89 us  [the longest x1 0.75 us: local(): gains[0:1]]
    unnamed x117 -> x14, local copies, waits for them, and re-layouts: 8.83 us -> 2.98 us
  transfers between devices with their start and end apart: 6 -> 3, of which waited for: 4 -> 0; matrix products, arithmetic and copies ran while one was open for 20% -> 5% of each run, Pallas kernels for 25% -> 42%
where the time goes in v2:
time: 342 us; the launch traced here: 341 us
  Pallas kernels  290 us (85%)
  between operations  14.2 us (4%)
  local copies, waits for them, and re-layouts  12.3 us (4%)
  other arithmetic  12.1 us (4%)
  starting transfers between devices  8.05 us (2%)
    pallas_call x1, Pallas kernels, reduce_all(): pl.pallas_call(reduce_kernel, out_shape=(jax.ShapeDtypeStruct((QUARTERS,)...  93.7 us
    pallas_call x1, Pallas kernels, moe(): pl.pallas_call(moe_kernel, out_shape=(shape(rows_out.shape, low), shape(r...  71.9 us
    pallas_call x1, Pallas kernels, back(): pl.pallas_call(back_kernel, out_shape=(shape((width, 4 * width + TILE), l...  50.5 us
    pallas_call x1, Pallas kernels, gather_all(): pl.pallas_call(gather_kernel, out_shape=(jax.ShapeDtypeStruct((weights.sh...  39.7 us
    pallas_call x1, Pallas kernels, front(): pl.pallas_call(front_kernel, out_shape=(shape((keys, width), low), shape(...  34.5 us
    all_to_all x1, starting transfers between devices, local(): lax.all_to_all(result.reshape(expert_count, capacity, model_width), 'shar...  7.98 us
  transfers between devices with their start and end apart: 3, of which 0 were waited for; matrix products, arithmetic and copies ran while one was open for 5% of the time, Pallas kernels for 42%

profile of v2, /device:TPU:0, one launch (start us, length us, event | category | flops | bytes accessed | tf_op | source)
XLA Modules:
  0.0 340.9 jit_solution(8081602821589398111)
XLA Ops:
  7.2 0.8 copy.37
  8.0 0.7 fusion.9
  8.9 1.5 broadcast_in_dim.35.route_ref
  10.3 0.7 multiply_add_fusion
  11.6 2.0 pad_maximum_fusion.w_ref
  13.7 39.7 %gather_all.1 = (bf16[4,4,2,4,24,768]{5,4,3,2,1,0:T(8,128)(2,1)}, bf16[1536,768]{1,0:T(8,128)(2,1)}, bf16[4,2,96,128]{3,2,1,0:T(8,128)(2,1)}) custom-call(bf16[4,4,24,768]{3,2,1,0:T(8,128)(2,1)} %pad_maximum_fusion.w_ref, bf16[384,768]{1,0:T(8,128)(2,1)} %tok_ref.3, bf16[96,128]{1,0:T(8,128)(2,1)} %pad.9.small_ref), custom_call_target="tpu_custom_call" | custom-call | bytes 100000000 | tf_op jit(solution)/shard_map/gather_all/pallas_call | solution.py:728
  54.0 34.5 %front.1 = (bf16[1536,768]{1,0:T(8,128)(2,1)}, bf16[384,768]{1,0:T(8,128)(2,1)}, bf16[1536,768]{1,0:T(8,128)(2,1)}, bf16[1536,768]{1,0:T(8,128)(2,1)}, f32[384,7...) custom-call(bf16[1536,768]{1,0:T(8,128)(2,1)} %get-tuple-element.40., ...), custom_call_target="tpu_custom_call" | custom-call | flops 30000001024 | bytes 20000000 | tf_op jit(solution)/shard_map/front/pallas_call | solution.py:260
  88.6 71.9 %moe.1 = (bf16[4,2,96,768]{3,2,1,0:T(8,128)(2,1)}, bf16[4,2,96,768]{3,2,1,0:T(8,128)(2,1)}, bf16[768,3072]{1,0:T(8,128)(2,1)}, bf16[3072,768]{1,0:T(8,128)(2,1)}, f32[768,128]{1,0:T(8,128)}) custom-call(bf16[4,2,96,768]{3,2,1,0:T(8,128)(2,1)} %bitcast.42, bf16[4,2,96,768]{3,2,1,0:T(8,128)(2,1)} %bitcast.43, bf16[768,128]{1,0:T(8,128)(2,1)} %bitcast.40, ...), custom_call_target="tpu_custom_call" | custom-call | flops 40000000000 | bytes 40000000 | tf_op jit(solution)/shard_map/moe/pallas_call | solution.py:431
  160.6 0.7 reduce-scatter.5.cloned.1.call-update
  161.3 8.0 %all-to-all-start = ((bf16[8,96,768]{2,1,0:T(8,128)(2,1)}), bf16[8,96,768]{2,1,0:T(8,128)(2,1)}, u32[]{:S(2)}, u32[]{:S(2)}) async-start(bf16[8,96,768]{2,1,0:T(8,128)(2,1)} %bitcast.12), calls=%async_computation | async-start | bytes 2359296 | tf_op jit(solution)/shard_map/all_to_all | solution.py:917
  169.3 0.8 broadcast_in_dim.36.col_ref
  170.0 50.5 %back.1 = (bf16[768,3200]{1,0:T(8,128)(2,1)}, bf16[1024,768]{1,0:T(8,128)(2,1)}, bf16[256,768]{1,0:T(8,128)(2,1)}, f32[384,768]{1,0:T(8,128)}, f32[384,768]{1,0:T(8,128)}) custom-call(bf16[768,768]{1,0:T(8,128)(2,1)} %bitcast.41, s32[384,1]{1,0:T(8,128)} %broadcast_in_dim.36.col_ref, f32[384,768]{1,0:T(8,128)} %get-tuple-element.43.mid_ref, ...), custom_call_target="tpu_custom_call" | custom-call | flops 60000002048 | bytes 40000000 | tf_op jit(solution)/shard_map/back/pallas_call | solution.py:605
  220.5 93.7 %reduce_all.1 = (f32[4,24,3200]{2,1,0:T(8,128)}, f32[128,768]{1,0:T(8,128)}, bf16[256,768]{1,0:T(8,128)(2,1)}) custom-call(bf16[4,2,4,24,3200]{4,3,2,1,0:T(8,128)(2,1)} %bitcast.21, bf16[4,2,128,768]{3,2,1,0:T(8,128)(2,1)} %bitcast.24, bf16[256,768]{1,0:T(8,128)(2,1)} %get-tuple-element.62.e_ref), custom_call_target="tpu_custom_call" | custom-call | bytes 200000000 | tf_op jit(solution)/shard_map/reduce_all/pallas_call | solution.py:840
  314.3 0.9 slice.49
  315.2 1.3 slice.52
  316.5 1.0 convert_element_type.22
  318.2 0.8 slice_reduce_fusion.3
  319.0 1.6 slice_reduce_fusion.1
  321.2 0.9 copy-done.3
  322.1 1.0 fusion.11
  323.7 1.4 fusion.5
  325.1 3.2 fusion.1
  328.3 2.9 convert_element_type.23
  331.2 2.8 convert_element_type.24
  (24 shorter events, 3.3 us)
Async XLA Ops:
  7.2 321.1 %reduce-scatter.3.cloned.1.call-start = ((), (), s32[]{:S(2)}) async-start(), calls=%async_computation.3 | async-start | bytes 5898240 | tf_op jit(solution)/shard_map/reduce_scatter | solution.py:920
  160.5 170.7 %reduce-scatter.5.cloned.1.call-start = ((), (), s32[]{:S(2)}) async-start(), calls=%async_computation.4 | async-start | bytes 5898240 | tf_op jit(solution)/shard_map/reduce_scatter | solution.py:921
  161.3 163.8 %all-to-all-start = ((bf16[8,96,768]{2,1,0:T(8,128)(2,1)}), bf16[8,96,768]{2,1,0:T(8,128)(2,1)}, u32[]{:S(2)}, u32[]{:S(2)}) async-start(bf16[8,96,768]{2,1,0:T(8,128)(2,1)} %bitcast.12), calls=%async_computation | async-start | bytes 2359296 | tf_op jit(solution)/shard_map/all_to_all | solution.py:917
  220.5 100.2 %copy-start.1 = (f32[384,768]{1,0:T(8,128)S(1)}, f32[384,768]{1,0:T(8,128)}, u32[]{:S(2)}) copy-start(f32[384,768]{1,0:T(8,128)} %get-tuple-element.59) | copy-start | bytes 3538948
  314.3 6.3 %copy-start.5 = (f32[384,128]{1,0:T(8,128)S(1)}, f32[384,128]{1,0:T(8,128)}, u32[]{:S(2)}) copy-start(f32[384,128]{1,0:T(8,128)} %get-tuple-element.44) | copy-start | bytes 589828
  314.3 6.5 %copy-start = (bf16[384,768]{1,0:T(8,128)(2,1)S(1)}, bf16[384,768]{1,0:T(8,128)(2,1)}, u32[]{:S(2)}) copy-start(bf16[384,768]{1,0:T(8,128)(2,1)} %tok_ref.3) | copy-start | bytes 1769476
  314.3 6.5 %copy-start.2 = (f32[128,768]{1,0:T(8,128)S(1)}, f32[128,768]{1,0:T(8,128)}, u32[]{:S(2)}) copy-start(f32[128,768]{1,0:T(8,128)} %get-tuple-element.63) | copy-start | bytes 1179652
  320.8 1.3 copy-start.3
  322.1 1.7 copy-start.4
Sparse Core Ops, SparseCore 0:
  160.6 61.4 reduce-scatter.2
  225.1 88.8 reduce-scatter.4

commit v3 on v2

--- a/solution.py
+++ b/solution.py
@@ -9,6 +9,7 @@
 PR_DEV = 128
 TILE = 128
 SPAN = 2 * TILE
+BLOCK = 1536
 QUARTERS = 4
 far_before, far_after, causal_tile, hidden_tile, tile_kinds = 3, 4, 5, 6, 7
 vmem_cap = 60 * 1024 * 1024
@@ -286,16 +287,15 @@
 def moe_kernel(
     x_ref, g_ref, small_ref, w_in_ref, w_out_ref,
     back_ref, out_ref, gwin_ref, gwout_ref, rg_ref,
-    w_in, w_out, xin, gm, gg, hid, gpre, acc, gacc, logit_grads, x_t, gwin, gwout,
+    w_in, w_out, xin, gm, gg, hid, gpre, logit_grads, x_t, gwin, gwout,
     xs, xr, ms, mr, ws, ls, os_in, os_out,
 ):
     rep, chip, core, chips, quarter = places()
     experts = chips * 2
     here = chip * 2 + core
-    pair_rows = acc.shape[0]
-    cap = pair_rows // 2
+    pair_rows = 2 * xin.shape[2]
     hidden = w_in_ref.shape[1]
-    block = 512
+    block = BLOCK
     loads = [
         pltpu.make_async_copy(w_in_ref, w_in, ws.at[0]),
         pltpu.make_async_copy(w_out_ref, w_out, ws.at[1]),
@@ -304,15 +304,15 @@
         copy.start()
     twin = (rep, chip * 2 + 1 - core)
     targets = [
-        (k, side, (rep, (chip + k) % chips * 2 + side)) for k in range(1, chips) for side in range(2)
+        (k, side, (rep, chip_across(chip, k) * 2 + side)) for k in range(1, chips) for side in range(2)
     ]
     greet([twin] + [device for _, _, device in targets])
     sent = [send(x_ref.at[chip, 1 - core], xin.at[chip, core], (xs.at[0, 0], xr.at[0, core]), twin)]
     for k, side, device in targets:
         sent.append(
-            send(x_ref.at[(chip + k) % chips, side], xin.at[chip, core], (xs.at[k, side], xr.at[k, core]), device)
+            send(x_ref.at[chip_across(chip, k), side], xin.at[chip, core], (xs.at[k, side], xr.at[k, core]), device)
         )
-    for copy in sent:
+    for copy in sent[:5]:
         copy.start()
     xin[chip, core] = x_ref[chip, core]
     for copy in loads:
@@ -324,7 +324,7 @@
 
     @pl.loop(0, chips)
     def chunk(k):
-        source = (chip + chips - k) % chips
+        source = chip_across(chip, k)
 
         @pl.when(k == 0)
         def _():
@@ -343,35 +343,24 @@
         gated = (gate * grads.astype(single)).astype(low)
         span = pl.ds(pl.multiple_of(source * pair_rows, pair_rows), pair_rows)
         gg[span, :] = gated
-        acc[...] = jnp.zeros_like(acc)
-        gacc[...] = jnp.zeros_like(gacc)
-
-        @pl.loop(0, hidden // block)
-        def strip(part):
-            cols = pl.ds(pl.multiple_of(part * block, block), block)
-            pre = nn(rows, w_in[:, cols])
-            grad_hidden = nt(gated, w_out[cols, :])
-            square = pre * pre
-            wave = jnp.tanh(0.7978845608028654 * pre * (1.0 + 0.044715 * square))
-            left = 0.5 + 0.5 * wave
-            active = (pre * left).astype(low)
-            slope = left + (0.5 * pre) * (1.0 - wave * wave) * (
-                0.7978845608028654 + 0.10703222440890037 * square
-            )
-            grad_pre = (grad_hidden * slope).astype(low)
-            hid[span, cols] = active
-            gpre[span, cols] = grad_pre
-            acc[...] += nn(active, w_out[cols, :])
-            gacc[...] += nt(grad_pre, w_in[:, cols])
-
-        out = acc[...].astype(low)
+        pre = nn(rows, w_in[...])
+        grad_hidden = nt(gated, w_out[...])
+        square = pre * pre
+        wave = jnp.tanh(0.7978845608028654 * pre * (1.0 + 0.044715 * square))
+        left = 0.5 + 0.5 * wave
+        active = (pre * left).astype(low)
+        slope = left + (0.5 * pre) * (1.0 - wave * wave) * (0.7978845608028654 + 0.10703222440890037 * square)
+        grad_pre = (grad_hidden * slope).astype(low)
+        hid[span, :] = active
+        gpre[span, :] = grad_pre
+        out = nn(active, w_out[...]).astype(low)
         out_ref[source] = out.reshape(out_ref.shape[1:])
         grad_gate = jnp.sum(grads.astype(single) * out.astype(single), axis=1, keepdims=True)
         chosen = jnp.where(lanes == here, 1.0, 0.0)
         grad_logits = jnp.where(lanes < experts, gate * grad_gate * (chosen - probs), 0.0)
         logit_grads[span, :] = grad_logits
         router = small_ref[...]
-        total = gacc[...] + sum(nt(part, router) for part in thirds_of(grad_logits))
+        total = nt(grad_pre, w_in[...]) + sum(nt(part, router) for part in thirds_of(grad_logits))
         gm[source] = total.astype(low).reshape(gm.shape[1:])
 
         def reply(side, slot):
@@ -381,6 +370,8 @@
 
         @pl.when(k == 0)
         def _():
+            for copy in sent[5:]:
+                copy.start()
             reply(1 - core, 0).start()
             pltpu.make_async_copy(gm.at[chip, core], back_ref.at[chip, core], ls).start()
 
@@ -410,7 +401,7 @@
     replied(0, chip, 1 - core)
     for k in range(1, chips):
         for side in range(2):
-            replied(k, (chip + k) % chips, side)
+            replied(k, chip_across(chip, k), side)
     for copy in sent:
         copy.wait_send()
     for copy in writes:
@@ -427,7 +418,7 @@
     hidden = w_in.shape[1]
     shape = jax.ShapeDtypeStruct
     pairs = pltpu.SemaphoreType.DMA
-    strips = hidden // 512
+    strips = hidden // BLOCK
     return pl.pallas_call(
         moe_kernel,
         out_shape=(
@@ -440,8 +431,7 @@
             pltpu.VMEM((width, hidden), low), pltpu.VMEM((hidden, width), low),
             pltpu.VMEM(rows_out.shape, low), pltpu.VMEM(rows_out.shape, low), pltpu.VMEM((slots, width), low),
             pltpu.VMEM((slots, hidden), low), pltpu.VMEM((slots, hidden), low),
-            pltpu.VMEM((2 * cap, width), single), pltpu.VMEM((2 * cap, width), single), pltpu.VMEM((slots, TILE), single),
-            pltpu.VMEM((width, slots), low), pltpu.VMEM((width, hidden), low), pltpu.VMEM((hidden, width), low),
+            pltpu.VMEM((slots, TILE), single), pltpu.VMEM((width, slots), low), pltpu.VMEM((width, hidden), low), pltpu.VMEM((hidden, width), low),
             pairs((chips, 2)), pairs((chips, 2)), pairs((chips, 2)), pairs((chips, 2)), pairs((2,)), pairs,
             pairs((strips,)), pairs((strips,)),
         ],
@@ -452,10 +442,11 @@
 
 
 def back_kernel(
-    back_ref, col_ref, mid_ref, cot_ref, gain_ref, every_ref, w_ref, n_ref, q_ref, k_ref, v_ref, o_ref,
-    lse_ref, rev_ref, bucket_ref, rg_ref,
-    dense_ref, p_ref, e_ref, own_ref, gres_ref,
+    back_ref, col_ref, mid_ref, cot_ref, gain_ref, q_ref, k_ref, v_ref, o_ref,
+    lse_ref, rev_ref, bucket_ref, rg_ref, every_hbm, w_hbm, n_hbm, out_hbm, gwin_hbm, gwout_hbm,
+    dense_ref, p_ref, e_ref, own_ref, gres_ref, ret_hbm, ra_hbm, rb_hbm,
     tiles, sums, diag, kt, dqt, far_sums, dk_sum, dv_sum, g_ref, dq_ref, dk_ref, dv_ref, attn_gain,
+    every_ref, w_ref, n_ref, loc, xs, xr, as_, ar, bs, br,
 ):
     shard_id = lax.axis_index("shard")
     shards = lax.axis_size("shard")
@@ -464,6 +455,32 @@
     half = TILE // 2
     experts = shards
     heads_held = rev_ref.shape[0]
+    rep, slow, fast, slows, fasts = rep_places()
+    loads = [
+        pltpu.make_async_copy(w_hbm.at[3], w_ref.at[3], loc.at[0]),
+        pltpu.make_async_copy(w_hbm.at[pl.ds(0, 3)], w_ref.at[pl.ds(0, 3)], loc.at[1]),
+        pltpu.make_async_copy(n_hbm, n_ref, loc.at[2]),
+        pltpu.make_async_copy(every_hbm, every_ref, loc.at[3]),
+        pltpu.make_async_copy(out_hbm.at[shard_id], ret_hbm.at[shard_id], loc.at[4]),
+    ]
+    for copy in loads:
+        copy.start()
+    others = [(rep, (shard_id + k) % shards) for k in range(1, shards)]
+    beside = [(slow * fasts + (fast + j) % fasts, shard_id) for j in range(1, fasts)]
+    beyond = [((slow + j) % slows * fasts + fast, shard_id) for j in range(1, slows)]
+    greet(others + beside + beyond)
+    sent = [
+        send(gwin_hbm.at[:, (fast + j + 1) % fasts], ra_hbm.at[j], (as_.at[j], ar.at[j]), device)
+        for j, device in enumerate(beside)
+    ] + [
+        send(gwout_hbm.at[(slow + j + 1) % slows], rb_hbm.at[j], (bs.at[j], br.at[j]), device)
+        for j, device in enumerate(beyond)
+    ] + [
+        send(out_hbm.at[device[1]], ret_hbm.at[shard_id], (xs.at[k], xr.at[k]), device)
+        for k, device in enumerate(others)
+    ]
+    for copy in sent:
+        copy.start()
     diag[...] = jnp.zeros_like(diag)
     far_sums[...] = jnp.zeros_like(far_sums)
     tile_rows = lax.broadcasted_iota(jnp.int32, (TILE, TILE), 0)
@@ -477,6 +494,7 @@
     grad_resid = cot_ref[...].astype(single) + norm_pull(grad_mid, resid_mid, gain_ref[1:2, :])
     gres_ref[...] = grad_resid
     grad_attn = grad_resid.astype(low)
+    loads[0].wait()
     g_ref[...] = nt(grad_attn, w_ref[3]).astype(low)
     dense_ref[:, 3 * width : 4 * width] = tn(o_ref[...].astype(low), grad_attn).astype(low)
 
@@ -552,6 +570,8 @@
     grad_table = sum(nt(part, hot) for part in thirds_of(by_gap))
 
     attn_gain[...] = jnp.zeros_like(attn_gain)
+    for copy in loads[1:]:
+        copy.wait()
     own = pl.ds(pl.multiple_of(shard_id * TILE, TILE), TILE)
     tail = slice((blocks + 2) * TILE, (blocks + 4) * TILE)
     normed = jnp.concatenate([n_ref[own, :], n_ref[tail, :]], axis=0)
@@ -591,33 +611,51 @@
         axis=0,
     )
     dense_ref[:, 4 * width :] = (small_t.T + rg_ref[...]).astype(low)
-
-
-def back(returned, col_slots, mid, cotangent, gains, every_tok, weights, kept, bucket_row, router_grads):
+    for k in range(shards - 1):
+        piece = ret_hbm.at[(shard_id + shards - k - 1) % shards]
+        send(piece, piece, (xs.at[k], xr.at[k]), others[0]).wait_recv()
+    for j in range(fasts - 1):
+        send(ra_hbm.at[j], ra_hbm.at[j], (as_.at[j], ar.at[j]), others[0]).wait_recv()
+    for j in range(slows - 1):
+        send(rb_hbm.at[j], rb_hbm.at[j], (bs.at[j], br.at[j]), others[0]).wait_recv()
+    for copy in sent:
+        copy.wait_send()
+
+
+def back(
+    returned, col_slots, mid, cotangent, gains, every_tok, weights, kept, bucket_row, router_grads, result, gwin, gwout
+):
     rows, width = mid.shape
     normed, queries, keys, values, attended, lse, rev = kept
     count = keys.shape[0]
+    shards = result.shape[0]
+    slows, fasts = gwin.shape[:2]
     shape = jax.ShapeDtypeStruct
+    pairs = pltpu.SemaphoreType.DMA
     args = (
-        returned, col_slots, mid, cotangent, gains, every_tok, weights, normed, queries, keys, values, attended,
-        lse, rev, bucket_row, router_grads,
+        returned, col_slots, mid, cotangent, gains, queries, keys, values, attended, lse, rev, bucket_row,
+        router_grads, every_tok, weights, normed, result, gwin, gwout,
     )
     return pl.pallas_call(
         back_kernel,
         out_shape=(
             shape((width, 4 * width + TILE), low), shape((count - 2 * SPAN, width), low), shape((SPAN, width), low),
-            shape((rows, width), single), shape((rows, width), single),
+            shape((rows, width), single), shape((rows, width), single), shape(result.shape, low),
+            shape((fasts - 1, slows) + gwin.shape[2:], low), shape((slows - 1, fasts) + gwout.shape[2:], low),
         ),
-        in_specs=[in_vmem] * len(args),
-        out_specs=(in_vmem,) * 5,
+        in_specs=[in_vmem] * 13 + [anywhere] * 6,
+        out_specs=(in_vmem,) * 5 + (anywhere,) * 3,
         scratch_shapes=[
             pltpu.VMEM((tile_kinds, TILE, TILE), single), pltpu.VMEM((tile_kinds, TILE, TILE), single),
             pltpu.VMEM((16, 4 * TILE), single), pltpu.VMEM((TILE, count), low), pltpu.VMEM((TILE, rows), single),
             pltpu.VMEM((16, 2 * TILE), single), pltpu.VMEM((count, TILE), single), pltpu.VMEM((count, TILE), single),
             pltpu.VMEM((rows, width), low), pltpu.VMEM((rows, width), low), pltpu.VMEM((count, width), low),
             pltpu.VMEM((count, width), low), pltpu.VMEM((8, width), single),
+            pltpu.VMEM(every_tok.shape, low), pltpu.VMEM(weights.shape, low), pltpu.VMEM(normed.shape, low),
+            pairs((5,)), pairs((shards - 1,)), pairs((shards - 1,)), pairs((fasts - 1,)), pairs((fasts - 1,)),
+            pairs((slows - 1,)), pairs((slows - 1,)),
         ],
-        compiler_params=pltpu.CompilerParams(vmem_limit_bytes=vmem_cap),
+        compiler_params=pltpu.CompilerParams(collective_id=4, has_side_effects=True, vmem_limit_bytes=vmem_cap),
         cost_estimate=pl.CostEstimate(flops=60_000_000_000, bytes_accessed=40_000_000, transcendentals=8_000_000),
         name="back",
     )(*args)
@@ -634,6 +672,14 @@
     across = [(rep - quarter + (quarter + j) % QUARTERS, chip * 2 + core) for j in range(1, QUARTERS)]
     twin = (rep, chip * 2 + 1 - core)
     return along, across, twin
+
+
+def chip_across(chip, k):
+    partner, bit = 0, 1
+    while bit < lax.axis_size("shard") // 2:
+        partner = partner + bit * ((chip // bit + k // bit) % 2)
+        bit = bit * 2
+    return partner
 
 
 def greet(devices):
@@ -745,127 +791,220 @@
     )(weights, tokens, small)
 
 
+def rep_places():
+    rep, reps = lax.axis_index("rep"), lax.axis_size("rep")
+    fasts = QUARTERS if reps % (QUARTERS * QUARTERS) == 0 else 2
+    return rep, rep // fasts, rep % fasts, reps // fasts, fasts
+
+
 def reduce_kernel(
-    d_ref, p_ref, e_ref, out_ref, po_ref, eo_ref,
-    half, summed, third, thirds, fourth, fourths, last, gathered, p_half, p_sum, p_in,
-    ds_s, ds_r, ps_s, ps_r, dr_s, dr_r, dh_s, dh_r, dz_s, dz_r, pz_s, pz_r, da_s, da_r,
+    gain_ref, col_ref, d_hbm, p_hbm, e_hbm, own_hbm, gres_hbm, tok_hbm, mid_hbm, gate_hbm, ret_hbm,
+    gwin_hbm, ra_hbm, gwout_hbm, rb_hbm,
+    gt_ref, mix_ref, dq_ref, dk_ref, dv_ref, do_ref, sm_ref, ka_ref, la_hbm, kb_ref, lb_hbm,
+    d_own, half, hr, hz, tr, mr, cr, cz, zs, tz, last, above_in, gathered,
+    p_own, p_half, p_sum, p_in, e_in, own, gres, tok, mid, gate, ret,
+    a_own, a_in, a_sum, b_own, b_in, b_sum,
+    loc, ps_s, ps_r, ds_s, ds_r, pz_s, pz_r, rr_s, rr_r, rz_s, rz_r, zz_s, zz_r, zr_s, zr_r, dh_s, dh_r,
+    da_s, da_r, ea_s, ea_r, eb_s, eb_r,
 ):
     rep, chip, core, chips, quarter = places()
     along, across, twin = peer_lists()
+    _, slow, fast, slows, fasts = rep_places()
     classes = lax.axis_size("rep") // QUARTERS
-    above = [
-        ((rep // QUARTERS + k) % classes * QUARTERS + quarter, chip * 2 + core) for k in range(1, classes)
-    ]
-    greet(along + across + above + [twin])
-    first = [
-        send(p_ref.at[:, 1 - core], p_half, (ps_s.at[0], ps_r.at[0]), twin),
-        send(e_ref, eo_ref, (ps_s.at[1], ps_r.at[1]), twin),
-    ] + [
-        send(d_ref.at[k, 1 - core], half.at[k], (ds_s.at[k], ds_r.at[k]), twin) for k in range(chips)
-    ]
-    for copy in first:
+    here = chip * 2 + core
+    beside = [(slow * fasts + (fast + j) % fasts, here) for j in range(1, fasts)]
+    beyond = [((slow + j) % slows * fasts + fast, here) for j in range(1, slows)]
+    above = [((rep // QUARTERS + k) % classes * QUARTERS + quarter, here) for k in range(1, classes)]
+    width = gain_ref.shape[1]
+    cut = hr.shape[3]
+    wide = lambda ref_value: ref_value.astype(single)
+    pending = []
+
+    def load(source, target, index):
+        copy = pltpu.make_async_copy(source, target, loc.at[index])
         copy.start()
-    pending = list(first)
-    first[0].wait_recv()
-    for k in range(chips):
-        p_sum[k] = (p_ref[k, core].astype(single) + p_half[k].astype(single)).astype(p_sum.dtype)
-    for k, device in enumerate(along):
-        copy = send(p_sum.at[(chip + k + 1) % chips], p_in.at[k], (pz_s.at[k], pz_r.at[k]), device)
+        return copy
+
+    def go(source, target, sems, device):
+        copy = send(source, target, sems, device)
         copy.start()
         pending.append(copy)
+
+    def landed(piece, sems):
+        send(piece, piece, sems, twin).wait_recv()
+
+    experts_in = [
+        load(gwin_hbm.at[:, fast], a_own, 0), load(ra_hbm, a_in, 1),
+        load(gwout_hbm.at[slow], b_own, 2), load(rb_hbm, b_in, 3),
+    ]
+    halves = [load(p_hbm.at[:, core], p_own, 4), load(d_hbm.at[:, core], d_own, 5)]
+    rest = [
+        load(ret_hbm, ret, 6), load(mid_hbm, mid, 7), load(gate_hbm, gate, 8), load(own_hbm, own, 9),
+        load(gres_hbm, gres, 10), load(tok_hbm, tok, 11),
+    ]
+    greets = [twin] + along
+    for device in across + beside + beyond + above:
+        greets.append(device)
+    greet(greets)
+    go(p_hbm.at[:, 1 - core], p_half, (ps_s.at[0], ps_r.at[0]), twin)
     for k in range(chips):
-        first[2 + k].wait_recv()
+        go(d_hbm.at[k, 1 - core], half.at[k], (ds_s.at[k], ds_r.at[k]), twin)
+    go(e_hbm, e_in, (ps_s.at[1], ps_r.at[1]), twin)
+
+    for copy in experts_in:
+        copy.wait()
+    for t in range(slows):
+        total = wide(a_own[t])
+        for j in range(fasts - 1):
+            total = total + wide(a_in[j, t])
+        a_sum[t] = total.astype(low)
+    for t in range(fasts):
+        total = wide(b_own[t])
+        for j in range(slows - 1):
+            total = total + wide(b_in[j, t])
+        b_sum[t] = total.astype(low)
+    for j, device in enumerate(beyond):
+        go(a_sum.at[(slow + j + 1) % slows], la_hbm.at[j], (ea_s.at[j], ea_r.at[j]), device)
+    for j, device in enumerate(beside):
+        go(b_sum.at[(fast + j + 1) % fasts], lb_hbm.at[j], (eb_s.at[j], eb_r.at[j]), device)
+
+    halves[0].wait()
+    landed(p_half, (ps_s.at[0], ps_r.at[0]))
+    for k in range(chips):
+        p_sum[k] = (wide(p_own[k]) + wide(p_half[k])).astype(low)
+    for k, device in enumerate(along):
+        go(p_sum.at[(chip + k + 1) % chips], p_in.at[k], (pz_s.at[k], pz_r.at[k]), device)
+    halves[1].wait()
+    for k in range(chips):
+        landed(half.at[k], (ds_s.at[k], ds_r.at[k]))
         for t in range(QUARTERS):
-            summed[t, k] = (d_ref[k, core, t].astype(single) + half[k, t].astype(single)).astype(summed.dtype)
+            total = (wide(d_own[k, t]) + wide(half[k, t])).astype(low)
+            hr[t, k] = total[:, :cut]
+            hz[k, t] = total[:, cut:]
     for j, device in enumerate(across):
-        copy = send(summed.at[(quarter + j + 1) % QUARTERS], third.at[j], (dr_s.at[j], dr_r.at[j]), device)
-        copy.start()
-        pending.append(copy)
+        go(hr.at[(quarter + j + 1) % QUARTERS], tr.at[j], (rr_s.at[j], rr_r.at[j]), device)
+    for k, device in enumerate(along):
+        go(hz.at[(chip + k + 1) % chips], cz.at[k], (zz_s.at[k], zz_r.at[k]), device)
+
+    for copy in rest:
+        copy.wait()
+    slots = lax.broadcasted_iota(jnp.int32, (tok.shape[0], ret.shape[0]), 1)
+    chosen = nn((slots == col_ref[...]).astype(low), ret[...])
+    mix_ref[...] = (mid[...] + gate[:, 0:1] * chosen).astype(low)
+    ka_ref[...] = a_sum[slow]
+    kb_ref[...] = b_sum[fast]
+
     for j in range(QUARTERS - 1):
-        send(third.at[j], third.at[j], (dr_s.at[j], dr_r.at[j]), twin).wait_recv()
+        landed(tr.at[j], (rr_s.at[j], rr_r.at[j]))
     for k in range(chips):
-        total = summed[quarter, k].astype(single)
+        total = wide(hr[quarter, k])
         for j in range(QUARTERS - 1):
-            total = total + third[j, k].astype(single)
-        thirds[k] = total.astype(thirds.dtype)
+            total = total + wide(tr[j, k])
+        mr[k] = total.astype(low)
+    for k, device in enumerate(along):
+        go(mr.at[(chip + k + 1) % chips], cr.at[k], (rz_s.at[k], rz_r.at[k]), device)
+
+    for k in range(chips - 1):
+        landed(p_in.at[k], (pz_s.at[k], pz_r.at[k]))
+    landed(e_in, (ps_s.at[1], ps_r.at[1]))
+    total = wide(p_sum[chip])
+    for k in range(chips - 1):
+        total = total + wide(p_in[k])
+    grads = own[...] + jnp.concatenate([total, wide(e_in[...])], axis=0)
+    gt_ref[...] = gres[...] + norm_pull(grads, wide(tok[...]), gain_ref[0:1, :])
+
+    for k in range(chips - 1):
+        landed(cz.at[k], (zz_s.at[k], zz_r.at[k]))
+    for t in range(QUARTERS):
+        total = wide(hz[chip, t])
+        for k in range(chips - 1):
+            total = total + wide(cz[k, t])
+        zs[t] = total.astype(low)
+    for j, device in enumerate(across):
+        go(zs.at[(quarter + j + 1) % QUARTERS], tz.at[j], (zr_s.at[j], zr_r.at[j]), device)
+    for k in range(chips - 1):
+        landed(cr.at[k], (rz_s.at[k], rz_r.at[k]))
+    left = wide(mr[chip])
+    for k in range(chips - 1):
+        left = left + wide(cr[k])
+    for j in range(QUARTERS - 1):
+        landed(tz.at[j], (zr_s.at[j], zr_r.at[j]))
+    right = wide(zs[quarter])
+    for j in range(QUARTERS - 1):
+        right = right + wide(tz[j])
+    last[...] = jnp.concatenate([left, right], axis=1).astype(low)
     if classes > 1:
         for j, device in enumerate(above):
-            copy = send(thirds, fourth.at[j], (dh_s.at[j], dh_r.at[j]), device)
-            copy.start()
-            pending.append(copy)
+            go(last, above_in.at[j], (dh_s.at[j], dh_r.at[j]), device)
+        total = wide(last[...])
         for j in range(classes - 1):
-            send(thirds, fourth.at[j], (dh_s.at[j], dh_r.at[j]), twin).wait_recv()
-        for k in range(chips):
-            total = thirds[k].astype(single)
-            for j in range(classes - 1):
-                total = total + fourth[j, k].astype(single)
-            fourths[k] = total.astype(fourths.dtype)
+            landed(above_in.at[j], (dh_s.at[j], dh_r.at[j]))
+            total = total + wide(above_in[j])
+        gathered[quarter] = total.astype(low)
     else:
-        fourths = thirds
-    for k, device in enumerate(along):
-        copy = send(fourths.at[(chip + k + 1) % chips], last.at[k], (dz_s.at[k], dz_r.at[k]), device)
-        copy.start()
-        pending.append(copy)
-    for k in range(chips - 1):
-        send(p_in.at[k], p_in.at[k], (pz_s.at[k], pz_r.at[k]), twin).wait_recv()
-    total = p_sum[chip].astype(single)
-    for k in range(chips - 1):
-        total = total + p_in[k].astype(single)
-    po_ref[...] = total
-    for k in range(chips - 1):
-        send(last.at[k], last.at[k], (dz_s.at[k], dz_r.at[k]), twin).wait_recv()
-    total = fourths[chip].astype(single)
-    for k in range(chips - 1):
-        total = total + last[k].astype(single)
-    gathered[quarter] = total.astype(gathered.dtype)
+        gathered[quarter] = last[...]
     for j, device in enumerate(across):
-        copy = send(gathered.at[quarter], gathered.at[quarter], (da_s.at[j], da_r.at[j]), device)
-        copy.start()
-        pending.append(copy)
+        go(gathered.at[quarter], gathered.at[quarter], (da_s.at[j], da_r.at[j]), device)
     for j in range(QUARTERS - 1):
-        piece = gathered.at[(quarter + QUARTERS - j - 1) % QUARTERS]
-        send(piece, piece, (da_s.at[j], da_r.at[j]), twin).wait_recv()
-    out_ref[...] = gathered[...].astype(single)
-    first[1].wait_recv()
+        landed(gathered.at[(quarter + QUARTERS - j - 1) % QUARTERS], (da_s.at[j], da_r.at[j]))
+    for i, ref in enumerate((dq_ref, dk_ref, dv_ref, do_ref)):
+        ref[...] = wide(gathered[:, :, i * width : (i + 1) * width])
+    sm_ref[...] = wide(gathered[:, :, 4 * width :])
+    for j in range(slows - 1):
+        landed(la_hbm.at[j], (ea_s.at[j], ea_r.at[j]))
+    for j in range(fasts - 1):
+        landed(lb_hbm.at[j], (eb_s.at[j], eb_r.at[j]))
     for copy in pending:
         copy.wait_send()
 
 
-def reduce_all(dense, prompt_part, near_part):
+def reduce_all(gains, col_slots, dense, prompt_part, near_part, own, gres, tokens, mid, gate, returned, gwin, ra, gwout, rb):
     chips = lax.axis_size("shard") // 2
     classes = lax.axis_size("rep") // QUARTERS
-    piece = dense.shape[3:]
-    pairs = pltpu.SemaphoreType.DMA
-    count = chips - 1
+    slows, fasts = gwin.shape[:2]
+    rows, width = mid.shape
+    lines, lanes = dense.shape[3:]
+    cut = 2 * width
+    shape = jax.ShapeDtypeStruct
+    sem = pltpu.SemaphoreType.DMA
+    vm = pltpu.VMEM
+    count, others = chips - 1, QUARTERS - 1
+    ours = prompt_part.shape[2:]
+    extra = max(classes - 1, 1)
+    args = (gains, col_slots, dense, prompt_part, near_part, own, gres, tokens, mid, gate, returned, gwin, ra, gwout, rb)
     return pl.pallas_call(
         reduce_kernel,
         out_shape=(
-            jax.ShapeDtypeStruct((QUARTERS,) + piece, single),
-            jax.ShapeDtypeStruct(prompt_part.shape[2:], single),
-            jax.ShapeDtypeStruct(near_part.shape, low),
+            shape((rows, width), single), shape((rows, width), low),
+            shape((QUARTERS, lines, width), single), shape((QUARTERS, lines, width), single),
+            shape((QUARTERS, lines, width), single), shape((QUARTERS, lines, width), single),
+            shape((QUARTERS, lines, TILE), single),
+            shape(gwin.shape[2:], low), shape((slows - 1,) + gwin.shape[2:], low),
+            shape(gwout.shape[2:], low), shape((fasts - 1,) + gwout.shape[2:], low),
         ),
-        in_specs=[in_vmem] * 3,
-        out_specs=(in_vmem,) * 3,
+        in_specs=[in_vmem] * 2 + [anywhere] * 13,
+        out_specs=(in_vmem,) * 8 + (anywhere, in_vmem, anywhere),
         scratch_shapes=[
-            pltpu.VMEM((chips, QUARTERS) + piece, low),
-            pltpu.VMEM((QUARTERS, chips) + piece, low),
-            pltpu.VMEM((QUARTERS - 1, chips) + piece, low),
-            pltpu.VMEM((chips,) + piece, low),
-            pltpu.VMEM((max(classes - 1, 1), chips if classes > 1 else 1) + piece, low),
-            pltpu.VMEM((chips if classes > 1 else 1,) + piece, low),
-            pltpu.VMEM((count,) + piece, low),
-            pltpu.VMEM((QUARTERS,) + piece, low),
-            pltpu.VMEM((chips,) + prompt_part.shape[2:], low),
-            pltpu.VMEM((chips,) + prompt_part.shape[2:], low),
-            pltpu.VMEM((count,) + prompt_part.shape[2:], low),
-            pairs((chips,)), pairs((chips,)), pairs((2,)), pairs((2,)), pairs((3,)), pairs((3,)),
-            pairs((max(classes - 1, 1),)), pairs((max(classes - 1, 1),)),
-            pairs((count,)), pairs((count,)), pairs((count,)), pairs((count,)), pairs((3,)), pairs((3,)),
+            vm((chips, QUARTERS, lines, lanes), low), vm((chips, QUARTERS, lines, lanes), low),
+            vm((QUARTERS, chips, lines, cut), low), vm((chips, QUARTERS, lines, lanes - cut), low),
+            vm((others, chips, lines, cut), low), vm((chips, lines, cut), low), vm((count, lines, cut), low),
+            vm((count, QUARTERS, lines, lanes - cut), low), vm((QUARTERS, lines, lanes - cut), low),
+            vm((others, lines, lanes - cut), low), vm((lines, lanes), low), vm((extra, lines, lanes), low),
+            vm((QUARTERS, lines, lanes), low),
+            vm((chips,) + ours, low), vm((chips,) + ours, low), vm((chips,) + ours, low), vm((count,) + ours, low),
+            vm(near_part.shape, low), vm((rows, width), single), vm((rows, width), single), vm((rows, width), low),
+            vm((rows, width), single), vm(gate.shape, single), vm(returned.shape, low),
+            vm((slows,) + gwin.shape[2:], low), vm(ra.shape, low), vm((slows,) + gwin.shape[2:], low),
+            vm((fasts,) + gwout.shape[2:], low), vm(rb.shape, low), vm((fasts,) + gwout.shape[2:], low),
+            sem((12,)), sem((2,)), sem((2,)), sem((chips,)), sem((chips,)), sem((count,)), sem((count,)),
+            sem((others,)), sem((others,)), sem((count,)), sem((count,)), sem((count,)), sem((count,)),
+            sem((others,)), sem((others,)), sem((extra,)), sem((extra,)), sem((others,)), sem((others,)),
+            sem((slows - 1,)), sem((slows - 1,)), sem((fasts - 1,)), sem((fasts - 1,)),
         ],
         compiler_params=pltpu.CompilerParams(collective_id=1, has_side_effects=True, vmem_limit_bytes=vmem_cap),
         cost_estimate=pl.CostEstimate(flops=0, bytes_accessed=200_000_000, transcendentals=0),
         name="reduce_all",
-    )(dense, prompt_part, near_part)
+    )(*args)
 
 
 def local(
@@ -912,42 +1051,34 @@
     grad_back, result, grad_w_in, grad_w_out, router_grads = moe(
         slots_out.reshape(by_chip), grad_in.reshape(by_chip), small, w_in[0], w_out[0]
     )
-    grad_w_in, grad_w_out = grad_w_in[None], grad_w_out[None]
-    grad_back = grad_back.reshape(slot_count, model_width)
-    returned = lax.all_to_all(
-        result.reshape(expert_count, capacity, model_width), "shard", split_axis=0, concat_axis=0, tiled=True
-    ).reshape(slot_count, model_width)
-    expert_in_grad = lax.psum_scatter(grad_w_in, "rep", scatter_dimension=1, tiled=True).astype(single)
-    expert_out_grad = lax.psum_scatter(grad_w_out, "rep", scatter_dimension=1, tiled=True).astype(single)
-    dense, prompt_part, near_part, grad_own, grad_resid = back(
-        grad_back, dispatch[:, None], mid, cotangent, gains, every_tok, weights,
+    rep_count = lax.axis_size("rep")
+    slows, fasts = rep_places()[3:]
+    gwin = grad_w_in.reshape(slows, fasts, model_width // rep_count, -1)
+    gwout = grad_w_out.reshape(slows, fasts, -1, model_width)
+    col_slots = dispatch[:, None]
+    dense, prompt_part, near_part, grad_own, grad_resid, returned, ra, rb = back(
+        grad_back.reshape(slot_count, model_width), col_slots, mid, cotangent, gains, every_tok, weights,
         (normed, queries, keys, values, attended, lse, rev), bucket_row, router_grads,
+        result.reshape(expert_count, capacity, model_width), gwin, gwout,
     )
-    place = (jnp.arange(slot_count, dtype=jnp.int32)[:, None] == dispatch[None, :]).astype(low)
-    expert_single = lax.dot_general(
-        place, returned, (((0,), (0,)), ((), ())), preferred_element_type=single
+    chips = shard_count // 2
+    grad_tokens, mixed, gq, gk, gv, go, tail, ka, la, kb, lb = reduce_all(
+        gains, col_slots, dense.reshape(chips, 2, QUARTERS, weight_rows // QUARTERS, -1),
+        prompt_part.reshape(chips, 2, PR_DEV, model_width), near_part, grad_own, grad_resid, tokens, mid, gate,
+        returned.reshape(slot_count, model_width), gwin, ra, gwout, rb,
     )
-    mixed = (mid + gate[:, :1] * expert_single).astype(low)
-    chips = shard_count // 2
-    dense, prompt_sum, near_grad = reduce_all(
-        dense.reshape(chips, 2, QUARTERS, weight_rows // QUARTERS, -1),
-        prompt_part.reshape(chips, 2, PR_DEV, model_width), near_part,
-    )
-    grad_normed = grad_own + jnp.concatenate([prompt_sum, near_grad.astype(single)])
-    grad_tokens = grad_resid + norm_pull(grad_normed, tokens.astype(single), gains[0:1])
-    dense = dense.reshape(weight_rows, -1)
-    parts = [dense[:, i * model_width : (i + 1) * model_width] for i in range(4)]
-    tail = dense[:, 4 * model_width :]
+    total = lambda held, come: (held.astype(single) + jnp.sum(come.astype(single), axis=0))[None]
+    tail = tail.reshape(weight_rows, TILE)
     return (
         mixed,
         grad_tokens,
-        *parts,
+        *(part.reshape(weight_rows, model_width) for part in (gq, gk, gv, go)),
         tail[:, :expert_count],
         tail[:, expert_count],
         tail[:, expert_count + 1],
         tail[:table_rows, expert_count + 2 : expert_count + 2 + head_count],
-        expert_in_grad,
-        expert_out_grad,
+        total(ka, la),
+        total(kb, lb),
     )
 
 

time: 342 us -> 292 us (0.85)
  Pallas kernels: 290 us -> 269 us
  between operations: 14.2 us -> 0.72 us
  starting transfers between devices: 8.05 us -> 0 us
  other arithmetic: 12.1 us -> 8.61 us
    pallas_call x1, Pallas kernels: 93.7 us -> 68.2 us  [reduce_all(): pl.pallas_call(reduce_kernel, out_shape=(shape((rows, width), single), sh...]
    pallas_call x1, Pallas kernels: 50.5 us -> 69.3 us  [back(): pl.pallas_call(back_kernel, out_shape=(shape((width, 4 * width + TILE), l...]
    pallas_call x1, Pallas kernels: 71.9 us -> 56.9 us  [moe(): pl.pallas_call(moe_kernel, out_shape=(shape(rows_out.shape, low), shape(r...]
    all_to_all x1 -> x0, starting transfers between devices: 7.98 us -> none  [local(): lax.all_to_all(result.reshape(expert_count, capacity, model_width), 'shar...]
    convert_element_type x3 -> x0, other arithmetic: 6.83 us -> none  [the longest x1 2.94 us: local(): lax.psum_scatter(grad_w_in, 'rep', scatter_dimension=1, tiled=True)]
    broadcast_in_dim x0 -> x2, other arithmetic: none -> 5.16 us  [local(): (held.astype(single) + jnp.sum(come.astype(single), axis=0))[None]]
    unnamed x14 -> x24, local copies, waits for them, and re-layouts: 2.98 us -> 6.94 us
  transfers between devices with their start and end apart: 3 -> 0, of which waited for: 0 -> 0; matrix products, arithmetic and copies ran while one was open for 5% -> 0% of each run, Pallas kernels for 42% -> 0%
where the time goes in v3:
time: 292 us; the launch traced here: 291 us
  Pallas kernels  269 us (92%)
  local copies, waits for them, and re-layouts  13.5 us (5%)
  other arithmetic  8.61 us (3%)
    pallas_call x1, Pallas kernels, back(): pl.pallas_call(back_kernel, out_shape=(shape((width, 4 * width + TILE), l...  69.3 us
    pallas_call x1, Pallas kernels, reduce_all(): pl.pallas_call(reduce_kernel, out_shape=(shape((rows, width), single), sh...  68.2 us
    pallas_call x1, Pallas kernels, moe(): pl.pallas_call(moe_kernel, out_shape=(shape(rows_out.shape, low), shape(r...  56.9 us
    pallas_call x1, Pallas kernels, gather_all(): pl.pallas_call(gather_kernel, out_shape=(jax.ShapeDtypeStruct((weights.sh...  39.7 us
    pallas_call x1, Pallas kernels, front(): pl.pallas_call(front_kernel, out_shape=(shape((keys, width), low), shape(...  34.4 us
    unnamed x24, local copies, waits for them, and re-layouts  6.94 us

profile of v3, /device:TPU:0, one launch (start us, length us, event | category | flops | bytes accessed | tf_op | source)
XLA Modules:
  0.0 291.4 jit_solution(17533427617248657682)
XLA Ops:
  0.6 0.7 multiply_add_fusion
  1.3 0.8 copy.38
  2.1 0.7 fusion.3
  2.9 0.6 broadcast_in_dim.27.row_ref
  3.6 0.6 pad.9.small_ref
  4.2 0.8 broadcast_in_dim.32.col_ref
  5.0 1.5 broadcast_in_dim.31.route_ref
  6.5 2.0 pad_maximum_fusion.w_ref
  8.5 39.7 %gather_all.1 = (bf16[4,4,2,4,24,768]{5,4,3,2,1,0:T(8,128)(2,1)}, bf16[1536,768]{1,0:T(8,128)(2,1)}, bf16[4,2,96,128]{3,2,1,0:T(8,128)(2,1)}) custom-call(bf16[4,4,24,768]{3,2,1,0:T(8,128)(2,1)} %pad_maximum_fusion.w_ref, bf16[384,768]{1,0:T(8,128)(2,1)} %tok_hbm.1, bf16[96,128]{1,0:T(8,128)(2,1)} %pad.9.small_ref), custom_call_target="tpu_custom_call" | custom-call | bytes 100000000 | tf_op jit(solution)/shard_map/gather_all/pallas_call | solution.py:774
  48.2 34.4 %front.1 = (bf16[1536,768]{1,0:T(8,128)(2,1)}, bf16[384,768]{1,0:T(8,128)(2,1)}, bf16[1536,768]{1,0:T(8,128)(2,1)}, bf16[1536,768]{1,0:T(8,128)(2,1)}, f32[384,7...) custom-call(bf16[1536,768]{1,0:T(8,128)(2,1)} %get-tuple-element.51., ...), custom_call_target="tpu_custom_call" | custom-call | flops 30000001024 | bytes 20000000 | tf_op jit(solution)/shard_map/front/pallas_call | solution.py:261
  82.7 56.9 %moe.1 = (bf16[4,2,96,768]{3,2,1,0:T(8,128)(2,1)}, bf16[4,2,96,768]{3,2,1,0:T(8,128)(2,1)}, bf16[768,3072]{1,0:T(8,128)(2,1)}, bf16[3072,768]{1,0:T(8,128)(2,1)}, f32[768,128]{1,0:T(8,128)}) custom-call(bf16[4,2,96,768]{3,2,1,0:T(8,128)(2,1)} %bitcast.63, bf16[4,2,96,768]{3,2,1,0:T(8,128)(2,1)} %bitcast.64, bf16[768,128]{1,0:T(8,128)(2,1)} %bitcast.60, ...), custom_call_target="tpu_custom_call" | custom-call | flops 40000000000 | bytes 40000000 | tf_op jit(solution)/shard_map/moe/pallas_call | solution.py:422
  139.6 69.3 %back.1 = (bf16[768,3200]{1,0:T(8,128)(2,1)}, bf16[1024,768]{1,0:T(8,128)(2,1)}, bf16[256,768]{1,0:T(8,128)(2,1)}, f32[384,768]{1,0:T(8,128)}, f32[384,768]{1,0:...) custom-call(bf16[768,768]{1,0:T(8,128)(2,1)} %bitcast.61, ...), custom_call_target="tpu_custom_call" | custom-call | flops 60000002048 | bytes 40000000 | tf_op jit(solution)/shard_map/back/pallas_call | solution.py:639
  208.9 68.2 %reduce_all.1 = (f32[384,768]{1,0:T(8,128)}, bf16[384,768]{1,0:T(8,128)(2,1)}, f32[4,24,768]{2,1,0:T(8,128)}, f32[4,24,768]{2,1,0:T(8,128)}, f32[4,24,768]{2,1,0...) custom-call(f32[8,768]{1,0:T(8,128)} %get-tuple-element.54.gain_ref,, ...), custom_call_target="tpu_custom_call" | custom-call | bytes 200000000 | tf_op jit(solution)/shard_map/reduce_all/pallas_call | solution.py:975
  277.2 1.6 slice_reduce_fusion
  278.7 1.3 slice.19
  280.1 1.5 copy.43
  281.5 3.5 %fusion.1 = f32[1,192,3072]{2,1,0:T(8,128)} fusion(bf16[192,3072]{1,0:T(8,128)(2,1)} %get-tuple-element.86, bf16[1,192,3072]{2,1,0:T(8,128)(2,1)} %get-tuple-element.87), kind=kLoop, calls=%fused_computation.3 | loop fusion | flops 1769472 | bytes 4718592 | tf_op jit(solution)/shard_map/broadcast_in_dim | solution.py:1070
  285.0 1.7 fusion
  286.7 0.8 copy.50
  287.5 1.0 copy.51
  288.6 0.7 copy.52
  289.3 0.7 copy.53
  290.0 0.7 copy.54
  290.7 0.7 copy.55
  (17 shorter events, 0.1 us)
Async XLA Ops:
  281.5 3.5 %copy-start.1 = (bf16[768,768]{1,0:T(8,128)(2,1)S(1)}, bf16[768,768]{1,0:T(8,128)(2,1)}, u32[]{:S(2)}) copy-start(bf16[768,768]{1,0:T(8,128)(2,1)} %get-tuple-element.88) | copy-start | bytes 3538948
  281.5 3.5 %copy-start.2 = (bf16[1,768,768]{2,1,0:T(8,128)(2,1)S(1)}, bf16[1,768,768]{2,1,0:T(8,128)(2,1)}, u32[]{:S(2)}) copy-start(bf16[1,768,768]{2,1,0:T(8,128)(2,1)} %get-tuple-element.89) | copy-start | bytes 3538948
  285.0 1.7 copy-start.3
  285.0 2.5 copy-start
  286.7 1.9 copy-start.7
  286.7 2.6 copy-start.6
  286.7 3.3 %copy-start.5 = (f32[4,24,768]{2,1,0:T(8,128)S(1)}, f32[4,24,768]{2,1,0:T(8,128)}, u32[]{:S(2)}) copy-start(f32[4,24,768]{2,1,0:T(8,128)} %get-tuple-element.83) | copy-start | bytes 884740
  286.7 4.0 %copy-start.4 = (f32[4,24,768]{2,1,0:T(8,128)S(1)}, f32[4,24,768]{2,1,0:T(8,128)}, u32[]{:S(2)}) copy-start(f32[4,24,768]{2,1,0:T(8,128)} %get-tuple-element.84) | copy-start | bytes 884740

commit v4 on v3

--- a/solution.py
+++ b/solution.py
@@ -129,32 +129,100 @@
 
 
 def front_kernel(
-    every_ref, tok_ref, w_ref, small_ref, bucket_ref, route_ref, row_ref, cot_ref,
-    n_ref, q_ref, k_ref, v_ref, o_ref, lse_ref, rev_ref, mid_ref, gate_ref, gain_ref, x_ref, gin_ref,
-    tiles, vt, sp, sl, ot, gbuf, gs, gr, loc,
+    ints_ref, bucket_ref, cot_ref, wq_hbm, wk_hbm, wv_hbm, wo_hbm, tok_hbm, little_hbm,
+    n_ref, q_ref, k_ref, v_ref, o_ref, lse_ref, rev_ref, mid_ref, gate_ref, col_ref, gain_ref, x_ref, gin_hbm,
+    w_hbm, every_hbm, small_hbm,
+    tiles, vt, sp, sl, ot, gbuf, w_ref, every_ref, small_ref, tok_ref, shard_w, little,
+    gs, gr, loc, wz_s, wz_r, tz_s, tz_r, sz_s, sz_r, wr_s, wr_r, wt_s, wt_r, tt_s, tt_r, st_s, st_r, et_s, et_r,
 ):
-    shard_id = lax.axis_index("shard")
-    shards = lax.axis_size("shard")
+    rep, chip, core, chips, quarter = places()
+    along, across, twin = peer_lists()
+    shards = chips * 2
+    shard_id = chip * 2 + core
     rows, width = tok_ref.shape
     experts = shards
     blocks = every_ref.shape[0] // TILE - 4
     half = TILE // 2
     heads_held = rev_ref.shape[0]
-
-    rep = lax.axis_index("rep")
+    lines = shard_w.shape[1]
+    rest_rows = rows - PR_DEV
+    prompt_len = blocks * TILE
     others = [(rep, (shard_id + k) % shards) for k in range(1, shards)]
+
+    def w_rows(source, side):
+        return pl.ds(pl.multiple_of((source * 2 + side) * lines, lines), lines)
+
+    def t_rows(source, side):
+        return every_ref.at[pl.ds(pl.multiple_of((source * 2 + side) * PR_DEV, PR_DEV), PR_DEV)]
+
+    loads = [
+        pltpu.make_async_copy(source, shard_w.at[i], loc.at[i])
+        for i, source in enumerate((wq_hbm, wk_hbm, wv_hbm, wo_hbm))
+    ] + [pltpu.make_async_copy(tok_hbm, tok_ref, loc.at[4]), pltpu.make_async_copy(little_hbm, little, loc.at[5])]
+    for copy in loads:
+        copy.start()
+    greeted = [twin] + along
+    for device in across + [(rep, (chip + k) % chips * 2 + 1 - core) for k in range(1, chips)]:
+        greeted.append(device)
+    greet(greeted)
+    started = []
+
+    def go(source, target, sems, device):
+        copy = send(source, target, sems, device)
+        copy.start()
+        started.append(copy)
+
+    def landed(piece, sems):
+        send(piece, piece, sems, twin).wait_recv()
+
+    for copy in loads:
+        copy.wait()
+    mine = w_rows(chip, core)
+    prompt, rest = tok_ref.at[pl.ds(0, PR_DEV)], tok_ref.at[pl.ds(PR_DEV, rest_rows)]
+    for k, device in enumerate(along):
+        go(shard_w.at[quarter], w_ref.at[quarter, mine], (wz_s.at[k], wz_r.at[k]), device)
+        go(little, small_ref.at[mine], (sz_s.at[k], sz_r.at[k]), device)
+    go(little, small_ref.at[mine], (st_s.at[0], st_r.at[0]), twin)
+    go(rest, every_ref.at[pl.ds(prompt_len, rest_rows)], (et_s.at[0], et_r.at[0]), twin)
+    go(prompt, t_rows(chip, core), (tt_s.at[0], tt_r.at[0]), twin)
+    go(shard_w, w_ref.at[:, mine], (wt_s.at[0], wt_r.at[0]), twin)
+    w_ref[:, mine, :] = shard_w[...]
+    small_ref[mine, :] = little[...]
+    every_ref[pl.ds(pl.multiple_of(shard_id * PR_DEV, PR_DEV), PR_DEV), :] = tok_ref[:PR_DEV, :]
+    every_ref[prompt_len + rest_rows :, :] = tok_ref[PR_DEV:, :]
+    ints = ints_ref[...].astype(single).T
+    route_col = ints[:, 0:1].astype(jnp.int32)
+    col_ref[...] = jnp.broadcast_to(ints[:, 1:2].astype(jnp.int32), col_ref.shape)
     slots = lax.broadcasted_iota(jnp.int32, (x_ref.shape[0], rows), 0)
-    place = (slots == row_ref[0:1, :]).astype(low)
+    place = (slots == ints_ref[1:2, :]).astype(low)
     gbuf[...] = nn(place, cot_ref[...]).astype(low).reshape(gbuf.shape)
-    greet(others)
-    mine = pltpu.make_async_copy(gbuf.at[shard_id], gin_ref.at[shard_id], loc)
-    mine.start()
-    sent = [
-        send(gbuf.at[device[1]], gin_ref.at[shard_id], (gs.at[k], gr.at[k]), device)
-        for k, device in enumerate(others)
-    ]
-    for copy in sent:
-        copy.start()
+    own_g = pltpu.make_async_copy(gbuf.at[shard_id], gin_hbm.at[shard_id], loc.at[6])
+    own_g.start()
+
+    for k in range(1, chips):
+        source = (chip + chips - k) % chips
+        piece = w_ref.at[quarter, w_rows(source, core)]
+        landed(piece, (wz_s.at[k - 1], wz_r.at[k - 1]))
+        for j, device in enumerate(across):
+            go(piece, piece, (wr_s.at[k - 1, j], wr_r.at[k - 1, j]), device)
+        go(prompt, t_rows(chip, core), (tz_s.at[k - 1], tz_r.at[k - 1]), along[k - 1])
+    for k in range(1, chips):
+        source = (chip + chips - k) % chips
+        piece = small_ref.at[w_rows(source, core)]
+        landed(piece, (sz_s.at[k - 1], sz_r.at[k - 1]))
+        go(piece, piece, (st_s.at[k], st_r.at[k]), twin)
+    for k in range(1, chips):
+        source = (chip + chips - k) % chips
+        piece = t_rows(source, core)
+        landed(piece, (tz_s.at[k - 1], tz_r.at[k - 1]))
+        go(piece, piece, (tt_s.at[k], tt_r.at[k]), twin)
+    for k, device in enumerate(others):
+        go(gbuf.at[device[1]], gin_hbm.at[shard_id], (gs.at[k], gr.at[k]), device)
+    for k in range(chips):
+        source = (chip + chips - k) % chips
+        landed(small_ref.at[w_rows(source, 1 - core)], (st_s.at[k], st_r.at[k]))
+    writes = [pltpu.make_async_copy(small_ref, small_hbm, loc.at[7])]
+    writes[0].start()
 
     small_t = small_ref[...].astype(single).T
     gain_attn = small_t[experts : experts + 1]
@@ -169,14 +237,37 @@
     table_t = small_t[experts + 2 : experts + 2 + heads_held].astype(low)
     rev_ref[...] = nn(table_t, hot)
 
+    for k in range(chips):
+        source = (chip + chips - k) % chips
+        landed(t_rows(source, 1 - core), (tt_s.at[k], tt_r.at[k]))
+    landed(every_ref.at[pl.ds(prompt_len, rest_rows)], (et_s.at[0], et_r.at[0]))
+    writes.append(pltpu.make_async_copy(every_ref, every_hbm, loc.at[8]))
+    writes[-1].start()
+
     @pl.loop(0, every_ref.shape[0] // SPAN)
-    def project(part):
+    def scale(part):
         span = pl.ds(pl.multiple_of(part * SPAN, SPAN), SPAN)
         values = every_ref[span, :].astype(single)
-        normed = (values * inverse_rms(values) * gain_attn).astype(low)
-        n_ref[span, :] = normed
-        k_ref[span, :] = nn(normed, w_ref[1]).astype(low)
-        v_ref[span, :] = nn(normed, w_ref[2]).astype(low)
+        n_ref[span, :] = (values * inverse_rms(values) * gain_attn).astype(low)
+
+    for k in range(1, chips):
+        source = (chip + chips - k) % chips
+        for j in range(1, QUARTERS):
+            piece = w_ref.at[(quarter + QUARTERS - j) % QUARTERS, w_rows(source, core)]
+            landed(piece, (wr_s.at[k - 1, j - 1], wr_r.at[k - 1, j - 1]))
+        piece = w_ref.at[:, w_rows(source, core)]
+        go(piece, piece, (wt_s.at[k], wt_r.at[k]), twin)
+    for k in range(chips):
+        source = (chip + chips - k) % chips
+        landed(w_ref.at[:, w_rows(source, 1 - core)], (wt_s.at[k], wt_r.at[k]))
+    writes.append(pltpu.make_async_copy(w_ref, w_hbm, loc.at[9]))
+    writes[-1].start()
+
+    @pl.loop(0, every_ref.shape[0] // (2 * SPAN))
+    def project(part):
+        span = pl.ds(pl.multiple_of(part * 2 * SPAN, 2 * SPAN), 2 * SPAN)
+        k_ref[span, :] = nn(n_ref[span, :], w_ref[1]).astype(low)
+        v_ref[span, :] = nn(n_ref[span, :], w_ref[2]).astype(low)
 
     own = pl.ds(pl.multiple_of(shard_id * TILE, TILE), TILE)
     normed = jnp.concatenate([n_ref[own, :], n_ref[(blocks + 2) * TILE :, :]], axis=0)
@@ -234,14 +325,15 @@
     mid_low = (resid_mid * inverse_rms(resid_mid) * gain_moe).astype(low)
     probs = router_softmax(mid_low, small_ref[...], experts)
     lanes = lax.broadcasted_iota(jnp.int32, probs.shape, 1)
-    gate = jnp.sum(jnp.where(lanes == route_ref[...], probs, 0.0), axis=1, keepdims=True)
+    gate = jnp.sum(jnp.where(lanes == route_col, probs, 0.0), axis=1, keepdims=True)
     gate_ref[...] = jnp.broadcast_to(gate, gate_ref.shape)
     x_ref[...] = nn(place, mid_low).astype(low)
-    mine.wait()
+    own_g.wait()
     for k in range(shards - 1):
-        piece = gin_ref.at[(shard_id + shards - k - 1) % shards]
-        send(piece, piece, (gs.at[k], gr.at[k]), others[0]).wait_recv()
-    for copy in sent:
+        landed(gin_hbm.at[(shard_id + shards - k - 1) % shards], (gs.at[k], gr.at[k]))
+    for copy in writes:
+        copy.wait()
+    for copy in started:
         copy.wait_send()
 
 
@@ -253,35 +345,40 @@
     return powers / jnp.sum(powers, axis=1, keepdims=True)
 
 
-def front(every_tok, tokens, weights, small, bucket_row, route_col, row_slots, cotangent, slot_count):
+def front(ints, bucket_row, cotangent, weights, tokens, small, slot_count):
     rows, width = tokens.shape
-    keys = every_tok.shape[0]
     shards = lax.axis_size("shard")
+    chips, count = shards // 2, shards // 2 - 1
+    keys = shards * PR_DEV + 2 * (rows - PR_DEV)
+    lines = small.shape[0]
     shape = jax.ShapeDtypeStruct
+    sem = pltpu.SemaphoreType.DMA
+    vm = pltpu.VMEM
     return pl.pallas_call(
         front_kernel,
         out_shape=(
             shape((keys, width), low), shape((rows, width), low), shape((keys, width), low),
             shape((keys, width), low), shape((rows, width), single), shape((16, rows), single),
             shape((16, 4 * TILE), single), shape((rows, width), single), shape((rows, TILE), single),
-            shape((8, width), single), shape((slot_count, width), low),
-            shape((shards, slot_count // shards, width), low),
+            shape((rows, TILE), jnp.int32), shape((8, width), single), shape((slot_count, width), low),
+            shape((shards, slot_count // shards, width), low), shape((4, width, width), low),
+            shape((keys, width), low), shape((width, TILE), low),
         ),
-        in_specs=[in_vmem] * 8,
-        out_specs=(in_vmem,) * 11 + (anywhere,),
+        in_specs=[in_vmem] * 3 + [anywhere] * 6,
+        out_specs=(in_vmem,) * 12 + (anywhere,) * 4,
         scratch_shapes=[
-            pltpu.VMEM((tile_kinds, TILE, TILE), single),
-            pltpu.VMEM((TILE, keys), low),
-            pltpu.VMEM((keys - 2 * SPAN, rows), single),
-            pltpu.VMEM((2 * SPAN, rows - TILE), single),
-            pltpu.VMEM((TILE, rows), single),
-            pltpu.VMEM((shards, slot_count // shards, width), low),
-            pltpu.SemaphoreType.DMA((shards - 1,)), pltpu.SemaphoreType.DMA((shards - 1,)), pltpu.SemaphoreType.DMA,
+            vm((tile_kinds, TILE, TILE), single), vm((TILE, keys), low), vm((keys - 2 * SPAN, rows), single),
+            vm((2 * SPAN, rows - TILE), single), vm((TILE, rows), single),
+            vm((shards, slot_count // shards, width), low), vm((4, width, width), low), vm((keys, width), low),
+            vm((width, TILE), low), vm((rows, width), low), vm((4, lines, width), low), vm((lines, TILE), low),
+            sem((shards - 1,)), sem((shards - 1,)), sem((10,)), sem((count,)), sem((count,)), sem((count,)),
+            sem((count,)), sem((count,)), sem((count,)), sem((count, 3)), sem((count, 3)), sem((chips,)), sem((chips,)),
+            sem((chips,)), sem((chips,)), sem((chips,)), sem((chips,)), sem((1,)), sem((1,)),
         ],
         compiler_params=pltpu.CompilerParams(collective_id=2, has_side_effects=True, vmem_limit_bytes=vmem_cap),
         cost_estimate=pl.CostEstimate(flops=30_000_000_000, bytes_accessed=20_000_000, transcendentals=8_000_000),
         name="front",
-    )(every_tok, tokens, weights, small, bucket_row, route_col, row_slots, cotangent)
+    )(ints, bucket_row, cotangent, *weights, tokens, small)
 
 
 def moe_kernel(
@@ -444,9 +541,9 @@
 def back_kernel(
     back_ref, col_ref, mid_ref, cot_ref, gain_ref, q_ref, k_ref, v_ref, o_ref,
     lse_ref, rev_ref, bucket_ref, rg_ref, every_hbm, w_hbm, n_hbm, out_hbm, gwin_hbm, gwout_hbm,
-    dense_ref, p_ref, e_ref, own_ref, gres_ref, ret_hbm, ra_hbm, rb_hbm,
+    dense_ref, p_ref, e_ref, own_ref, gres_ref, zo_ref, ret_hbm, ra_hbm, rb_hbm,
     tiles, sums, diag, kt, dqt, far_sums, dk_sum, dv_sum, g_ref, dq_ref, dk_ref, dv_ref, attn_gain,
-    every_ref, w_ref, n_ref, loc, xs, xr, as_, ar, bs, br,
+    every_ref, w_ref, n_ref, o_grad, o_half, o_sum, o_in, loc, xs, xr, as_, ar, bs, br, os_, or_, oz_s, oz_r,
 ):
     shard_id = lax.axis_index("shard")
     shards = lax.axis_size("shard")
@@ -456,6 +553,8 @@
     experts = shards
     heads_held = rev_ref.shape[0]
     rep, slow, fast, slows, fasts = rep_places()
+    _, chip, core, chips, _ = places()
+    along, _, twin = peer_lists()
     loads = [
         pltpu.make_async_copy(w_hbm.at[3], w_ref.at[3], loc.at[0]),
         pltpu.make_async_copy(w_hbm.at[pl.ds(0, 3)], w_ref.at[pl.ds(0, 3)], loc.at[1]),
@@ -488,7 +587,7 @@
     flip = (tile_rows + tile_cols == TILE - 1).astype(single)
 
     slots = lax.broadcasted_iota(jnp.int32, (rows, back_ref.shape[0]), 1)
-    grad_mid = nn((slots == col_ref[...]).astype(low), back_ref[...])
+    grad_mid = nn((slots == col_ref[:, 0:1]).astype(low), back_ref[...])
     resid_mid = mid_ref[...]
     grad_gain_moe = jnp.sum(grad_mid * resid_mid * inverse_rms(resid_mid), axis=0, keepdims=True)
     grad_resid = cot_ref[...].astype(single) + norm_pull(grad_mid, resid_mid, gain_ref[1:2, :])
@@ -496,7 +595,14 @@
     grad_attn = grad_resid.astype(low)
     loads[0].wait()
     g_ref[...] = nt(grad_attn, w_ref[3]).astype(low)
-    dense_ref[:, 3 * width : 4 * width] = tn(o_ref[...].astype(low), grad_attn).astype(low)
+    o_grad[...] = tn(o_ref[...].astype(low), grad_attn).reshape(o_grad.shape).astype(low)
+    o_halves = [send(o_grad.at[2 * k + 1 - core], o_half.at[k], (os_.at[k], or_.at[k]), twin) for k in range(chips)]
+    o_sends = [
+        send(o_sum.at[(chip + k + 1) % chips], o_in.at[k], (oz_s.at[k], oz_r.at[k]), device)
+        for k, device in enumerate(along)
+    ]
+    for copy in o_halves:
+        copy.start()
 
     @pl.loop(0, width // TILE)
     def pair_loop(pair):
@@ -557,6 +663,14 @@
             )
         dq_ref[:, cols] = (dqt[...].T * 0.125).astype(low)
 
+        @pl.when(pair == 0)
+        def _():
+            for k in range(chips):
+                o_halves[k].wait_recv()
+                o_sum[k] = (o_grad[2 * k + core].astype(single) + o_half[k].astype(single)).astype(low)
+            for copy in o_sends:
+                copy.start()
+
     lanes = lax.broadcasted_iota(jnp.int32, (heads_held, 4 * TILE), 1)
     before = jnp.sum(far_sums[:, :TILE], axis=1, keepdims=True)
     after = jnp.sum(far_sums[:, TILE:], axis=1, keepdims=True)
@@ -610,7 +724,14 @@
         ],
         axis=0,
     )
-    dense_ref[:, 4 * width :] = (small_t.T + rg_ref[...]).astype(low)
+    dense_ref[:, 3 * width :] = (small_t.T + rg_ref[...]).astype(low)
+    o_total = o_sum[chip].astype(single)
+    for k in range(chips - 1):
+        o_sends[k].wait_recv()
+        o_total = o_total + o_in[k].astype(single)
+    zo_ref[...] = o_total.astype(low)
+    for copy in o_halves + o_sends:
+        copy.wait_send()
     for k in range(shards - 1):
         piece = ret_hbm.at[(shard_id + shards - k - 1) % shards]
         send(piece, piece, (xs.at[k], xr.at[k]), others[0]).wait_recv()
@@ -630,6 +751,7 @@
     count = keys.shape[0]
     shards = result.shape[0]
     slows, fasts = gwin.shape[:2]
+    chips, lines = shards // 2, width // shards
     shape = jax.ShapeDtypeStruct
     pairs = pltpu.SemaphoreType.DMA
     args = (
@@ -639,12 +761,13 @@
     return pl.pallas_call(
         back_kernel,
         out_shape=(
-            shape((width, 4 * width + TILE), low), shape((count - 2 * SPAN, width), low), shape((SPAN, width), low),
-            shape((rows, width), single), shape((rows, width), single), shape(result.shape, low),
+            shape((width, 3 * width + TILE), low), shape((count - 2 * SPAN, width), low), shape((SPAN, width), low),
+            shape((rows, width), single), shape((rows, width), single), shape((lines, width), low),
+            shape(result.shape, low),
             shape((fasts - 1, slows) + gwin.shape[2:], low), shape((slows - 1, fasts) + gwout.shape[2:], low),
         ),
         in_specs=[in_vmem] * 13 + [anywhere] * 6,
-        out_specs=(in_vmem,) * 5 + (anywhere,) * 3,
+        out_specs=(in_vmem,) * 6 + (anywhere,) * 3,
         scratch_shapes=[
             pltpu.VMEM((tile_kinds, TILE, TILE), single), pltpu.VMEM((tile_kinds, TILE, TILE), single),
             pltpu.VMEM((16, 4 * TILE), single), pltpu.VMEM((TILE, count), low), pltpu.VMEM((TILE, rows), single),
@@ -652,8 +775,11 @@
             pltpu.VMEM((rows, width), low), pltpu.VMEM((rows, width), low), pltpu.VMEM((count, width), low),
             pltpu.VMEM((count, width), low), pltpu.VMEM((8, width), single),
             pltpu.VMEM(every_tok.shape, low), pltpu.VMEM(weights.shape, low), pltpu.VMEM(normed.shape, low),
+            pltpu.VMEM((shards, lines, width), low), pltpu.VMEM((chips, lines, width), low),
+            pltpu.VMEM((chips, lines, width), low), pltpu.VMEM((chips - 1, lines, width), low),
             pairs((5,)), pairs((shards - 1,)), pairs((shards - 1,)), pairs((fasts - 1,)), pairs((fasts - 1,)),
-            pairs((slows - 1,)), pairs((slows - 1,)),
+            pairs((slows - 1,)), pairs((slows - 1,)), pairs((chips,)), pairs((chips,)), pairs((chips - 1,)),
+            pairs((chips - 1,)),
         ],
         compiler_params=pltpu.CompilerParams(collective_id=4, has_side_effects=True, vmem_limit_bytes=vmem_cap),
         cost_estimate=pl.CostEstimate(flops=60_000_000_000, bytes_accessed=40_000_000, transcendentals=8_000_000),
@@ -696,101 +822,6 @@
     )
 
 
-def gather_kernel(
-    w_ref, tok_ref, small_ref, wg_ref, tg_ref, sg_ref,
-    wz_s, wz_r, tz_s, tz_r, sz_s, sz_r, wr_s, wr_r, wt_s, wt_r, tt_s, tt_r, et_s, et_r, loc,
-):
-    rep, chip, core, chips, quarter = places()
-    along, across, twin = peer_lists()
-    rest_rows = tok_ref.shape[0] - PR_DEV
-    prompt_len = chips * 2 * PR_DEV
-    prompt = tok_ref.at[pl.ds(0, PR_DEV)]
-    rest = tok_ref.at[pl.ds(PR_DEV, rest_rows)]
-    near_rows = tg_ref.at[pl.ds(prompt_len, rest_rows)]
-
-    def tok_rows(source, side):
-        return tg_ref.at[pl.ds(pl.multiple_of((source * 2 + side) * PR_DEV, PR_DEV), PR_DEV)]
-
-    mine = tok_rows(chip, core)
-    own = [
-        pltpu.make_async_copy(w_ref, wg_ref.at[:, chip, core], loc.at[0]),
-        pltpu.make_async_copy(prompt, mine, loc.at[1]),
-        pltpu.make_async_copy(small_ref, sg_ref.at[chip, core], loc.at[2]),
-        pltpu.make_async_copy(rest, tg_ref.at[pl.ds(prompt_len + rest_rows, rest_rows)], loc.at[3]),
-    ]
-    for copy in own:
-        copy.start()
-    greet(along + across + [twin])
-    started = []
-
-    def go(copy):
-        copy.start()
-        started.append(copy)
-
-    for k, device in enumerate(along):
-        go(send(w_ref.at[:, quarter], wg_ref.at[:, chip, core, quarter], (wz_s.at[k], wz_r.at[k]), device))
-        go(send(small_ref, sg_ref.at[chip, core], (sz_s.at[k], sz_r.at[k]), device))
-    go(send(rest, near_rows, (et_s.at[0], et_r.at[0]), twin))
-    go(send(prompt, mine, (tt_s.at[0], tt_r.at[0]), twin))
-    go(send(w_ref, wg_ref.at[:, chip, core], (wt_s.at[0], wt_r.at[0]), twin))
-    for k in range(1, chips):
-        source = (chip + chips - k) % chips
-        piece = wg_ref.at[:, source, core, quarter]
-        send(piece, piece, (wz_s.at[k - 1], wz_r.at[k - 1]), twin).wait_recv()
-        for j, device in enumerate(across):
-            go(send(piece, piece, (wr_s.at[k - 1, j], wr_r.at[k - 1, j]), device))
-        go(send(prompt, mine, (tz_s.at[k - 1], tz_r.at[k - 1]), along[k - 1]))
-    for k in range(1, chips):
-        source = (chip + chips - k) % chips
-        for j in range(1, QUARTERS):
-            piece = wg_ref.at[:, source, core, (quarter + QUARTERS - j) % QUARTERS]
-            send(piece, piece, (wr_s.at[k - 1, j - 1], wr_r.at[k - 1, j - 1]), twin).wait_recv()
-        row = wg_ref.at[:, source, core]
-        go(send(row, row, (wt_s.at[k], wt_r.at[k]), twin))
-        theirs = tok_rows(source, core)
-        send(theirs, theirs, (tz_s.at[k - 1], tz_r.at[k - 1]), twin).wait_recv()
-        go(send(theirs, theirs, (tt_s.at[k], tt_r.at[k]), twin))
-        send(small_ref, sg_ref.at[source, core], (sz_s.at[k - 1], sz_r.at[k - 1]), twin).wait_recv()
-    for copy in own:
-        copy.wait()
-    go(send(sg_ref.at[:, core], sg_ref.at[:, core], (et_s.at[1], et_r.at[1]), twin))
-    send(rest, near_rows, (et_s.at[0], et_r.at[0]), twin).wait_recv()
-    for k in range(chips):
-        source = (chip + chips - k) % chips
-        row = wg_ref.at[:, source, 1 - core]
-        send(row, row, (wt_s.at[k], wt_r.at[k]), twin).wait_recv()
-        theirs = tok_rows(source, 1 - core)
-        send(theirs, theirs, (tt_s.at[k], tt_r.at[k]), twin).wait_recv()
-    send(sg_ref.at[:, core], sg_ref.at[:, 1 - core], (et_s.at[1], et_r.at[1]), twin).wait_recv()
-    for copy in started:
-        copy.wait_send()
-
-
-def gather_all(weights, tokens, small):
-    chips = lax.axis_size("shard") // 2
-    width = tokens.shape[1]
-    pairs = pltpu.SemaphoreType.DMA
-    count = chips - 1
-    return pl.pallas_call(
-        gather_kernel,
-        out_shape=(
-            jax.ShapeDtypeStruct((weights.shape[0], chips, 2) + weights.shape[1:], weights.dtype),
-            jax.ShapeDtypeStruct((2 * chips * PR_DEV + 2 * (tokens.shape[0] - PR_DEV), width), tokens.dtype),
-            jax.ShapeDtypeStruct((chips, 2) + small.shape, small.dtype),
-        ),
-        in_specs=[anywhere] * 3,
-        out_specs=(anywhere,) * 3,
-        scratch_shapes=[
-            pairs((count,)), pairs((count,)), pairs((count,)), pairs((count,)), pairs((count,)), pairs((count,)),
-            pairs((count, 3)), pairs((count, 3)), pairs((chips,)), pairs((chips,)), pairs((chips,)), pairs((chips,)),
-            pairs((2,)), pairs((2,)), pairs((4,)),
-        ],
-        compiler_params=pltpu.CompilerParams(collective_id=0, has_side_effects=True),
-        cost_estimate=pl.CostEstimate(flops=0, bytes_accessed=100_000_000, transcendentals=0),
-        name="gather_all",
-    )(weights, tokens, small)
-
-
 def rep_places():
     rep, reps = lax.axis_index("rep"), lax.axis_size("rep")
     fasts = QUARTERS if reps % (QUARTERS * QUARTERS) == 0 else 2
@@ -799,11 +830,11 @@
 
 def reduce_kernel(
     gain_ref, col_ref, d_hbm, p_hbm, e_hbm, own_hbm, gres_hbm, tok_hbm, mid_hbm, gate_hbm, ret_hbm,
-    gwin_hbm, ra_hbm, gwout_hbm, rb_hbm,
-    gt_ref, mix_ref, dq_ref, dk_ref, dv_ref, do_ref, sm_ref, ka_ref, la_hbm, kb_ref, lb_hbm,
+    gwin_hbm, ra_hbm, gwout_hbm, rb_hbm, zo_hbm,
+    gt_ref, mix_ref, gathered_ref, ka_ref, la_hbm, kb_ref, lb_hbm,
     d_own, half, hr, hz, tr, mr, cr, cz, zs, tz, last, above_in, gathered,
     p_own, p_half, p_sum, p_in, e_in, own, gres, tok, mid, gate, ret,
-    a_own, a_in, a_sum, b_own, b_in, b_sum,
+    a_own, a_in, a_sum, b_own, b_in, b_sum, zo,
     loc, ps_s, ps_r, ds_s, ds_r, pz_s, pz_r, rr_s, rr_r, rz_s, rz_r, zz_s, zz_r, zr_s, zr_r, dh_s, dh_r,
     da_s, da_r, ea_s, ea_r, eb_s, eb_r,
 ):
@@ -840,7 +871,7 @@
     halves = [load(p_hbm.at[:, core], p_own, 4), load(d_hbm.at[:, core], d_own, 5)]
     rest = [
         load(ret_hbm, ret, 6), load(mid_hbm, mid, 7), load(gate_hbm, gate, 8), load(own_hbm, own, 9),
-        load(gres_hbm, gres, 10), load(tok_hbm, tok, 11),
+        load(gres_hbm, gres, 10), load(tok_hbm, tok, 11), load(zo_hbm, zo, 12),
     ]
     greets = [twin] + along
     for device in across + beside + beyond + above:
@@ -889,7 +920,7 @@
     for copy in rest:
         copy.wait()
     slots = lax.broadcasted_iota(jnp.int32, (tok.shape[0], ret.shape[0]), 1)
-    chosen = nn((slots == col_ref[...]).astype(low), ret[...])
+    chosen = nn((slots == col_ref[:, 0:1]).astype(low), ret[...])
     mix_ref[...] = (mid[...] + gate[:, 0:1] * chosen).astype(low)
     ka_ref[...] = a_sum[slow]
     kb_ref[...] = b_sum[fast]
@@ -919,7 +950,7 @@
         total = wide(hz[chip, t])
         for k in range(chips - 1):
             total = total + wide(cz[k, t])
-        zs[t] = total.astype(low)
+        zs[t] = jnp.concatenate([total.astype(low), zo[t]], axis=1)
     for j, device in enumerate(across):
         go(zs.at[(quarter + j + 1) % QUARTERS], tz.at[j], (zr_s.at[j], zr_r.at[j]), device)
     for k in range(chips - 1):
@@ -947,9 +978,7 @@
         go(gathered.at[quarter], gathered.at[quarter], (da_s.at[j], da_r.at[j]), device)
     for j in range(QUARTERS - 1):
         landed(gathered.at[(quarter + QUARTERS - j - 1) % QUARTERS], (da_s.at[j], da_r.at[j]))
-    for i, ref in enumerate((dq_ref, dk_ref, dv_ref, do_ref)):
-        ref[...] = wide(gathered[:, :, i * width : (i + 1) * width])
-    sm_ref[...] = wide(gathered[:, :, 4 * width :])
+    gathered_ref[...] = gathered[...]
     for j in range(slows - 1):
         landed(la_hbm.at[j], (ea_s.at[j], ea_r.at[j]))
     for j in range(fasts - 1):
@@ -958,45 +987,43 @@
         copy.wait_send()
 
 
-def reduce_all(gains, col_slots, dense, prompt_part, near_part, own, gres, tokens, mid, gate, returned, gwin, ra, gwout, rb):
+def reduce_all(gains, col_slots, dense, prompt_part, near_part, own, gres, tokens, mid, gate, returned, gwin, ra, gwout, rb, zo):
     chips = lax.axis_size("shard") // 2
     classes = lax.axis_size("rep") // QUARTERS
     slows, fasts = gwin.shape[:2]
     rows, width = mid.shape
     lines, lanes = dense.shape[3:]
-    cut = 2 * width
+    cut, full = 2 * width, 4 * width + TILE
     shape = jax.ShapeDtypeStruct
     sem = pltpu.SemaphoreType.DMA
     vm = pltpu.VMEM
     count, others = chips - 1, QUARTERS - 1
     ours = prompt_part.shape[2:]
     extra = max(classes - 1, 1)
-    args = (gains, col_slots, dense, prompt_part, near_part, own, gres, tokens, mid, gate, returned, gwin, ra, gwout, rb)
+    args = (gains, col_slots, dense, prompt_part, near_part, own, gres, tokens, mid, gate, returned, gwin, ra, gwout, rb, zo)
     return pl.pallas_call(
         reduce_kernel,
         out_shape=(
             shape((rows, width), single), shape((rows, width), low),
-            shape((QUARTERS, lines, width), single), shape((QUARTERS, lines, width), single),
-            shape((QUARTERS, lines, width), single), shape((QUARTERS, lines, width), single),
-            shape((QUARTERS, lines, TILE), single),
+            shape((QUARTERS, lines, full), low),
             shape(gwin.shape[2:], low), shape((slows - 1,) + gwin.shape[2:], low),
             shape(gwout.shape[2:], low), shape((fasts - 1,) + gwout.shape[2:], low),
         ),
-        in_specs=[in_vmem] * 2 + [anywhere] * 13,
-        out_specs=(in_vmem,) * 8 + (anywhere, in_vmem, anywhere),
+        in_specs=[in_vmem] * 2 + [anywhere] * 14,
+        out_specs=(in_vmem,) * 4 + (anywhere, in_vmem, anywhere),
         scratch_shapes=[
             vm((chips, QUARTERS, lines, lanes), low), vm((chips, QUARTERS, lines, lanes), low),
             vm((QUARTERS, chips, lines, cut), low), vm((chips, QUARTERS, lines, lanes - cut), low),
             vm((others, chips, lines, cut), low), vm((chips, lines, cut), low), vm((count, lines, cut), low),
-            vm((count, QUARTERS, lines, lanes - cut), low), vm((QUARTERS, lines, lanes - cut), low),
-            vm((others, lines, lanes - cut), low), vm((lines, lanes), low), vm((extra, lines, lanes), low),
-            vm((QUARTERS, lines, lanes), low),
+            vm((count, QUARTERS, lines, lanes - cut), low), vm((QUARTERS, lines, full - cut), low),
+            vm((others, lines, full - cut), low), vm((lines, full), low), vm((extra, lines, full), low),
+            vm((QUARTERS, lines, full), low),
             vm((chips,) + ours, low), vm((chips,) + ours, low), vm((chips,) + ours, low), vm((count,) + ours, low),
             vm(near_part.shape, low), vm((rows, width), single), vm((rows, width), single), vm((rows, width), low),
             vm((rows, width), single), vm(gate.shape, single), vm(returned.shape, low),
             vm((slows,) + gwin.shape[2:], low), vm(ra.shape, low), vm((slows,) + gwin.shape[2:], low),
             vm((fasts,) + gwout.shape[2:], low), vm(rb.shape, low), vm((fasts,) + gwout.shape[2:], low),
-            sem((12,)), sem((2,)), sem((2,)), sem((chips,)), sem((chips,)), sem((count,)), sem((count,)),
+            vm(zo.shape, low), sem((13,)), sem((2,)), sem((2,)), sem((chips,)), sem((chips,)), sem((count,)), sem((count,)),
             sem((others,)), sem((others,)), sem((count,)), sem((count,)), sem((count,)), sem((count,)),
             sem((others,)), sem((others,)), sem((extra,)), sem((extra,)), sem((others,)), sem((others,)),
             sem((slows - 1,)), sem((slows - 1,)), sem((fasts - 1,)), sem((fasts - 1,)),
@@ -1005,6 +1032,61 @@
         cost_estimate=pl.CostEstimate(flops=0, bytes_accessed=200_000_000, transcendentals=0),
         name="reduce_all",
     )(*args)
+
+
+def finish_kernel(ka_ref, la_ref, kb_ref, lb_ref, g_ref, small_ref, *outs):
+    ea_ref, eb_ref, q_ref, k_ref, v_ref, o_ref, router_ref, attn_ref, moe_ref, table_ref = outs
+    width = q_ref.shape[2]
+    experts = router_ref.shape[1]
+    ea_ref[...] = ka_ref[...].astype(single) + jnp.sum(la_ref[...].astype(single), axis=0)
+    eb_ref[...] = kb_ref[...].astype(single) + jnp.sum(lb_ref[...].astype(single), axis=0)
+    starts = (0, width, 2 * width, 3 * width + TILE)
+    for start, ref in zip(starts, (q_ref, k_ref, v_ref, o_ref)):
+        ref[...] = g_ref[:, :, start : start + width].astype(single)
+
+    @pl.when(pl.program_id(0) == 0)
+    def _():
+        small = small_ref[...].astype(single)
+        router_ref[...] = small[:, :experts]
+        turned = small.T
+        attn_ref[...] = turned[experts : experts + 1]
+        moe_ref[...] = turned[experts + 1 : experts + 2]
+        table_ref[...] = small[: table_ref.shape[0], experts + 2 : experts + 2 + table_ref.shape[1]]
+
+
+def finish(ka, la, kb, lb, gathered, experts, table_rows, heads):
+    shape = jax.ShapeDtypeStruct
+    _, lines, full = gathered.shape
+    width = kb.shape[1]
+    rows = QUARTERS * lines
+    small = gathered[:, :, 3 * width : 3 * width + TILE].reshape(rows, TILE)
+    steps = QUARTERS
+    a_cols, b_rows = ka.shape[1] // steps, kb.shape[0] // steps
+    part = pl.BlockSpec((1, lines, width), lambda i: (i, 0, 0))
+    once = lambda *dims: pl.BlockSpec(dims, lambda i: (0,) * len(dims))
+    return pl.pallas_call(
+        finish_kernel,
+        grid=(steps,),
+        out_shape=(
+            shape(ka.shape, single), shape(kb.shape, single), *(shape((QUARTERS, lines, width), single),) * 4,
+            shape((rows, experts), single), shape((1, rows), single), shape((1, rows), single),
+            shape((table_rows, heads), single),
+        ),
+        in_specs=[
+            pl.BlockSpec((ka.shape[0], a_cols), lambda i: (0, i)),
+            pl.BlockSpec((la.shape[0], ka.shape[0], a_cols), lambda i: (0, 0, i)),
+            pl.BlockSpec((b_rows, width), lambda i: (i, 0)),
+            pl.BlockSpec((lb.shape[0], b_rows, width), lambda i: (0, i, 0)),
+            pl.BlockSpec((1, lines, full), lambda i: (i, 0, 0)), once(rows, TILE),
+        ],
+        out_specs=(
+            pl.BlockSpec((ka.shape[0], a_cols), lambda i: (0, i)), pl.BlockSpec((b_rows, width), lambda i: (i, 0)),
+            part, part, part, part, once(rows, experts), once(1, rows), once(1, rows), once(table_rows, heads),
+        ),
+        compiler_params=pltpu.CompilerParams(vmem_limit_bytes=vmem_cap),
+        cost_estimate=pl.CostEstimate(flops=0, bytes_accessed=12_000_000, transcendentals=0),
+        name="finish",
+    )(ka, la, kb, lb, gathered, small)
 
 
 def local(
@@ -1031,7 +1113,6 @@
     capacity = 2 * token_rows // expert_count
     slot_count = expert_count * capacity
 
-    weights = jnp.stack([w_query, w_key, w_value, w_output]).reshape(4, QUARTERS, -1, model_width)
     small = jnp.concatenate(
         [w_router, norm_attn[:, None], norm_moe[:, None],
          jnp.pad(rel_table, ((0, weight_rows - table_rows), (0, 0)))], axis=1
@@ -1039,14 +1120,12 @@
     small = jnp.pad(small, ((0, 0), (0, TILE - small.shape[1])))
     dispatch = routes * capacity + slot_ids
 
-    weights, every_tok, small = gather_all(weights, tokens, small)
-    weights = weights.reshape(4, model_width, model_width)
-    small = small.reshape(model_width, TILE)
+    ints = jnp.concatenate([routes[None], dispatch[None], jnp.zeros((6, token_rows), jnp.int32)])
     bucket_row = jnp.asarray(np.tile(distance_buckets(table_rows * shard_count), (8, 1)), jnp.int32)
-    normed, queries, keys, values, attended, lse, rev, mid, gate, gains, slots_out, grad_in = front(
-        every_tok, tokens, weights, small, bucket_row, routes[:, None],
-        jnp.broadcast_to(dispatch[None, :], (8, token_rows)), cotangent, slot_count,
-    )
+    (
+        normed, queries, keys, values, attended, lse, rev, mid, gate, col_slots, gains, slots_out, grad_in, weights,
+        every_tok, small,
+    ) = front(ints, bucket_row, cotangent, (w_query, w_key, w_value, w_output), tokens, small, slot_count)
     by_chip = (shard_count // 2, 2, capacity, model_width)
     grad_back, result, grad_w_in, grad_w_out, router_grads = moe(
         slots_out.reshape(by_chip), grad_in.reshape(by_chip), small, w_in[0], w_out[0]
@@ -1055,30 +1134,32 @@
     slows, fasts = rep_places()[3:]
     gwin = grad_w_in.reshape(slows, fasts, model_width // rep_count, -1)
     gwout = grad_w_out.reshape(slows, fasts, -1, model_width)
-    col_slots = dispatch[:, None]
-    dense, prompt_part, near_part, grad_own, grad_resid, returned, ra, rb = back(
+    dense, prompt_part, near_part, grad_own, grad_resid, output_part, returned, ra, rb = back(
         grad_back.reshape(slot_count, model_width), col_slots, mid, cotangent, gains, every_tok, weights,
         (normed, queries, keys, values, attended, lse, rev), bucket_row, router_grads,
         result.reshape(expert_count, capacity, model_width), gwin, gwout,
     )
     chips = shard_count // 2
-    grad_tokens, mixed, gq, gk, gv, go, tail, ka, la, kb, lb = reduce_all(
-        gains, col_slots, dense.reshape(chips, 2, QUARTERS, weight_rows // QUARTERS, -1),
+    lines = weight_rows // QUARTERS
+    grad_tokens, mixed, gathered, ka, la, kb, lb = reduce_all(
+        gains, col_slots, dense.reshape(chips, 2, QUARTERS, lines, -1),
         prompt_part.reshape(chips, 2, PR_DEV, model_width), near_part, grad_own, grad_resid, tokens, mid, gate,
         returned.reshape(slot_count, model_width), gwin, ra, gwout, rb,
+        output_part.reshape(QUARTERS, lines, model_width),
     )
-    total = lambda held, come: (held.astype(single) + jnp.sum(come.astype(single), axis=0))[None]
-    tail = tail.reshape(weight_rows, TILE)
+    in_grad, out_grad, gq, gk, gv, go, router, gain_attn, gain_moe, table = finish(
+        ka, la, kb, lb, gathered, expert_count, table_rows, head_count
+    )
     return (
         mixed,
         grad_tokens,
         *(part.reshape(weight_rows, model_width) for part in (gq, gk, gv, go)),
-        tail[:, :expert_count],
-        tail[:, expert_count],
-        tail[:, expert_count + 1],
-        tail[:table_rows, expert_count + 2 : expert_count + 2 + head_count],
-        total(ka, la),
-        total(kb, lb),
+        router,
+        gain_attn[0],
+        gain_moe[0],
+        table,
+        in_grad[None],
+        out_grad[None],
     )
 
 

time: 292 us -> 270 us (0.925)
  Pallas kernels: 269 us -> 260 us
  other arithmetic: 8.61 us -> 2.11 us
  local copies, waits for them, and re-layouts: 13.5 us -> 7.01 us
    pallas_call x1, Pallas kernels: 34.4 us -> 69 us  [front(): pl.pallas_call(front_kernel, out_shape=(shape((keys, width), low), shape(...]
    pallas_call x2, Pallas kernels: 109 us -> 74.9 us  [the longest x1 69.1 us: back(): pl.pallas_call(back_kernel, out_shape=(shape((width, 3 * width + TILE), l...]
    pallas_call x1, Pallas kernels: 68.2 us -> 63 us  [reduce_all(): pl.pallas_call(reduce_kernel, out_shape=(shape((rows, width), single), sh...]
    broadcast_in_dim x2 -> x0, other arithmetic: 5.16 us -> none  [local(): (held.astype(single) + jnp.sum(come.astype(single), axis=0))[None]]
    pallas_call x1, Pallas kernels: 56.9 us -> 52.9 us  [moe(): pl.pallas_call(moe_kernel, out_shape=(shape(rows_out.shape, low), shape(r...]
    unnamed x24 -> x8, local copies, waits for them, and re-layouts: 6.94 us -> 4.16 us
where the time goes in v4:
time: 270 us
  Pallas kernels  260 us (96%)
  local copies, waits for them, and re-layouts  7.01 us (3%)
    pallas_call x1, Pallas kernels, back(): pl.pallas_call(back_kernel, out_shape=(shape((width, 3 * width + TILE), l...  69.1 us
    pallas_call x1, Pallas kernels, front(): pl.pallas_call(front_kernel, out_shape=(shape((keys, width), low), shape(...  69 us
    pallas_call x1, Pallas kernels, reduce_all(): pl.pallas_call(reduce_kernel, out_shape=(shape((rows, width), single), sh...  63 us
    pallas_call x1, Pallas kernels, moe(): pl.pallas_call(moe_kernel, out_shape=(shape(rows_out.shape, low), shape(r...  52.9 us
    pallas_call x1, Pallas kernels, finish(): pl.pallas_call(finish_kernel, grid=(steps,), out_shape=(shape(ka.shape, s...  5.79 us

profile of v4, /device:TPU:0, one launch (start us, length us, event | category | flops | bytes accessed | tf_op | source)
XLA Modules:
  0.0 269.5 jit_solution(5153412411820153448)
XLA Ops:
  0.7 0.1 pad.16.clone
  0.7 0.7 broadcast_in_dim.21
  1.4 0.7 multiply_add_fusion
  2.1 0.8 copy.31
  2.9 0.7 fusion.1
  3.6 0.7 add_add_fusion.ints_ref
  4.3 0.1 copy.32
  4.4 0.6 pad.9.little_hbm
  5.0 69.0 %front.1 = (bf16[1536,768]{1,0:T(8,128)(2,1)}, bf16[384,768]{1,0:T(8,128)(2,1)}, bf16[1536,768]{1,0:T(8,128)(2,1)}, bf16[1536,768]{1,0:T(8,128)(2,1)}, f32[384,7...) custom-call(s32[8,384]{1,0:T(8,128)} %add_add_fusion.ints_ref, ...), custom_call_target="tpu_custom_call" | custom-call | flops 30000001024 | bytes 20000000 | tf_op jit(solution)/shard_map/front/pallas_call | solution.py:357
  74.0 52.9 %moe.1 = (bf16[4,2,96,768]{3,2,1,0:T(8,128)(2,1)}, bf16[4,2,96,768]{3,2,1,0:T(8,128)(2,1)}, bf16[768,3072]{1,0:T(8,128)(2,1)}, bf16[3072,768]{1,0:T(8,128)(2,1)}, f32[768,128]{1,0:T(8,128)}) custom-call(bf16[4,2,96,768]{3,2,1,0:T(8,128)(2,1)} %bitcast.46, bf16[4,2,96,768]{3,2,1,0:T(8,128)(2,1)} %bitcast.47, bf16[768,128]{1,0:T(8,128)(2,1)} %get-tuple-element.63.small_ref, ...), custom_call_target="tpu_custom_call" | custom-call | flops 40000000000 | bytes 40000000 | tf_op jit(solution)/shard_map/moe/pallas_call | solution.py:519
  126.9 69.1 %back.1 = (bf16[768,2432]{1,0:T(8,128)(2,1)}, bf16[1024,768]{1,0:T(8,128)(2,1)}, bf16[256,768]{1,0:T(8,128)(2,1)}, f32[384,768]{1,0:T(8,128)}, f32[384,768]{1,0:...) custom-call(bf16[768,768]{1,0:T(8,128)(2,1)} %bitcast.44, ...), custom_call_target="tpu_custom_call" | custom-call | flops 60000002048 | bytes 40000000 | tf_op jit(solution)/shard_map/back/pallas_call | solution.py:761
  196.0 63.0 %reduce_all.1 = (f32[384,768]{1,0:T(8,128)}, bf16[384,768]{1,0:T(8,128)(2,1)}, bf16[4,24,3200]{2,1,0:T(8,128)(2,1)}, bf16[192,3072]{1,0:T(8,128)(2,1)}, bf16[1,1...) custom-call(f32[8,768]{1,0:T(8,128)} %get-tuple-element.59.gain_ref, ...), custom_call_target="tpu_custom_call" | custom-call | bytes 200000000 | tf_op jit(solution)/shard_map/reduce_all/pallas_call | solution.py:1004
  259.0 1.3 slice.3
  260.3 0.0 copy-start.1
  260.3 5.8 %finish.1 = (f32[192,3072]{1,0:T(8,128)}, f32[768,768]{1,0:T(8,128)}, f32[4,24,768]{2,1,0:T(8,128)}, f32[4,24,768]{2,1,0:T(8,128)}, f32[4,24,768]{2,1,0:T(8,128)...) custom-call(bf16[192,3072]{1,0:T(8,128)(2,1)} %get-tuple-element.91.ka_r, ...), custom_call_target="tpu_custom_call" | custom-call | bytes 12000000 | tf_op jit(solution)/shard_map/finish/pallas_call | solution.py:1067
  266.1 0.0 copy-start
  266.1 1.6 copy.33
  267.7 0.0 copy-done.1
  267.7 0.8 copy.36
  268.5 0.0 copy-done
  268.5 1.0 copy.37
  (2 shorter events, 0.0 us)
Async XLA Ops:
  260.3 7.4 %copy-start.1 = (bf16[384,768]{1,0:T(8,128)(2,1)S(1)}, bf16[384,768]{1,0:T(8,128)(2,1)}, u32[]{:S(2)}) copy-start(bf16[384,768]{1,0:T(8,128)(2,1)} %get-tuple-element.142) | copy-start | bytes 1769476
  266.1 2.4 copy-start
